TPU v7x, 128 devices: a whole 4x4x4 slice. The times are simulated.
128 devices in a mesh: section: 4 (over x), dom: 32 (over z, y, core).
Axes of the slice: x: 4, y: 4, z: 4, core: 2. Of those that a mesh axis runs over, the one named last changes fastest.
Arguments:
- features: bfloat16 [2, 16384, 1024], P(None, 'dom'), may hold values from -6 to 6
- tiles: bfloat16 [2, 128, 12, 128, 128], P(None, 'dom'), may hold values from -0.15625 to 0.15625
- w_first: bfloat16 [4, 1024, 1024], P('section'), may hold values from -0.1875 to 0.1875
- w_second: bfloat16 [4, 1024, 1024], P('section'), may hold values from -0.1875 to 0.1875
- tile_block: int32 [2, 128, 12], replicated, may hold values from 0 to 255, as said below
Outputs:
- layer_outputs: bfloat16 [4, 2, 16384, 1024], P('section', None, 'dom')
Inputs may be any that keep to these rules, and one draw needn't show every extreme that they name: `tile_block`: block row r belongs to partition r // 4 of a cycle of partitions. Entry [c, r, j] names a block of span c or an earlier span, owned by the partition of row r or by one of the two partitions beside it on the cycle. Among the 48 entries of one partition's block rows in one span, at most 6 name blocks of the partition one below and at most 6 name blocks of the partition one above, and one of these two counts is exactly 6 in every span and partition. Entries may repeat.
All inputs are finite; a program needn't handle non-finite values.
Results may differ from a plain program's by a relative error of at most 0.012.
Values may be sent and summed in bfloat16 or wider, within the bound.
No kernel may reach another device: no remote copies, remote signals or barrier semaphores. Data moves between devices by JAX's collectives and lax.ppermute only.
A program may use at most 128 MiB of HBM per device.

v0:
```python
import functools

import jax
import jax.numpy as jnp
from jax import lax
from jax.experimental import pallas as pl
from jax.experimental.pallas import tpu as pltpu
from jax.sharding import PartitionSpec as P


ANY = pl.BlockSpec(memory_space=pl.ANY)
SMEM = pl.BlockSpec(memory_space=pltpu.SMEM)
VMEM = pl.BlockSpec(memory_space=pltpu.VMEM)
HBM = pl.BlockSpec(memory_space=pltpu.HBM)
MIB = 2**20


def entry_tables(ids, me, parts, nbc):
    spans, blk_rows, n_tiles = ids.shape
    count = blk_rows * n_tiles
    ids = ids.reshape(spans, count)
    within = ids % nbc
    rel = (within // blk_rows - me + parts) % parts
    local = ids // nbc * blk_rows + within % blk_rows
    on_chip = jnp.where(me % 2 == 0, 1, parts - 1)
    across = (rel != 0) & (rel != on_chip)
    held = (1 + jnp.arange(spans, dtype=jnp.int32)[:, None]) * blk_rows
    slot = jnp.where(across, 0, jnp.where(rel == on_chip, held + local, local))
    near = jnp.stack([slot, jnp.where(across, 0, 1)], axis=1).astype(jnp.int32)
    order = jnp.arange(count, dtype=jnp.int32)
    before = (order[None, :] < order[:, None])[None]
    rank = jnp.sum(jnp.where(before & across[:, None, :], 1, 0), axis=2)
    chosen = across[:, None, :] & (rank[:, None, :] == order[None, :, None])
    place = jnp.sum(jnp.where(chosen, order[None, None, :], 0), axis=2)
    block = jnp.sum(jnp.where(chosen, local[:, None, :], 0), axis=2)
    total = jnp.sum(jnp.where(across, 1, 0), axis=1, keepdims=True) + jnp.zeros_like(place)
    far = jnp.stack([place, block, total], axis=1).astype(jnp.int32)
    return near, far


def early_kernel(span, n_src, near_ref, tiles_ref, *refs):
    srcs = refs[:n_src]
    acc_ref, buf, tbuf, src_sem, tile_sem = refs[n_src:]
    blk_rows, n_tiles, _, _ = tbuf.shape
    copies = [pltpu.make_async_copy(tiles_ref.at[span], tbuf, tile_sem)]
    for i, src in enumerate(srcs):
        size = buf.shape[0] // n_src
        rows = pl.ds(i * size, size)
        copies.append(pltpu.make_async_copy(src.at[pl.ds(0, size)], buf.at[rows], src_sem.at[i]))
    for copy in copies:
        copy.start()
    for copy in copies:
        copy.wait()

    def one_row(row, carry):
        total = None
        for pair in range(n_tiles // 2):
            lhs, rhs = [], []
            for j in (2 * pair, 2 * pair + 1):
                e = row * n_tiles + j
                tile = tbuf[row, j]
                lhs.append(jnp.where(near_ref[span, 1, e] == 0, jnp.zeros_like(tile), tile))
                rhs.append(buf[near_ref[span, 0, e]])
            part = jnp.dot(
                jnp.concatenate(lhs, axis=1),
                jnp.concatenate(rhs, axis=0),
                preferred_element_type=jnp.float32,
            )
            total = part if total is None else total + part
        acc_ref[row] = total
        return carry

    lax.fori_loop(0, blk_rows, one_row, 0)


def pick_kernel(n_got, meta_ref, *refs):
    got_refs = refs[:n_got]
    w1_ref, w2_ref, sem = refs[n_got:]
    feat = w1_ref.shape[0]
    mid = feat // 2
    mode = meta_ref[1]

    def fetch(one, two):
        for part, dst, k in ((one, w1_ref, 0), (two, w2_ref, 1)):
            for src, rows in part:
                pltpu.make_async_copy(src, dst.at[rows], sem.at[k]).start()

    def halves(a, b):
        return [(a, pl.ds(0, mid)), (b, pl.ds(mid, mid))]

    def shards(a, b):
        z = meta_ref[0]
        quarter = a.shape[0] // 4
        part = []
        for k, away in enumerate((0, 3, 1, 2)):
            start = pl.multiple_of((z + away) % 4 * quarter, quarter)
            part.append((a.at[pl.ds(k * quarter, quarter)], pl.ds(start, quarter)))
        return part + [(b, pl.ds(4 * quarter, feat - 4 * quarter))]

    choices = []
    for at in range(0, n_got, 4):
        form = halves if at < 8 else shards
        one, two = form(*got_refs[at : at + 2]), form(*got_refs[at + 2 : at + 4])
        choices += [(at // 2, one, two), (at // 2 + 1, two, one)]
    for value, one, two in choices:
        pl.when(mode == value)(functools.partial(fetch, one, two))
    pltpu.make_async_copy(w1_ref, w1_ref, sem.at[0]).wait()
    pltpu.make_async_copy(w2_ref, w2_ref, sem.at[1]).wait()


def pick(meta, got):
    feat = got[0].shape[-1]
    shape = jax.ShapeDtypeStruct((feat, feat), jnp.bfloat16)
    return list(
        pl.pallas_call(
            functools.partial(pick_kernel, len(got)),
            out_shape=[shape, shape],
            in_specs=[SMEM] + [ANY] * len(got),
            out_specs=[VMEM, VMEM],
            scratch_shapes=[pltpu.SemaphoreType.DMA((2,))],
            compiler_params=pltpu.CompilerParams(vmem_limit_bytes=6 * MIB),
            cost_estimate=pl.CostEstimate(flops=0, bytes_accessed=8 * MIB, transcendentals=0),
            name="pick",
        )(meta, *got)
    )


CUT = 384


def mine_kernel(meta_ref, first_ref, second_ref, quarter_ref, rest_ref, a_ref, b_ref, sem):
    size = quarter_ref.shape[0]
    mid = a_ref.shape[0]

    def fetch(src):
        start = pl.multiple_of(meta_ref[0] * size, size)
        pltpu.make_async_copy(src.at[pl.ds(start, size)], quarter_ref, sem.at[0]).start()
        pltpu.make_async_copy(src.at[pl.ds(4 * size, rest_ref.shape[0])], rest_ref, sem.at[1]).start()
        pltpu.make_async_copy(src.at[pl.ds(0, mid)], a_ref, sem.at[2]).start()
        pltpu.make_async_copy(src.at[pl.ds(mid, mid)], b_ref, sem.at[3]).start()

    pl.when(meta_ref[1] == 0)(functools.partial(fetch, first_ref))
    pl.when(meta_ref[1] != 0)(functools.partial(fetch, second_ref))
    for k, dst in enumerate((quarter_ref, rest_ref, a_ref, b_ref)):
        pltpu.make_async_copy(dst, dst, sem.at[k]).wait()


def mine(meta, w_first, w_second):
    feat = w_first.shape[0]
    rows = (CUT // 4, feat - CUT, feat // 2, feat // 2)
    return pl.pallas_call(
        mine_kernel,
        out_shape=[jax.ShapeDtypeStruct((size, feat), jnp.bfloat16) for size in rows],
        in_specs=[SMEM, HBM, HBM],
        out_specs=[VMEM] * 4,
        scratch_shapes=[pltpu.SemaphoreType.DMA((4,))],
        compiler_params=pltpu.CompilerParams(vmem_limit_bytes=56 * MIB),
        cost_estimate=pl.CostEstimate(flops=0, bytes_accessed=8 * MIB, transcendentals=0),
        name="mine",
    )(meta, w_first, w_second)


def join_kernel(*refs):
    *parts, out_ref, sem = refs
    size = parts[0].shape[0]
    for k, part in enumerate(parts):
        pltpu.make_async_copy(part, out_ref.at[pl.ds(k * size, size)], sem).start()
    pltpu.make_async_copy(out_ref, out_ref, sem).wait()


def join(*parts):
    size, feat = parts[0].shape
    return pl.pallas_call(
        join_kernel,
        out_shape=jax.ShapeDtypeStruct((len(parts) * size, feat), jnp.bfloat16),
        in_specs=[ANY] * len(parts),
        out_specs=VMEM,
        scratch_shapes=[pltpu.SemaphoreType.DMA],
        compiler_params=pltpu.CompilerParams(vmem_limit_bytes=4 * MIB),
        cost_estimate=pl.CostEstimate(flops=0, bytes_accessed=2 * MIB, transcendentals=0),
        name="join",
    )(*parts)


def place_kernel(sizes, meta_ref, *refs):
    count = sum(len(one) for one in sizes)
    others = refs[:count]
    out_ref, buf, sem = refs[count + 1 :]
    at = 0
    for k, one in enumerate(sizes):
        mine_refs = others[at : at + len(one)]
        at += len(one)

        @pl.when(meta_ref[2] == k)
        def _():
            start = 0
            for src, size in zip(mine_refs, one):
                pltpu.make_async_copy(src, buf.at[pl.ds(start, size)], sem).start()
                start += size
            pltpu.make_async_copy(buf, buf, sem).wait()
            copy = pltpu.make_async_copy(buf, out_ref, sem)
            copy.start()
            copy.wait()


def place(meta, others, out):
    flat = sum(others, [])
    sizes = [[part.shape[0] for part in one] for one in others]
    return pl.pallas_call(
        functools.partial(place_kernel, sizes),
        out_shape=jax.ShapeDtypeStruct(out.shape, out.dtype),
        in_specs=[SMEM] + [ANY] * len(flat) + [HBM],
        out_specs=HBM,
        scratch_shapes=[pltpu.VMEM(out.shape, out.dtype), pltpu.SemaphoreType.DMA],
        input_output_aliases={len(flat) + 1: 0},
        compiler_params=pltpu.CompilerParams(vmem_limit_bytes=6 * MIB),
        cost_estimate=pl.CostEstimate(flops=0, bytes_accessed=4 * MIB, transcendentals=0),
        name="place",
    )(meta, *flat, out)


def late_kernel(span, n_cross, final, far_ref, meta_ref, tiles_ref, acc_ref, resid_ref, w1_ref, w2_ref, *refs):
    crosses = refs[:n_cross]
    out_ref, cacc, tb, t_sem, *more_refs = refs[n_cross + (1 if final and span else 0) :]
    obuf = more_refs[0] if final else out_ref
    blk_rows, tile_len, feat = cacc.shape
    n_tiles = tiles_ref.shape[2]
    total = jnp.minimum(far_ref[span, 2, 0], tb.shape[0])

    def tile_copy(k):
        e = far_ref[span, 0, k]
        return pltpu.make_async_copy(tiles_ref.at[span, e // n_tiles, e % n_tiles], tb.at[k], t_sem.at[k])

    def start_tile(k, carry):
        tile_copy(k).start()
        return carry

    lax.fori_loop(0, total, start_tile, 0)
    cacc[...] = jnp.zeros_like(cacc)

    def one_entry(k, carry):
        row = far_ref[span, 0, k] // n_tiles
        block = far_ref[span, 1, k]
        tile_copy(k).wait()
        for c, src in enumerate(crosses):

            @pl.when((len(crosses) == 1) | (block // blk_rows == c))
            def _():
                cacc[row] += jnp.dot(tb[k], src[block - c * blk_rows], preferred_element_type=jnp.float32)

        return carry

    lax.fori_loop(0, total, one_entry, 0)
    step = 2

    def one_part(i, carry):
        rows = pl.ds(i * step, step)
        first = (resid_ref.shape[0] // blk_rows - 1) * span * blk_rows
        from_rows = pl.ds(first + i * step, step)
        agg = (acc_ref[rows] + cacc[rows]).reshape(step * tile_len, feat).astype(jnp.bfloat16)
        hidden = jnp.dot(agg, w1_ref[...], preferred_element_type=jnp.float32)
        hidden = jnp.maximum(hidden, 0.0).astype(jnp.bfloat16)
        more = jnp.dot(hidden, w2_ref[...], preferred_element_type=jnp.float32)
        more = more.reshape(step, tile_len, feat)
        obuf[rows] = (resid_ref[from_rows].astype(jnp.float32) + more).astype(jnp.bfloat16)
        if final:
            dst = out_ref.at[pl.ds(span * blk_rows + i * step, step)]
            pltpu.make_async_copy(obuf.at[rows], dst, more_refs[1]).start()
        return carry

    parts = jnp.where(meta_ref[3] != 0, blk_rows // step, 0)
    lax.fori_loop(0, parts, one_part, 0)
    if final:

        @pl.when(meta_ref[3] != 0)
        def _():
            pltpu.make_async_copy(obuf, out_ref.at[pl.ds(span * blk_rows, blk_rows)], more_refs[1]).wait()


def early(span, near, tiles, srcs):
    _, blk_rows, n_tiles, tile_len, _ = tiles.shape
    feat = srcs[0].shape[-1]
    n_src = len(srcs)
    return pl.pallas_call(
        functools.partial(early_kernel, span, n_src),
        out_shape=jax.ShapeDtypeStruct((blk_rows, tile_len, feat), jnp.float32),
        in_specs=[SMEM, ANY] + [ANY] * n_src,
        out_specs=VMEM,
        scratch_shapes=[
            pltpu.VMEM((2 * (span + 1) * blk_rows, tile_len, feat), jnp.bfloat16),
            pltpu.VMEM((blk_rows, n_tiles, tile_len, tile_len), jnp.bfloat16),
            pltpu.SemaphoreType.DMA((n_src,)),
            pltpu.SemaphoreType.DMA,
        ],
        compiler_params=pltpu.CompilerParams(vmem_limit_bytes=14 * MIB),
        cost_estimate=pl.CostEstimate(
            flops=2 * blk_rows * n_tiles * tile_len * tile_len * feat,
            bytes_accessed=8 * MIB,
            transcendentals=0,
        ),
    )(near, tiles, *srcs)


FAR = 8


def late(span, far, meta, tiles, acc, resid, crosses, weights, final=False, prior=None):
    spans, blk_rows, _, tile_len, _ = tiles.shape
    feat = acc.shape[-1]
    tail = [] if prior is None else [prior]
    args = [far, meta, tiles, acc, resid, *weights, *crosses, *tail]
    out_rows = spans * blk_rows if final else blk_rows
    return pl.pallas_call(
        functools.partial(late_kernel, span, len(crosses), final),
        out_shape=jax.ShapeDtypeStruct((out_rows, tile_len, feat), jnp.bfloat16),
        in_specs=[SMEM, SMEM, ANY] + [VMEM] * (4 + len(crosses)) + [HBM] * len(tail),
        out_specs=HBM if final else VMEM,
        scratch_shapes=[
            pltpu.VMEM((blk_rows, tile_len, feat), jnp.float32),
            pltpu.VMEM((FAR, tile_len, tile_len), jnp.bfloat16),
            pltpu.SemaphoreType.DMA((FAR,)),
        ]
        + ([pltpu.VMEM((blk_rows, tile_len, feat), jnp.bfloat16), pltpu.SemaphoreType.DMA] if final else []),
        compiler_params=pltpu.CompilerParams(vmem_limit_bytes=14 * MIB),
        input_output_aliases={len(args) - 1: 0} if tail else {},
        cost_estimate=pl.CostEstimate(
            flops=4 * blk_rows * tile_len * feat * feat,
            bytes_accessed=8 * MIB,
            transcendentals=0,
        ),
    )(*args)


def after(value, *deps):
    return lax.optimization_barrier((value, *deps))[0]


def on_device(features, tiles, w_first, w_second, tile_block):
    spans, row_count, feat = features.shape
    _, blk_rows, _, tile_len, _ = tiles.shape
    parts = lax.axis_size("dom")
    section = lax.axis_index("section")
    me = lax.axis_index("dom")
    hub = lax.axis_size("section") - 1
    row_parts = parts // 4
    z = me // row_parts
    swap_pairs = [(p, p ^ 1) for p in range(parts)]
    cross_pairs = [(p, (p + 1) % parts if p % 2 else (p - 1) % parts) for p in range(parts)]

    def swap(value):
        return lax.ppermute(value, "dom", swap_pairs)

    def cross(value):
        return lax.ppermute(value, "dom", cross_pairs)

    def hop(value, pairs):
        return lax.ppermute(value, "section", pairs)

    def along_z(value, by):
        return lax.ppermute(value, "dom", [(p, (p + by * row_parts) % parts) for p in range(parts)])

    def sums(span, h, chip):
        return early(span, near, tiles, h[: span + 1] + chip[: span + 1])

    w_first, w_second = w_first[0], w_second[0]

    def meta(mode, active):
        return jnp.stack([z, mode + me % 2, section, active.astype(jnp.int32)]).astype(jnp.int32)

    is_hub = section == hub
    metas = [
        meta(jnp.where(section == 0, 0, jnp.where(is_hub, 4, 2)), section != 2),
        meta(jnp.where(section == 1, 0, 2), (section == 1) | is_hub),
        meta(jnp.zeros_like(me), is_hub),
        meta(jnp.zeros_like(me), is_hub),
    ]

    def layer(num, acc, h, over, weights):
        out, chip_out, over_out = [], [], []
        for s in range(spans):
            out.append(late(s, far, metas[num], tiles, acc[s], h[s], over[: s + 1], weights))
            chip_out.append(swap(out[s]))
            over_out.append(cross(out[s]))
        return out, chip_out, over_out, [sums(s, out, chip_out) for s in range(spans)]

    shard, rest, mine_a, mine_b = mine(metas[3], w_first, w_second)
    shard = hop(shard, [(0, hub)])
    start = features.reshape(spans * blk_rows, tile_len, feat)
    chip0 = swap(start)
    over0 = cross(start)
    zero_b = hop(rest, [(0, hub)])
    next_a = hop(mine_a, [(0, 1), (1, 2), (2, hub)])
    zero_a = join(shard, along_z(shard, 1), along_z(shard, -1), along_z(shard, 2))
    next_b = hop(mine_b, [(0, 1)])
    ids = lax.dynamic_slice_in_dim(tile_block, me * blk_rows, blk_rows, 1)
    near, far = entry_tables(ids, me, parts, parts * blk_rows)
    near, far, *metas = lax.optimization_barrier((near, far, *metas))

    acc = [sums(s, [start], [chip0]) for s in range(spans)]
    one_a = hop(after(next_a, *acc), [(2, hub)])
    one_b = hop(after(mine_b, *acc), [(1, hub)])
    two_b = hop(after(mine_b, *acc), [(2, hub)])
    kept = [mine_a, mine_b, swap(mine_a), swap(mine_b)]
    swap_next = [swap(after(next_a, *acc)), swap(after(next_b, *acc))]
    swap_zero = [swap(zero_a), swap(after(zero_b, *acc))]
    got = [*kept, next_a, next_b, *swap_next, zero_a, zero_b, *swap_zero]
    h1, _, over1, acc = layer(0, acc, [start] * spans, [over0], pick(metas[0], got))
    one_a, one_b = after(one_a, *acc), after(one_b, *acc)
    got = [*kept, one_a, one_b, swap(one_a), swap(one_b)]
    weights = pick(metas[1], got)

    h2, _, over2, acc = layer(1, acc, h1, over1, weights)
    two_b = after(two_b, *acc)
    got = [next_a, two_b, swap_next[0], swap(two_b)]
    weights = pick(metas[2], got)

    h3, _, over3, acc = layer(2, acc, h2, over2, weights)
    half = blk_rows // 2
    away = hop(h3[0][half:], [(hub, 0)])
    away = hop(away, [(0, 1)])
    away = hop(away, [(1, 2)])
    back = [hop(h3[0][:half], [(hub, 2)]), away, hop(h3[1], [(hub, 2)])]

    out = None
    for s in range(spans):
        out = late(s, far, metas[3], tiles, acc[s], h3[s], over3[: s + 1], [w_first, w_second], True, out)
    out = place(metas[3], [h1, h2, back], out)
    return out.reshape(1, spans, row_count, feat)


def solution(mesh):
    placed = (
        P(None, "dom", None),
        P(None, "dom", None, None, None),
        P("section", None, None),
        P("section", None, None),
        P(),
    )
    return jax.shard_map(
        on_device,
        mesh=mesh,
        in_specs=placed,
        out_specs=P("section", None, "dom", None),
        check_vma=False,
    )
```

profile of v0, /device:TPU:4, one launch (start us, length us, event | category | flops | bytes accessed | tf_op | source)
XLA Modules:
  0.0 294.6 jit_solution(4186716417935437736)
XLA Ops:
  0.0 0.7 pad_add_fusion.4.meta_ref
  0.7 4.9 %mine.1 = (bf16[96,1024]{1,0:T(8,128)(2,1)}, bf16[640,1024]{1,0:T(8,128)(2,1)}, bf16[512,1024]{1,0:T(8,128)(2,1)}, bf16[512,1024]{1,0:T(8,128)(2,1)}) custom-call(s32[4]{0:T(128)} %pad_add_fusion.4.meta_ref, bf16[1024,1024]{1,0:T(8,128)(2,1)} %bitcast.25, bf16[1024,1024]{1,0:T(8,128)(2,1)} %bitcast.28), custom_call_target="tpu_custom_call" | custom-call | bytes 8388608 | tf_op jit(solution)/shard_map/mine/pallas_call | solution.py:151
  5.6 1.8 collective-permute-start.11
  7.4 0.7 collective-permute-start.7
  8.0 3.3 %collective-permute-start.3 = (bf16[512,1024]{1,0:T(8,128)(2,1)}, bf16[512,1024]{1,0:T(8,128)(2,1)}, u32[]{:S(2)}, u32[]{:S(2)}) collective-permute-start(bf16[512,1024]{1,0:T(8,128)(2,1)} %get-tuple-element.32.refs_0_), channel_id=1, source_target_pairs={{0,32},{32,64},{64,96},{1,33},{33,65},{65,97},{2,34},{34,66},{66,9... | collective-permute-start | bytes 3145736 | tf_op jit(solution)/shard_map/ppermute | solution.py:357
  11.3 1.6 collective-permute-start.4
  13.0 0.8 fusion.3
  14.2 0.6 fusion.5
  14.8 3.9 %collective-permute-start.10 = (bf16[96,1024]{1,0:T(8,128)(2,1)S(1)}, bf16[96,1024]{1,0:T(8,128)(2,1)S(1)}, u32[]{:S(2)}, u32[]{:S(2)}) collective-permute-start(bf16[96,1024]{1,0:T(8,128)(2,1)S(1)} %collective-permute-done.7.refs_0_), channel_id=1, source_target_pairs={{0,16},{1,17},{2,18},{3,19},{4,20},{5,21},{6,22},{7,23},{8,24},{9,... | collective-permute-start | bytes 589832 | tf_op jit(solution)/shard_map/ppermute | solution.py:360
  18.7 5.3 %collective-permute-done.10.refs_3_ = bf16[96,1024]{1,0:T(8,128)(2,1)S(1)} collective-permute-done((bf16[96,1024]{1,0:T(8,128)(2,1)S(1)}, bf16[96,1024]{1,0:T(8,128)(2,1)S(1)}, u32[]{:S(2)}, u32[]{:S(2)}) %collective-permute-start.10) | collective-permute-done | bytes 196640 | tf_op jit(solution)/shard_map/ppermute | solution.py:360
  23.9 1.3 collective-permute-start.8
  25.3 6.5 %collective-permute-done.8.refs_1_ = bf16[96,1024]{1,0:T(8,128)(2,1)S(1)} collective-permute-done((bf16[96,1024]{1,0:T(8,128)(2,1)S(1)}, bf16[96,1024]{1,0:T(8,128)(2,1)S(1)}, u32[]{:S(2)}, u32[]{:S(2)}) %collective-permute-start.8) | collective-permute-done | bytes 196640 | tf_op jit(solution)/shard_map/ppermute | solution.py:360
  31.8 0.7 copy-done.7
  32.5 4.3 %collective-permute-start.14 = (bf16[8,128,1024]{2,1,0:T(8,128)(2,1)}, bf16[8,128,1024]{2,1,0:T(8,128)(2,1)}, u32[]{:S(2)}, u32[]{:S(2)}) collective-permute-start(bf16[8,128,1024]{2,1,0:T(8,128)(2,1)} %bitcast.20), channel_id=1, source_target_pairs={{0,31},{1,2},{2,1},{3,4},{4,3},{5,6},{6,5},{7,8},{8,7},{9,10},{10,... | collective-permute-start | bytes 6291464 | tf_op jit(solution)/shard_map/ppermute | solution.py:354
  36.9 0.8 select_reduce_fusion.1
  37.9 0.7 stack.71
  38.7 1.6 copy-done.1
  40.3 4.3 %shard_map.55.acc_ref = f32[4,128,1024]{2,1,0:T(8,128)S(1)} custom-call(s32[2,2,48]{2,1,0:T(2,128)S(1)} %pad_add_fusion.1.near_ref, bf16[2,4,12,128,128]{4,3,2,1,0:T(8,128)(2,1)S(1)} %copy-done, bf16[8,128,1024]{2,1,0:T(8,128)(2,1)S(1)} %bitcast.21, bf16[8,128,1024]{2,1,0:T(8,128)(2,1)} %collective-permute-done.refs_1_), custom_call_target="tpu_custom_call" | custom-call | flops 1610612736 | bytes 8388608 | tf_op jit(solution)/shard_map/pallas_call | solution.py:284
  44.6 4.8 %shard_map.56.acc_ref = f32[4,128,1024]{2,1,0:T(8,128)S(1)} custom-call(s32[2,2,48]{2,1,0:T(2,128)S(1)} %pad_add_fusion.1.near_ref, bf16[2,4,12,128,128]{4,3,2,1,0:T(8,128)(2,1)S(1)} %copy-done, bf16[8,128,1024]{2,1,0:T(8,128)(2,1)S(1)} %bitcast.22, bf16[8,128,1024]{2,1,0:T(8,128)(2,1)} %collective-permute-done.refs_1_), custom_call_target="tpu_custom_call" | custom-call | flops 1610612736 | bytes 8388608 | tf_op jit(solution)/shard_map/pallas_call | solution.py:284
  49.4 0.6 collective-permute-start.13
  50.0 0.4 collective-permute-start.9
  50.4 6.5 %collective-permute-done.9.refs_2_ = bf16[96,1024]{1,0:T(8,128)(2,1)S(1)} collective-permute-done((bf16[96,1024]{1,0:T(8,128)(2,1)S(1)}, bf16[96,1024]{1,0:T(8,128)(2,1)S(1)}, u32[]{:S(2)}, u32[]{:S(2)}) %collective-permute-start.9) | collective-permute-done | bytes 196640 | tf_op jit(solution)/shard_map/ppermute | solution.py:360
  56.9 0.5 collective-permute-start.6
  57.4 1.0 join.1.refs_8_
  58.6 3.8 %collective-permute-done.12.refs_10_ = bf16[384,1024]{1,0:T(8,128)(2,1)S(1)} collective-permute-done((bf16[384,1024]{1,0:T(8,128)(2,1)S(1)}, bf16[384,1024]{1,0:T(8,128)(2,1)S(1)}, u32[]{:S(2)}, u32[]{:S(2)}) %collective-permute-start.12) | collective-permute-done | bytes 786464 | tf_op jit(solution)/shard_map/ppermute | solution.py:351
  62.4 2.1 pick.3
  64.6 3.6 %shard_map.57.refs_0_.resid_ref = bf16[4,128,1024]{2,1,0:T(8,128)(2,1)S(1)} custom-call(s32[2,3,48]{2,1,0:T(4,128)S(1)} %pad_add_fusion.far_ref, s32[4]{0:T(128)S(1)} %get-tuple-element.30.meta_ref, bf16[2,4,12,128,128]{4,3,2,1,0:T(8,128)(2,1)S(1)} %copy-done, f32[4,128,1024]{2,1,0:T(8,128)S(1)} %shard_map.55.acc_ref, bf16[8,128,1024]{2,1,0:T(8,128)(2,1)S(1)} %bitcast.23, ...), custom_call_target="tpu_custom_call" | custom-call | flops 2147483648 | bytes 8388608 | tf_op jit(solution)/shard_map/pallas_call | solution.py:313
  68.2 0.4 collective-permute-start.15
  68.5 3.6 %shard_map.58.refs_1_.resid_ref = bf16[4,128,1024]{2,1,0:T(8,128)(2,1)S(1)} custom-call(s32[2,3,48]{2,1,0:T(4,128)S(1)} %pad_add_fusion.far_ref, s32[4]{0:T(128)S(1)} %get-tuple-element.30.meta_ref, bf16[2,4,12,128,128]{4,3,2,1,0:T(8,128)(2,1)S(1)} %copy-done, f32[4,128,1024]{2,1,0:T(8,128)S(1)} %shard_map.56.acc_ref, bf16[8,128,1024]{2,1,0:T(8,128)(2,1)S(1)} %bitcast.24, ...), custom_call_target="tpu_custom_call" | custom-call | flops 2147483648 | bytes 8388608 | tf_op jit(solution)/shard_map/pallas_call | solution.py:313
  72.4 0.7 collective-permute-start.18
  73.1 39.2 %collective-permute-start.16 = (bf16[512,1024]{1,0:T(8,128)(2,1)}, bf16[512,1024]{1,0:T(8,128)(2,1)S(1)}, u32[]{:S(2)}, u32[]{:S(2)}) collective-permute-start(bf16[512,1024]{1,0:T(8,128)(2,1)} %collective-permute-done.3.refs_4_.refs_0_), channel_id=1, source_target_pairs={{64,96},{65,97},{66,98},{67,99},{68,100},{69,101},{70,102},{71,103... | collective-permute-start | bytes 3145736 | tf_op jit(solution)/shard_map/ppermute | solution.py:357
  112.4 3.2 %shard_map.59.acc_ref = f32[4,128,1024]{2,1,0:T(8,128)S(1)} custom-call(s32[2,2,48]{2,1,0:T(2,128)S(1)} %pad_add_fusion.1.near_ref, bf16[2,4,12,128,128]{4,3,2,1,0:T(8,128)(2,1)S(1)} %copy-done, bf16[4,128,1024]{2,1,0:T(8,128)(2,1)S(1)} %shard_map.57.refs_0_.resid_ref, bf16[4,128,1024]{2,1,0:T(8,128)(2,1)S(1)} %collective-permute-done.15.refs_1_.refs_2_), custom_call_target="tpu_custom_call" | custom-call | flops 1610612736 | bytes 8388608 | tf_op jit(solution)/shard_map/pallas_call | solution.py:284
  115.6 3.4 %shard_map.60.acc_ref = f32[4,128,1024]{2,1,0:T(8,128)S(1)} custom-call(s32[2,2,48]{2,1,0:T(2,128)S(1)} %pad_add_fusion.1.near_ref, bf16[2,4,12,128,128]{4,3,2,1,0:T(8,128)(2,1)S(1)} %copy-done, bf16[4,128,1024]{2,1,0:T(8,128)(2,1)S(1)} %shard_map.57.refs_0_.resid_ref, bf16[4,128,1024]{2,1,0:T(8,128)(2,1)S(1)} %shard_map.58.refs_1_.resid_ref, ...), custom_call_target="tpu_custom_call" | custom-call | flops 1610612736 | bytes 8388608 | tf_op jit(solution)/shard_map/pallas_call | solution.py:284
  119.2 16.4 %collective-permute-done.16.refs_4_ = bf16[512,1024]{1,0:T(8,128)(2,1)S(1)} collective-permute-done((bf16[512,1024]{1,0:T(8,128)(2,1)}, bf16[512,1024]{1,0:T(8,128)(2,1)S(1)}, u32[]{:S(2)}, u32[]{:S(2)}) %collective-permute-start.16) | collective-permute-done | bytes 1048608 | tf_op jit(solution)/shard_map/ppermute | solution.py:357
  135.7 13.8 %collective-permute-start.21 = (bf16[4,128,1024]{2,1,0:T(8,128)(2,1)S(1)}, bf16[4,128,1024]{2,1,0:T(8,128)(2,1)S(1)}, u32[]{:S(2)}, u32[]{:S(2)}) collective-permute-start(bf16[4,128,1024]{2,1,0:T(8,128)(2,1)S(1)} %shard_map.57.refs_0_.resid_ref), channel_id=1, source_target_pairs={{0,31},{1,2},{2,1},{3,4},{4,3},{5,6},{6,5},{7,8},{8,7},{9,10},{10,... | collective-permute-start | bytes 3145736 | tf_op jit(solution)/shard_map/ppermute | solution.py:354
  149.5 0.9 pick.4
  150.3 11.6 %collective-permute-done.21.refs_0_ = bf16[4,128,1024]{2,1,0:T(8,128)(2,1)S(1)} collective-permute-done((bf16[4,128,1024]{2,1,0:T(8,128)(2,1)S(1)}, bf16[4,128,1024]{2,1,0:T(8,128)(2,1)S(1)}, u32[]{:S(2)}, u32[]{:S(2)}) %collective-permute-start.21) | collective-permute-done | bytes 1048608 | tf_op jit(solution)/shard_map/ppermute | solution.py:354
  161.9 2.7 shard_map.61.refs_0_.resid_ref.refs_2_
  164.7 8.4 %collective-permute-done.22.refs_1_ = bf16[4,128,1024]{2,1,0:T(8,128)(2,1)S(1)} collective-permute-done((bf16[4,128,1024]{2,1,0:T(8,128)(2,1)S(1)}, bf16[4,128,1024]{2,1,0:T(8,128)(2,1)S(1)}, u32[]{:S(2)}, u32[]{:S(2)}) %collective-permute-start.22) | collective-permute-done | bytes 1048608 | tf_op jit(solution)/shard_map/ppermute | solution.py:354
  173.1 2.7 shard_map.62.refs_1_.resid_ref.refs_3_
  175.9 7.0 %collective-permute-start.24 = (bf16[512,1024]{1,0:T(8,128)(2,1)S(1)}, bf16[512,1024]{1,0:T(8,128)(2,1)S(1)}, u32[]{:S(2)}, u32[]{:S(2)}) collective-permute-start(bf16[512,1024]{1,0:T(8,128)(2,1)S(1)} %copy-done.5), channel_id=1, source_target_pairs={{64,96},{65,97},{66,98},{67,99},{68,100},{69,101},{70,102},{71,103... | collective-permute-start | bytes 3145736 | tf_op jit(solution)/shard_map/ppermute | solution.py:357
  182.9 3.2 %shard_map.63.acc_ref = f32[4,128,1024]{2,1,0:T(8,128)S(1)} custom-call(s32[2,2,48]{2,1,0:T(2,128)S(1)} %pad_add_fusion.1.near_ref, bf16[2,4,12,128,128]{4,3,2,1,0:T(8,128)(2,1)S(1)} %copy-done, bf16[4,128,1024]{2,1,0:T(8,128)(2,1)S(1)} %shard_map.61.refs_0_.resid_ref.refs_2_, bf16[4,128,1024]{2,1,0:T(8,128)(2,1)S(1)} %collective-permute-done.23.refs_1_.refs_2_), custom_call_target="tpu_custom_call" | custom-call | flops 1610612736 | bytes 8388608 | tf_op jit(solution)/shard_map/pallas_call | solution.py:284
  186.1 3.4 %shard_map.64.acc_ref = f32[4,128,1024]{2,1,0:T(8,128)S(1)} custom-call(s32[2,2,48]{2,1,0:T(2,128)S(1)} %pad_add_fusion.1.near_ref, bf16[2,4,12,128,128]{4,3,2,1,0:T(8,128)(2,1)S(1)} %copy-done, bf16[4,128,1024]{2,1,0:T(8,128)(2,1)S(1)} %shard_map.61.refs_0_.resid_ref.refs_2_, bf16[4,128,1024]{2,1,0:T(8,128)(2,1)S(1)} %shard_map.62.refs_1_.resid_ref.refs_3_, ...), custom_call_target="tpu_custom_call" | custom-call | flops 1610612736 | bytes 8388608 | tf_op jit(solution)/shard_map/pallas_call | solution.py:284
  189.5 16.4 %collective-permute-done.24.refs_1_ = bf16[512,1024]{1,0:T(8,128)(2,1)S(1)} collective-permute-done((bf16[512,1024]{1,0:T(8,128)(2,1)S(1)}, bf16[512,1024]{1,0:T(8,128)(2,1)S(1)}, u32[]{:S(2)}, u32[]{:S(2)}) %collective-permute-start.24) | collective-permute-done | bytes 1048608 | tf_op jit(solution)/shard_map/ppermute | solution.py:357
  205.9 5.1 %collective-permute-start.27 = (bf16[4,128,1024]{2,1,0:T(8,128)(2,1)S(1)}, bf16[4,128,1024]{2,1,0:T(8,128)(2,1)S(1)}, u32[]{:S(2)}, u32[]{:S(2)}) collective-permute-start(bf16[4,128,1024]{2,1,0:T(8,128)(2,1)S(1)} %shard_map.61.refs_0_.resid_ref.refs_2_), channel_id=1, source_target_pairs={{0,31},{1,2},{2,1},{3,4},{4,3},{5,6},{6,5},{7,8},{8,7},{9,10},{10,... | collective-permute-start | bytes 3145736 | tf_op jit(solution)/shard_map/ppermute | solution.py:354
  211.0 1.8 pick.5
  212.8 10.6 %collective-permute-done.27.refs_0_ = bf16[4,128,1024]{2,1,0:T(8,128)(2,1)S(1)} collective-permute-done((bf16[4,128,1024]{2,1,0:T(8,128)(2,1)S(1)}, bf16[4,128,1024]{2,1,0:T(8,128)(2,1)S(1)}, u32[]{:S(2)}, u32[]{:S(2)}) %collective-permute-start.27) | collective-permute-done | bytes 1048608 | tf_op jit(solution)/shard_map/ppermute | solution.py:354
  223.4 2.6 shard_map.65.refs_0_.resid_ref
  226.1 8.6 %collective-permute-done.32.refs_1_ = bf16[4,128,1024]{2,1,0:T(8,128)(2,1)S(1)} collective-permute-done((bf16[4,128,1024]{2,1,0:T(8,128)(2,1)S(1)}, bf16[4,128,1024]{2,1,0:T(8,128)(2,1)S(1)}, u32[]{:S(2)}, u32[]{:S(2)}) %collective-permute-start.32) | collective-permute-done | bytes 1048608 | tf_op jit(solution)/shard_map/ppermute | solution.py:354
  234.7 2.7 shard_map.66.refs_1_.resid_ref
  237.5 0.7 collective-permute-start.29
  238.2 5.1 %collective-permute-start.36 = (bf16[4,128,1024]{2,1,0:T(8,128)(2,1)S(1)}, bf16[4,128,1024]{2,1,0:T(8,128)(2,1)S(1)}, u32[]{:S(2)}, u32[]{:S(2)}) collective-permute-start(bf16[4,128,1024]{2,1,0:T(8,128)(2,1)S(1)} %shard_map.65.refs_0_.resid_ref), channel_id=1, source_target_pairs={{0,31},{1,2},{2,1},{3,4},{4,3},{5,6},{6,5},{7,8},{8,7},{9,10},{10,... | collective-permute-start | bytes 3145736 | tf_op jit(solution)/shard_map/ppermute | solution.py:354
  243.5 0.7 collective-permute-start.30
  244.2 1.3 collective-permute-start.33
  245.5 3.2 %shard_map.68.acc_ref = f32[4,128,1024]{2,1,0:T(8,128)S(1)} custom-call(s32[2,2,48]{2,1,0:T(2,128)S(1)} %pad_add_fusion.1.near_ref, bf16[2,4,12,128,128]{4,3,2,1,0:T(8,128)(2,1)S(1)} %copy-done, bf16[4,128,1024]{2,1,0:T(8,128)(2,1)S(1)} %shard_map.65.refs_0_.resid_ref, bf16[4,128,1024]{2,1,0:T(8,128)(2,1)S(1)} %collective-permute-done.34.refs_2_.refs_1_), custom_call_target="tpu_custom_call" | custom-call | flops 1610612736 | bytes 8388608 | tf_op jit(solution)/shard_map/pallas_call | solution.py:284
  248.7 1.6 collective-permute-start.28
  250.3 1.3 collective-permute-start.31
  251.6 3.4 %shard_map.67.acc_ref = f32[4,128,1024]{2,1,0:T(8,128)S(1)} custom-call(s32[2,2,48]{2,1,0:T(2,128)S(1)} %pad_add_fusion.1.near_ref, bf16[2,4,12,128,128]{4,3,2,1,0:T(8,128)(2,1)S(1)} %copy-done, bf16[4,128,1024]{2,1,0:T(8,128)(2,1)S(1)} %shard_map.65.refs_0_.resid_ref, bf16[4,128,1024]{2,1,0:T(8,128)(2,1)S(1)} %shard_map.66.refs_1_.resid_ref, ...), custom_call_target="tpu_custom_call" | custom-call | flops 1610612736 | bytes 8388608 | tf_op jit(solution)/shard_map/pallas_call | solution.py:284
  255.0 0.9 collective-permute-done.36.refs_0_
  255.9 2.8 shard_map.69.refs_2_
  258.7 8.4 %collective-permute-done.37.refs_1_ = bf16[4,128,1024]{2,1,0:T(8,128)(2,1)S(1)} collective-permute-done((bf16[4,128,1024]{2,1,0:T(8,128)(2,1)S(1)}, bf16[4,128,1024]{2,1,0:T(8,128)(2,1)S(1)}, u32[]{:S(2)}, u32[]{:S(2)}) %collective-permute-start.37) | collective-permute-done | bytes 1048608 | tf_op jit(solution)/shard_map/ppermute | solution.py:354
  267.1 2.7 shard_map.70.refs_7_
  269.8 22.6 %collective-permute-done.28.refs_4_ = bf16[2,128,1024]{2,1,0:T(8,128)(2,1)S(1)} collective-permute-done((bf16[2,128,1024]{2,1,0:T(8,128)(2,1)S(1)}, bf16[2,128,1024]{2,1,0:T(8,128)(2,1)S(1)}, u32[]{:S(2)}, u32[]{:S(2)}) %collective-permute-start.28) | collective-permute-done | bytes 524320 | tf_op jit(solution)/shard_map/ppermute | solution.py:357
  292.4 2.0 place.1
  (74 shorter events, 2.1 us)
Async XLA Ops:
  0.0 37.7 %collective-permute-start = (bf16[8,128,1024]{2,1,0:T(8,128)(2,1)}, bf16[8,128,1024]{2,1,0:T(8,128)(2,1)}, u32[]{:S(2)}, u32[]{:S(2)}) collective-permute-start(bf16[8,128,1024]{2,1,0:T(8,128)(2,1)} %bitcast.19), channel_id=1, source_target_pairs={{0,1},{1,0},{2,3},{3,2},{4,5},{5,4},{6,7},{7,6},{8,9},{9,8},{10,11... | collective-permute-start | bytes 6291464 | tf_op jit(solution)/shard_map/ppermute | solution.py:351
  0.7 12.3 %copy-start.10 = (s32[2,128,12]{1,0,2:T(2,128)S(1)}, s32[2,128,12]{1,0,2:T(2,128)}, u32[]{:S(2)}) copy-start(s32[2,128,12]{1,0,2:T(2,128)} %param.9) | copy-start | bytes 36868
  0.7 38.0 %copy-start = (bf16[2,4,12,128,128]{4,3,2,1,0:T(8,128)(2,1)S(1)}, bf16[2,4,12,128,128]{4,3,2,1,0:T(8,128)(2,1)}, u32[]{:S(2)}) copy-start(bf16[2,4,12,128,128]{4,3,2,1,0:T(8,128)(2,1)} %tiles_ref.31) | copy-start | bytes 9437188
  5.6 26.8 %collective-permute-start.11 = (bf16[640,1024]{1,0:T(8,128)(2,1)}, bf16[640,1024]{1,0:T(8,128)(2,1)}, u32[]{:S(2)}, u32[]{:S(2)}) collective-permute-start(bf16[640,1024]{1,0:T(8,128)(2,1)} %get-tuple-element.37), channel_id=1, source_target_pairs={{0,96},{1,97},{2,98},{3,99},{4,100},{5,101},{6,102},{7,103},{8,104... | collective-permute-start | bytes 3932168 | tf_op jit(solution)/shard_map/ppermute | solution.py:357
  7.4 7.4 %collective-permute-start.7 = (bf16[96,1024]{1,0:T(8,128)(2,1)}, bf16[96,1024]{1,0:T(8,128)(2,1)S(1)}, u32[]{:S(2)}, u32[]{:S(2)}) collective-permute-start(bf16[96,1024]{1,0:T(8,128)(2,1)} %get-tuple-element.36), channel_id=1, source_target_pairs={{0,96},{1,97},{2,98},{3,99},{4,100},{5,101},{6,102},{7,103},{8,104... | collective-permute-start | bytes 589832 | tf_op jit(solution)/shard_map/ppermute | solution.py:357
  8.0 41.4 %collective-permute-start.3 = (bf16[512,1024]{1,0:T(8,128)(2,1)}, bf16[512,1024]{1,0:T(8,128)(2,1)}, u32[]{:S(2)}, u32[]{:S(2)}) collective-permute-start(bf16[512,1024]{1,0:T(8,128)(2,1)} %get-tuple-element.32.refs_0_), channel_id=1, source_target_pairs={{0,32},{32,64},{64,96},{1,33},{33,65},{65,97},{2,34},{34,66},{66,9... | collective-permute-start | bytes 3145736 | tf_op jit(solution)/shard_map/ppermute | solution.py:357
  11.3 38.7 %collective-permute-start.4 = (bf16[512,1024]{1,0:T(8,128)(2,1)}, bf16[512,1024]{1,0:T(8,128)(2,1)}, u32[]{:S(2)}, u32[]{:S(2)}) collective-permute-start(bf16[512,1024]{1,0:T(8,128)(2,1)} %get-tuple-element.43.refs_1_), channel_id=1, source_target_pairs={{0,32},{1,33},{2,34},{3,35},{4,36},{5,37},{6,38},{7,39},{8,40},{9,... | collective-permute-start | bytes 3145736 | tf_op jit(solution)/shard_map/ppermute | solution.py:357
  14.8 9.2 %collective-permute-start.10 = (bf16[96,1024]{1,0:T(8,128)(2,1)S(1)}, bf16[96,1024]{1,0:T(8,128)(2,1)S(1)}, u32[]{:S(2)}, u32[]{:S(2)}) collective-permute-start(bf16[96,1024]{1,0:T(8,128)(2,1)S(1)} %collective-permute-done.7.refs_0_), channel_id=1, source_target_pairs={{0,16},{1,17},{2,18},{3,19},{4,20},{5,21},{6,22},{7,23},{8,24},{9,... | collective-permute-start | bytes 589832 | tf_op jit(solution)/shard_map/ppermute | solution.py:360
  23.9 7.8 %collective-permute-start.8 = (bf16[96,1024]{1,0:T(8,128)(2,1)S(1)}, bf16[96,1024]{1,0:T(8,128)(2,1)S(1)}, u32[]{:S(2)}, u32[]{:S(2)}) collective-permute-start(bf16[96,1024]{1,0:T(8,128)(2,1)S(1)} %collective-permute-done.7.refs_0_), channel_id=1, source_target_pairs={{0,8},{1,9},{2,10},{3,11},{4,12},{5,13},{6,14},{7,15},{8,16},{9,17... | collective-permute-start | bytes 589832 | tf_op jit(solution)/shard_map/ppermute | solution.py:360
  31.8 0.7 copy-start.7
  32.5 24.5 %collective-permute-start.1 = (bf16[512,1024]{1,0:T(8,128)(2,1)}, bf16[512,1024]{1,0:T(8,128)(2,1)}, u32[]{:S(2)}, u32[]{:S(2)}) collective-permute-start(bf16[512,1024]{1,0:T(8,128)(2,1)} %get-tuple-element.32.refs_0_), channel_id=1, source_target_pairs={{0,1},{1,0},{2,3},{3,2},{4,5},{5,4},{6,7},{7,6},{8,9},{9,8},{10,11... | collective-permute-start | bytes 3145736 | tf_op jit(solution)/shard_map/ppermute | solution.py:351
  32.5 32.1 %collective-permute-start.14 = (bf16[8,128,1024]{2,1,0:T(8,128)(2,1)}, bf16[8,128,1024]{2,1,0:T(8,128)(2,1)}, u32[]{:S(2)}, u32[]{:S(2)}) collective-permute-start(bf16[8,128,1024]{2,1,0:T(8,128)(2,1)} %bitcast.20), channel_id=1, source_target_pairs={{0,31},{1,2},{2,1},{3,4},{4,3},{5,6},{6,5},{7,8},{8,7},{9,10},{10,... | collective-permute-start | bytes 6291464 | tf_op jit(solution)/shard_map/ppermute | solution.py:354
  37.7 20.7 %collective-permute-start.2 = (bf16[512,1024]{1,0:T(8,128)(2,1)}, bf16[512,1024]{1,0:T(8,128)(2,1)S(1)}, u32[]{:S(2)}, u32[]{:S(2)}) collective-permute-start(bf16[512,1024]{1,0:T(8,128)(2,1)} %get-tuple-element.43.refs_1_), channel_id=1, source_target_pairs={{0,1},{1,0},{2,3},{3,2},{4,5},{5,4},{6,7},{7,6},{8,9},{9,8},{10,11... | collective-permute-start | bytes 3145736 | tf_op jit(solution)/shard_map/ppermute | solution.py:351
  38.7 1.6 copy-start.1
  44.6 12.8 %copy-start.8 = (bf16[96,1024]{1,0:T(8,128)(2,1)S(1)}, bf16[96,1024]{1,0:T(8,128)(2,1)}, u32[]{:S(2)}) copy-start(bf16[96,1024]{1,0:T(8,128)(2,1)} %copy-done.7) | copy-start | bytes 589828
  44.6 17.8 %copy-start.6 = (bf16[512,1024]{1,0:T(8,128)(2,1)S(1)}, bf16[512,1024]{1,0:T(8,128)(2,1)}, u32[]{:S(2)}) copy-start(bf16[512,1024]{1,0:T(8,128)(2,1)} %get-tuple-element.32.refs_0_) | copy-start | bytes 3145732
  49.4 13.0 %copy-start.5 = (bf16[512,1024]{1,0:T(8,128)(2,1)S(1)}, bf16[512,1024]{1,0:T(8,128)(2,1)}, u32[]{:S(2)}) copy-start(bf16[512,1024]{1,0:T(8,128)(2,1)} %get-tuple-element.43.refs_1_) | copy-start | bytes 3145732
  49.4 13.0 %collective-permute-start.13 = (bf16[640,1024]{1,0:T(8,128)(2,1)}, bf16[640,1024]{1,0:T(8,128)(2,1)S(1)}, u32[]{:S(2)}, u32[]{:S(2)}) collective-permute-start(bf16[640,1024]{1,0:T(8,128)(2,1)} %collective-permute-done.11.refs_9_), channel_id=1, source_target_pairs={{0,1},{1,0},{2,3},{3,2},{4,5},{5,4},{6,7},{7,6},{8,9},{9,8},{10,11... | collective-permute-start | bytes 3932168 | tf_op jit(solution)/shard_map/ppermute | solution.py:351
  50.0 6.9 %collective-permute-start.9 = (bf16[96,1024]{1,0:T(8,128)(2,1)S(1)}, bf16[96,1024]{1,0:T(8,128)(2,1)S(1)}, u32[]{:S(2)}, u32[]{:S(2)}) collective-permute-start(bf16[96,1024]{1,0:T(8,128)(2,1)S(1)} %collective-permute-done.7.refs_0_), channel_id=1, source_target_pairs={{0,24},{1,25},{2,26},{3,27},{4,28},{5,29},{6,30},{7,31},{8,0},{9,1... | collective-permute-start | bytes 589832 | tf_op jit(solution)/shard_map/ppermute | solution.py:360
  56.9 5.5 %collective-permute-start.5 = (bf16[512,1024]{1,0:T(8,128)(2,1)}, bf16[512,1024]{1,0:T(8,128)(2,1)S(1)}, u32[]{:S(2)}, u32[]{:S(2)}) collective-permute-start(bf16[512,1024]{1,0:T(8,128)(2,1)} %collective-permute-done.3.refs_4_.refs_0_), channel_id=1, source_target_pairs={{0,1},{1,0},{2,3},{3,2},{4,5},{5,4},{6,7},{7,6},{8,9},{9,8},{10,11... | collective-permute-start | bytes 3145736 | tf_op jit(solution)/shard_map/ppermute | solution.py:351
  56.9 5.5 %collective-permute-start.6 = (bf16[512,1024]{1,0:T(8,128)(2,1)}, bf16[512,1024]{1,0:T(8,128)(2,1)S(1)}, u32[]{:S(2)}, u32[]{:S(2)}) collective-permute-start(bf16[512,1024]{1,0:T(8,128)(2,1)} %collective-permute-done.4.refs_5_), channel_id=1, source_target_pairs={{0,1},{1,0},{2,3},{3,2},{4,5},{5,4},{6,7},{7,6},{8,9},{9,8},{10,11... | collective-permute-start | bytes 3145736 | tf_op jit(solution)/shard_map/ppermute | solution.py:351
  58.4 6.2 %copy-start.2 = (bf16[2,512,1024]{2,1,0:T(8,128)(2,1)S(1)}, bf16[2,512,1024]{2,1,0:T(8,128)(2,1)}, u32[]{:S(2)}) copy-start(bf16[2,512,1024]{2,1,0:T(8,128)(2,1)} %param.5) | copy-start | bytes 6291460
  58.5 3.9 %collective-permute-start.12 = (bf16[384,1024]{1,0:T(8,128)(2,1)S(1)}, bf16[384,1024]{1,0:T(8,128)(2,1)S(1)}, u32[]{:S(2)}, u32[]{:S(2)}) collective-permute-start(bf16[384,1024]{1,0:T(8,128)(2,1)S(1)} %join.1.refs_8_), channel_id=1, source_target_pairs={{0,1},{1,0},{2,3},{3,2},{4,5},{5,4},{6,7},{7,6},{8,9},{9,8},{10,11... | collective-permute-start | bytes 2359304 | tf_op jit(solution)/shard_map/ppermute | solution.py:351
  68.2 44.2 %collective-permute-start.15 = (bf16[4,128,1024]{2,1,0:T(8,128)(2,1)S(1)}, bf16[4,128,1024]{2,1,0:T(8,128)(2,1)S(1)}, u32[]{:S(2)}, u32[]{:S(2)}) collective-permute-start(bf16[4,128,1024]{2,1,0:T(8,128)(2,1)S(1)} %shard_map.57.refs_0_.resid_ref), channel_id=1, source_target_pairs={{0,1},{1,0},{2,3},{3,2},{4,5},{5,4},{6,7},{7,6},{8,9},{9,8},{10,11... | collective-permute-start | bytes 3145736 | tf_op jit(solution)/shard_map/ppermute | solution.py:351
  72.1 43.4 %collective-permute-start.17 = (bf16[4,128,1024]{2,1,0:T(8,128)(2,1)S(1)}, bf16[4,128,1024]{2,1,0:T(8,128)(2,1)S(1)}, u32[]{:S(2)}, u32[]{:S(2)}) collective-permute-start(bf16[4,128,1024]{2,1,0:T(8,128)(2,1)S(1)} %shard_map.58.refs_1_.resid_ref), channel_id=1, source_target_pairs={{0,1},{1,0},{2,3},{3,2},{4,5},{5,4},{6,7},{7,6},{8,9},{9,8},{10,11... | collective-permute-start | bytes 3145736 | tf_op jit(solution)/shard_map/ppermute | solution.py:351
  72.4 46.5 %collective-permute-start.18 = (bf16[512,1024]{1,0:T(8,128)(2,1)S(1)}, bf16[512,1024]{1,0:T(8,128)(2,1)S(1)}, u32[]{:S(2)}, u32[]{:S(2)}) collective-permute-start(bf16[512,1024]{1,0:T(8,128)(2,1)S(1)} %copy-done.5), channel_id=1, source_target_pairs={{32,96},{33,97},{34,98},{35,99},{36,100},{37,101},{38,102},{39,103... | collective-permute-start | bytes 3145736 | tf_op jit(solution)/shard_map/ppermute | solution.py:357
  73.1 62.5 %collective-permute-start.16 = (bf16[512,1024]{1,0:T(8,128)(2,1)}, bf16[512,1024]{1,0:T(8,128)(2,1)S(1)}, u32[]{:S(2)}, u32[]{:S(2)}) collective-permute-start(bf16[512,1024]{1,0:T(8,128)(2,1)} %collective-permute-done.3.refs_4_.refs_0_), channel_id=1, source_target_pairs={{64,96},{65,97},{66,98},{67,99},{68,100},{69,101},{70,102},{71,103... | collective-permute-start | bytes 3145736 | tf_op jit(solution)/shard_map/ppermute | solution.py:357
  119.0 30.5 %collective-permute-start.20 = (bf16[512,1024]{1,0:T(8,128)(2,1)S(1)}, bf16[512,1024]{1,0:T(8,128)(2,1)S(1)}, u32[]{:S(2)}, u32[]{:S(2)}) collective-permute-start(bf16[512,1024]{1,0:T(8,128)(2,1)S(1)} %collective-permute-done.18.refs_5_), channel_id=1, source_target_pairs={{0,1},{1,0},{2,3},{3,2},{4,5},{5,4},{6,7},{7,6},{8,9},{9,8},{10,11... | collective-permute-start | bytes 3145736 | tf_op jit(solution)/shard_map/ppermute | solution.py:351
  135.6 13.8 %collective-permute-start.19 = (bf16[512,1024]{1,0:T(8,128)(2,1)S(1)}, bf16[512,1024]{1,0:T(8,128)(2,1)S(1)}, u32[]{:S(2)}, u32[]{:S(2)}) collective-permute-start(bf16[512,1024]{1,0:T(8,128)(2,1)S(1)} %collective-permute-done.16.refs_4_), channel_id=1, source_target_pairs={{0,1},{1,0},{2,3},{3,2},{4,5},{5,4},{6,7},{7,6},{8,9},{9,8},{10,11... | collective-permute-start | bytes 3145736 | tf_op jit(solution)/shard_map/ppermute | solution.py:351
  135.7 26.2 %collective-permute-start.21 = (bf16[4,128,1024]{2,1,0:T(8,128)(2,1)S(1)}, bf16[4,128,1024]{2,1,0:T(8,128)(2,1)S(1)}, u32[]{:S(2)}, u32[]{:S(2)}) collective-permute-start(bf16[4,128,1024]{2,1,0:T(8,128)(2,1)S(1)} %shard_map.57.refs_0_.resid_ref), channel_id=1, source_target_pairs={{0,31},{1,2},{2,1},{3,4},{4,3},{5,6},{6,5},{7,8},{8,7},{9,10},{10,... | collective-permute-start | bytes 3145736 | tf_op jit(solution)/shard_map/ppermute | solution.py:354
  149.4 23.7 %collective-permute-start.22 = (bf16[4,128,1024]{2,1,0:T(8,128)(2,1)S(1)}, bf16[4,128,1024]{2,1,0:T(8,128)(2,1)S(1)}, u32[]{:S(2)}, u32[]{:S(2)}) collective-permute-start(bf16[4,128,1024]{2,1,0:T(8,128)(2,1)S(1)} %shard_map.58.refs_1_.resid_ref), channel_id=1, source_target_pairs={{0,31},{1,2},{2,1},{3,4},{4,3},{5,6},{6,5},{7,8},{8,7},{9,10},{10,... | collective-permute-start | bytes 3145736 | tf_op jit(solution)/shard_map/ppermute | solution.py:354
  164.6 18.2 %collective-permute-start.23 = (bf16[4,128,1024]{2,1,0:T(8,128)(2,1)S(1)}, bf16[4,128,1024]{2,1,0:T(8,128)(2,1)S(1)}, u32[]{:S(2)}, u32[]{:S(2)}) collective-permute-start(bf16[4,128,1024]{2,1,0:T(8,128)(2,1)S(1)} %shard_map.61.refs_0_.resid_ref.refs_2_), channel_id=1, source_target_pairs={{0,1},{1,0},{2,3},{3,2},{4,5},{5,4},{6,7},{7,6},{8,9},{9,8},{10,11... | collective-permute-start | bytes 3145736 | tf_op jit(solution)/shard_map/ppermute | solution.py:351
  175.8 10.3 %collective-permute-start.25 = (bf16[4,128,1024]{2,1,0:T(8,128)(2,1)S(1)}, bf16[4,128,1024]{2,1,0:T(8,128)(2,1)S(1)}, u32[]{:S(2)}, u32[]{:S(2)}) collective-permute-start(bf16[4,128,1024]{2,1,0:T(8,128)(2,1)S(1)} %shard_map.62.refs_1_.resid_ref.refs_3_), channel_id=1, source_target_pairs={{0,1},{1,0},{2,3},{3,2},{4,5},{5,4},{6,7},{7,6},{8,9},{9,8},{10,11... | collective-permute-start | bytes 3145736 | tf_op jit(solution)/shard_map/ppermute | solution.py:351
  175.9 30.0 %collective-permute-start.24 = (bf16[512,1024]{1,0:T(8,128)(2,1)S(1)}, bf16[512,1024]{1,0:T(8,128)(2,1)S(1)}, u32[]{:S(2)}, u32[]{:S(2)}) collective-permute-start(bf16[512,1024]{1,0:T(8,128)(2,1)S(1)} %copy-done.5), channel_id=1, source_target_pairs={{64,96},{65,97},{66,98},{67,99},{68,100},{69,101},{70,102},{71,103... | collective-permute-start | bytes 3145736 | tf_op jit(solution)/shard_map/ppermute | solution.py:357
  186.1 24.9 %copy-start.9 = (s32[4]{0:T(128)S(1)}, s32[4]{0:T(128)}, u32[]{:S(2)}) copy-start(s32[4]{0:T(128)} %pad_add_fusion.4.meta_ref) | copy-start | bytes 52
  205.9 5.1 %collective-permute-start.26 = (bf16[512,1024]{1,0:T(8,128)(2,1)S(1)}, bf16[512,1024]{1,0:T(8,128)(2,1)S(1)}, u32[]{:S(2)}, u32[]{:S(2)}) collective-permute-start(bf16[512,1024]{1,0:T(8,128)(2,1)S(1)} %collective-permute-done.24.refs_1_), channel_id=1, source_target_pairs={{0,1},{1,0},{2,3},{3,2},{4,5},{5,4},{6,7},{7,6},{8,9},{9,8},{10,11... | collective-permute-start | bytes 3145736 | tf_op jit(solution)/shard_map/ppermute | solution.py:351
  205.9 17.6 %collective-permute-start.27 = (bf16[4,128,1024]{2,1,0:T(8,128)(2,1)S(1)}, bf16[4,128,1024]{2,1,0:T(8,128)(2,1)S(1)}, u32[]{:S(2)}, u32[]{:S(2)}) collective-permute-start(bf16[4,128,1024]{2,1,0:T(8,128)(2,1)S(1)} %shard_map.61.refs_0_.resid_ref.refs_2_), channel_id=1, source_target_pairs={{0,31},{1,2},{2,1},{3,4},{4,3},{5,6},{6,5},{7,8},{8,7},{9,10},{10,... | collective-permute-start | bytes 3145736 | tf_op jit(solution)/shard_map/ppermute | solution.py:354
  210.9 23.7 %collective-permute-start.32 = (bf16[4,128,1024]{2,1,0:T(8,128)(2,1)S(1)}, bf16[4,128,1024]{2,1,0:T(8,128)(2,1)S(1)}, u32[]{:S(2)}, u32[]{:S(2)}) collective-permute-start(bf16[4,128,1024]{2,1,0:T(8,128)(2,1)S(1)} %shard_map.62.refs_1_.resid_ref.refs_3_), channel_id=1, source_target_pairs={{0,31},{1,2},{2,1},{3,4},{4,3},{5,6},{6,5},{7,8},{8,7},{9,10},{10,... | collective-permute-start | bytes 3145736 | tf_op jit(solution)/shard_map/ppermute | solution.py:354
  226.0 18.2 %collective-permute-start.34 = (bf16[4,128,1024]{2,1,0:T(8,128)(2,1)S(1)}, bf16[4,128,1024]{2,1,0:T(8,128)(2,1)S(1)}, u32[]{:S(2)}, u32[]{:S(2)}) collective-permute-start(bf16[4,128,1024]{2,1,0:T(8,128)(2,1)S(1)} %shard_map.65.refs_0_.resid_ref), channel_id=1, source_target_pairs={{0,1},{1,0},{2,3},{3,2},{4,5},{5,4},{6,7},{7,6},{8,9},{9,8},{10,11... | collective-permute-start | bytes 3145736 | tf_op jit(solution)/shard_map/ppermute | solution.py:351
  237.4 11.2 %collective-permute-start.35 = (bf16[4,128,1024]{2,1,0:T(8,128)(2,1)S(1)}, bf16[4,128,1024]{2,1,0:T(8,128)(2,1)S(1)}, u32[]{:S(2)}, u32[]{:S(2)}) collective-permute-start(bf16[4,128,1024]{2,1,0:T(8,128)(2,1)S(1)} %shard_map.66.refs_1_.resid_ref), channel_id=1, source_target_pairs={{0,1},{1,0},{2,3},{3,2},{4,5},{5,4},{6,7},{7,6},{8,9},{9,8},{10,11... | collective-permute-start | bytes 3145736 | tf_op jit(solution)/shard_map/ppermute | solution.py:351
  237.5 5.9 %collective-permute-start.29 = (bf16[2,128,1024]{2,1,0:T(8,128)(2,1)S(1)}, bf16[2,128,1024]{2,1,0:T(8,128)(2,1)S(1)}, u32[]{:S(2)}, u32[]{:S(2)}) collective-permute-start(bf16[2,128,1024]{2,1,0:T(8,128)(2,1)S(1)} %get-tuple-element.57), channel_id=1, source_target_pairs={{96,0},{97,1},{98,2},{99,3},{100,4},{101,5},{102,6},{103,7},{104,8... | collective-permute-start | bytes 1572872 | tf_op jit(solution)/shard_map/ppermute | solution.py:357
  238.2 17.6 %collective-permute-start.36 = (bf16[4,128,1024]{2,1,0:T(8,128)(2,1)S(1)}, bf16[4,128,1024]{2,1,0:T(8,128)(2,1)S(1)}, u32[]{:S(2)}, u32[]{:S(2)}) collective-permute-start(bf16[4,128,1024]{2,1,0:T(8,128)(2,1)S(1)} %shard_map.65.refs_0_.resid_ref), channel_id=1, source_target_pairs={{0,31},{1,2},{2,1},{3,4},{4,3},{5,6},{6,5},{7,8},{8,7},{9,10},{10,... | collective-permute-start | bytes 3145736 | tf_op jit(solution)/shard_map/ppermute | solution.py:354
  243.4 23.7 %collective-permute-start.37 = (bf16[4,128,1024]{2,1,0:T(8,128)(2,1)S(1)}, bf16[4,128,1024]{2,1,0:T(8,128)(2,1)S(1)}, u32[]{:S(2)}, u32[]{:S(2)}) collective-permute-start(bf16[4,128,1024]{2,1,0:T(8,128)(2,1)S(1)} %shard_map.66.refs_1_.resid_ref), channel_id=1, source_target_pairs={{0,31},{1,2},{2,1},{3,4},{4,3},{5,6},{6,5},{7,8},{8,7},{9,10},{10,... | collective-permute-start | bytes 3145736 | tf_op jit(solution)/shard_map/ppermute | solution.py:354
  243.5 6.8 %collective-permute-start.30 = (bf16[2,128,1024]{2,1,0:T(8,128)(2,1)S(1)}, bf16[2,128,1024]{2,1,0:T(8,128)(2,1)S(1)}, u32[]{:S(2)}, u32[]{:S(2)}) collective-permute-start(bf16[2,128,1024]{2,1,0:T(8,128)(2,1)S(1)} %collective-permute-done.29), channel_id=1, source_target_pairs={{0,32},{1,33},{2,34},{3,35},{4,36},{5,37},{6,38},{7,39},{8,40},{9,... | collective-permute-start | bytes 1572872 | tf_op jit(solution)/shard_map/ppermute | solution.py:357
  244.2 48.2 %collective-permute-start.33 = (bf16[4,128,1024]{2,1,0:T(8,128)(2,1)S(1)}, bf16[4,128,1024]{2,1,0:T(8,128)(2,1)S(1)}, u32[]{:S(2)}, u32[]{:S(2)}) collective-permute-start(bf16[4,128,1024]{2,1,0:T(8,128)(2,1)S(1)} %shard_map.66.refs_1_.resid_ref), channel_id=1, source_target_pairs={{96,64},{97,65},{98,66},{99,67},{100,68},{101,69},{102,70},{103,71... | collective-permute-start | bytes 3145736 | tf_op jit(solution)/shard_map/ppermute | solution.py:357
  248.7 7.2 %copy-start.3 = (bf16[1,1024,1024]{2,1,0:T(8,128)(2,1)S(1)}, bf16[1,1024,1024]{2,1,0:T(8,128)(2,1)}, u32[]{:S(2)}) copy-start(bf16[1,1024,1024]{2,1,0:T(8,128)(2,1)} %param.7) | copy-start | bytes 6291460
  248.7 7.2 %copy-start.4 = (bf16[1,1024,1024]{2,1,0:T(8,128)(2,1)S(1)}, bf16[1,1024,1024]{2,1,0:T(8,128)(2,1)}, u32[]{:S(2)}) copy-start(bf16[1,1024,1024]{2,1,0:T(8,128)(2,1)} %param.8) | copy-start | bytes 6291460
  248.7 43.7 %collective-permute-start.28 = (bf16[2,128,1024]{2,1,0:T(8,128)(2,1)S(1)}, bf16[2,128,1024]{2,1,0:T(8,128)(2,1)S(1)}, u32[]{:S(2)}, u32[]{:S(2)}) collective-permute-start(bf16[2,128,1024]{2,1,0:T(8,128)(2,1)S(1)} %get-tuple-element.58), channel_id=1, source_target_pairs={{96,64},{97,65},{98,66},{99,67},{100,68},{101,69},{102,70},{103,71... | collective-permute-start | bytes 1572872 | tf_op jit(solution)/shard_map/ppermute | solution.py:357
  250.3 42.1 %collective-permute-start.31 = (bf16[2,128,1024]{2,1,0:T(8,128)(2,1)S(1)}, bf16[2,128,1024]{2,1,0:T(8,128)(2,1)S(1)}, u32[]{:S(2)}, u32[]{:S(2)}) collective-permute-start(bf16[2,128,1024]{2,1,0:T(8,128)(2,1)S(1)} %collective-permute-done.30), channel_id=1, source_target_pairs={{32,64},{33,65},{34,66},{35,67},{36,68},{37,69},{38,70},{39,71},{4... | collective-permute-start | bytes 1572872 | tf_op jit(solution)/shard_map/ppermute | solution.py:357
where the time goes:
time: 295 us
  waiting for transfers between devices  126 us (43%)
  starting transfers between devices  96.3 us (33%)
  Pallas kernels  64.9 us (22%)
  local copies, waits for them, and re-layouts  3.38 us (1%)
  other arithmetic  3.26 us (1%)
    ppermute x12, starting transfers between devices, hop(): return lax.ppermute(value, 'section', pairs)  59.7 us
    ppermute x12, waiting for transfers between devices, hop(): return lax.ppermute(value, 'section', pairs)  55.4 us
    ppermute x7, waiting for transfers between devices, cross(): return lax.ppermute(value, 'dom', cross_pairs)  48.5 us
    pallas_call x8, Pallas kernels, early(): pl.pallas_call(functools.partial(early_kernel, span, n_src), out_shape=ja...  28.8 us
    ppermute x7, starting transfers between devices, cross(): return lax.ppermute(value, 'dom', cross_pairs)  28.5 us
    pallas_call x8, Pallas kernels, late(): pl.pallas_call(functools.partial(late_kernel, span, len(crosses), final),...  23.3 us
    ppermute x3, waiting for transfers between devices, along_z(): lax.ppermute(value, 'dom', [(p, (p + by * row_parts) % parts) for p in ra...  18.3 us
  transfers between devices with their start and end apart: 38, of which 13 were waited for; matrix products, arithmetic and copies ran while one was open for 1% of the time, Pallas kernels for 20%

commit v1 on v0

--- a/solution.py
+++ b/solution.py
@@ -128,34 +128,32 @@
 CUT = 384
 
 
-def mine_kernel(meta_ref, first_ref, second_ref, quarter_ref, rest_ref, a_ref, b_ref, sem):
-    size = quarter_ref.shape[0]
-    mid = a_ref.shape[0]
+def mine_kernel(pieces, meta_ref, first_ref, second_ref, *refs):
+    *outs, sem = refs
 
     def fetch(src):
-        start = pl.multiple_of(meta_ref[0] * size, size)
-        pltpu.make_async_copy(src.at[pl.ds(start, size)], quarter_ref, sem.at[0]).start()
-        pltpu.make_async_copy(src.at[pl.ds(4 * size, rest_ref.shape[0])], rest_ref, sem.at[1]).start()
-        pltpu.make_async_copy(src.at[pl.ds(0, mid)], a_ref, sem.at[2]).start()
-        pltpu.make_async_copy(src.at[pl.ds(mid, mid)], b_ref, sem.at[3]).start()
+        for k, ((start, per_z), dst) in enumerate(zip(pieces, outs)):
+            size = dst.shape[0]
+            rows = pl.ds(pl.multiple_of(meta_ref[0] * size, size) if per_z else start, size)
+            pltpu.make_async_copy(src.at[rows], dst, sem.at[k]).start()
 
     pl.when(meta_ref[1] == 0)(functools.partial(fetch, first_ref))
     pl.when(meta_ref[1] != 0)(functools.partial(fetch, second_ref))
-    for k, dst in enumerate((quarter_ref, rest_ref, a_ref, b_ref)):
+    for k, dst in enumerate(outs):
         pltpu.make_async_copy(dst, dst, sem.at[k]).wait()
 
 
-def mine(meta, w_first, w_second):
+def mine(meta, w_first, w_second, pieces):
     feat = w_first.shape[0]
-    rows = (CUT // 4, feat - CUT, feat // 2, feat // 2)
+    fixed = tuple((start or 0, start is None) for start, _ in pieces)
     return pl.pallas_call(
-        mine_kernel,
-        out_shape=[jax.ShapeDtypeStruct((size, feat), jnp.bfloat16) for size in rows],
+        functools.partial(mine_kernel, fixed),
+        out_shape=[jax.ShapeDtypeStruct((size, feat), jnp.bfloat16) for _, size in pieces],
         in_specs=[SMEM, HBM, HBM],
-        out_specs=[VMEM] * 4,
-        scratch_shapes=[pltpu.SemaphoreType.DMA((4,))],
-        compiler_params=pltpu.CompilerParams(vmem_limit_bytes=56 * MIB),
-        cost_estimate=pl.CostEstimate(flops=0, bytes_accessed=8 * MIB, transcendentals=0),
+        out_specs=[VMEM] * len(pieces),
+        scratch_shapes=[pltpu.SemaphoreType.DMA((len(pieces),))],
+        compiler_params=pltpu.CompilerParams(vmem_limit_bytes=52 * MIB),
+        cost_estimate=pl.CostEstimate(flops=0, bytes_accessed=4 * MIB, transcendentals=0),
         name="mine",
     )(meta, w_first, w_second)
 
@@ -383,12 +381,13 @@
             over_out.append(cross(out[s]))
         return out, chip_out, over_out, [sums(s, out, chip_out) for s in range(spans)]
 
-    shard, rest, mine_a, mine_b = mine(metas[3], w_first, w_second)
+    shard, rest = mine(metas[3], w_first, w_second, [(None, CUT // 4), (CUT, feat - CUT)])
     shard = hop(shard, [(0, hub)])
+    zero_b = hop(rest, [(0, hub)])
+    mine_a, mine_b = mine(metas[3], w_first, w_second, [(0, feat // 2), (feat // 2, feat // 2)])
     start = features.reshape(spans * blk_rows, tile_len, feat)
     chip0 = swap(start)
-    over0 = cross(start)
-    zero_b = hop(rest, [(0, hub)])
+    over0 = [cross(start[s * blk_rows : (s + 1) * blk_rows]) for s in range(spans)]
     next_a = hop(mine_a, [(0, 1), (1, 2), (2, hub)])
     zero_a = join(shard, along_z(shard, 1), along_z(shard, -1), along_z(shard, 2))
     next_b = hop(mine_b, [(0, 1)])
@@ -401,25 +400,21 @@
     one_b = hop(after(mine_b, *acc), [(1, hub)])
     two_b = hop(after(mine_b, *acc), [(2, hub)])
     kept = [mine_a, mine_b, swap(mine_a), swap(mine_b)]
-    swap_next = [swap(after(next_a, *acc)), swap(after(next_b, *acc))]
-    swap_zero = [swap(zero_a), swap(after(zero_b, *acc))]
+    swap_next = [swap(next_a), swap(next_b)]
+    swap_zero = [swap(zero_a), swap(zero_b)]
     got = [*kept, next_a, next_b, *swap_next, zero_a, zero_b, *swap_zero]
-    h1, _, over1, acc = layer(0, acc, [start] * spans, [over0], pick(metas[0], got))
-    one_a, one_b = after(one_a, *acc), after(one_b, *acc)
+    h1, _, over1, acc = layer(0, acc, [start] * spans, over0, pick(metas[0], got))
+    one_a, one_b = after(one_a, h1[1]), after(one_b, h1[1])
     got = [*kept, one_a, one_b, swap(one_a), swap(one_b)]
     weights = pick(metas[1], got)
 
     h2, _, over2, acc = layer(1, acc, h1, over1, weights)
-    two_b = after(two_b, *acc)
+    two_b = after(two_b, h2[1])
     got = [next_a, two_b, swap_next[0], swap(two_b)]
     weights = pick(metas[2], got)
 
     h3, _, over3, acc = layer(2, acc, h2, over2, weights)
-    half = blk_rows // 2
-    away = hop(h3[0][half:], [(hub, 0)])
-    away = hop(away, [(0, 1)])
-    away = hop(away, [(1, 2)])
-    back = [hop(h3[0][:half], [(hub, 2)]), away, hop(h3[1], [(hub, 2)])]
+    back = [hop(h3[s], [(hub, 2)]) for s in range(spans)]
 
     out = None
     for s in range(spans):

time: 295 us -> 231 us (0.78)
  waiting for transfers between devices: 126 us -> 88.1 us
  starting transfers between devices: 96.3 us -> 72.8 us
    ppermute x12 -> x9, starting transfers between devices: 59.7 us -> 40.6 us  [hop(): return lax.ppermute(value, 'section', pairs)]
    ppermute x7 -> x8, waiting for transfers between devices: 48.5 us -> 30.4 us  [cross(): return lax.ppermute(value, 'dom', cross_pairs)]
    ppermute x12 -> x9, waiting for transfers between devices: 55.4 us -> 46.7 us  [hop(): return lax.ppermute(value, 'section', pairs)]
    ppermute x7 -> x8, starting transfers between devices: 28.5 us -> 20.5 us  [cross(): return lax.ppermute(value, 'dom', cross_pairs)]
    ppermute x3, waiting for transfers between devices: 18.3 us -> 11 us  [along_z(): lax.ppermute(value, 'dom', [(p, (p + by * row_parts) % parts) for p in ra...]
    ppermute x16, waiting for transfers between devices: 3.88 us -> 0.04 us  [swap(): return lax.ppermute(value, 'dom', swap_pairs)]
    pallas_call x1 -> x2, Pallas kernels: 4.93 us -> 6.46 us  [mine(): pl.pallas_call(functools.partial(mine_kernel, fixed), out_shape=[jax.Shap...]
  transfers between devices with their start and end apart: 38 -> 36, of which waited for: 13 -> 12; matrix products, arithmetic and copies ran while one was open for 1% -> 2% of each run, Pallas kernels for 20% -> 25%
where the time goes in v1:
time: 231 us; the launch traced here: 230 us
  waiting for transfers between devices  88.1 us (38%)
  starting transfers between devices  72.8 us (32%)
  Pallas kernels  64.1 us (28%)
  local copies, waits for them, and re-layouts  2.48 us (1%)
    ppermute x9, waiting for transfers between devices, hop(): return lax.ppermute(value, 'section', pairs)  46.7 us
    ppermute x9, starting transfers between devices, hop(): return lax.ppermute(value, 'section', pairs)  40.6 us
    ppermute x8, waiting for transfers between devices, cross(): return lax.ppermute(value, 'dom', cross_pairs)  30.4 us
    pallas_call x8, Pallas kernels, early(): pl.pallas_call(functools.partial(early_kernel, span, n_src), out_shape=ja...  28.8 us
    pallas_call x8, Pallas kernels, late(): pl.pallas_call(functools.partial(late_kernel, span, len(crosses), final),...  21 us
    ppermute x8, starting transfers between devices, cross(): return lax.ppermute(value, 'dom', cross_pairs)  20.5 us
    ppermute x3, waiting for transfers between devices, along_z(): lax.ppermute(value, 'dom', [(p, (p + by * row_parts) % parts) for p in ra...  11 us
    ppermute x3, starting transfers between devices, along_z(): lax.ppermute(value, 'dom', [(p, (p + by * row_parts) % parts) for p in ra...  7.92 us
  transfers between devices with their start and end apart: 36, of which 12 were waited for; matrix products, arithmetic and copies ran while one was open for 2% of the time, Pallas kernels for 25%

profile of v1, /device:TPU:4, one launch (start us, length us, event | category | flops | bytes accessed | tf_op | source)
XLA Modules:
  0.0 230.2 jit_solution(8627123730284609907)
XLA Ops:
  0.1 3.4 %mine.2 = (bf16[512,1024]{1,0:T(8,128)(2,1)}, bf16[512,1024]{1,0:T(8,128)(2,1)}) custom-call(s32[4]{0:T(128)S(1)} %pad_add_fusion.4.meta_ref, bf16[1024,1024]{1,0:T(8,128)(2,1)} %bitcast.26, bf16[1024,1024]{1,0:T(8,128)(2,1)} %bitcast.30), custom_call_target="tpu_custom_call" | custom-call | bytes 4194304 | tf_op jit(solution)/shard_map/mine/pallas_call | solution.py:149
  3.5 3.2 %collective-permute-start.3 = (bf16[512,1024]{1,0:T(8,128)(2,1)}, bf16[512,1024]{1,0:T(8,128)(2,1)S(1)}, u32[]{:S(2)}, u32[]{:S(2)}) collective-permute-start(bf16[512,1024]{1,0:T(8,128)(2,1)} %get-tuple-element.30.refs_0_), channel_id=1, source_target_pairs={{0,32},{32,64},{64,96},{1,33},{33,65},{65,97},{2,34},{34,66},{66,9... | collective-permute-start | bytes 3145736 | tf_op jit(solution)/shard_map/ppermute | solution.py:355
  6.8 3.1 %mine.3 = (bf16[96,1024]{1,0:T(8,128)(2,1)S(1)}, bf16[640,1024]{1,0:T(8,128)(2,1)}) custom-call(s32[4]{0:T(128)S(1)} %pad_add_fusion.4.meta_ref, bf16[1024,1024]{1,0:T(8,128)(2,1)} %bitcast.27, bf16[1024,1024]{1,0:T(8,128)(2,1)} %bitcast.31), custom_call_target="tpu_custom_call" | custom-call | bytes 4194304 | tf_op jit(solution)/shard_map/mine/pallas_call | solution.py:149
  9.9 0.7 collective-permute-start.7
  10.6 0.6 collective-permute-start
  11.2 3.9 %collective-permute-start.10 = (bf16[96,1024]{1,0:T(8,128)(2,1)S(1)}, bf16[96,1024]{1,0:T(8,128)(2,1)S(1)}, u32[]{:S(2)}, u32[]{:S(2)}) collective-permute-start(bf16[96,1024]{1,0:T(8,128)(2,1)S(1)} %collective-permute-done.7.refs_0_), channel_id=1, source_target_pairs={{0,16},{1,17},{2,18},{3,19},{4,20},{5,21},{6,22},{7,23},{8,24},{9,... | collective-permute-start | bytes 589832 | tf_op jit(solution)/shard_map/ppermute | solution.py:358
  15.1 1.7 collective-permute-start.11
  16.8 3.4 %collective-permute-done.10.refs_3_ = bf16[96,1024]{1,0:T(8,128)(2,1)S(1)} collective-permute-done((bf16[96,1024]{1,0:T(8,128)(2,1)S(1)}, bf16[96,1024]{1,0:T(8,128)(2,1)S(1)}, u32[]{:S(2)}, u32[]{:S(2)}) %collective-permute-start.10) | collective-permute-done | bytes 196640 | tf_op jit(solution)/shard_map/ppermute | solution.py:358
  20.2 3.4 %collective-permute-start.9 = (bf16[96,1024]{1,0:T(8,128)(2,1)S(1)}, bf16[96,1024]{1,0:T(8,128)(2,1)}, u32[]{:S(2)}, u32[]{:S(2)}) collective-permute-start(bf16[96,1024]{1,0:T(8,128)(2,1)S(1)} %collective-permute-done.7.refs_0_), channel_id=1, source_target_pairs={{0,24},{1,25},{2,26},{3,27},{4,28},{5,29},{6,30},{7,31},{8,0},{9,1... | collective-permute-start | bytes 589832 | tf_op jit(solution)/shard_map/ppermute | solution.py:358
  23.6 3.6 %collective-permute-done.9.refs_2_ = bf16[96,1024]{1,0:T(8,128)(2,1)} collective-permute-done((bf16[96,1024]{1,0:T(8,128)(2,1)S(1)}, bf16[96,1024]{1,0:T(8,128)(2,1)}, u32[]{:S(2)}, u32[]{:S(2)}) %collective-permute-start.9) | collective-permute-done | bytes 196640 | tf_op jit(solution)/shard_map/ppermute | solution.py:358
  27.2 0.6 collective-permute-start.8
  27.8 1.5 fusion.3
  29.3 0.7 copy.16
  30.0 0.8 reshape.312
  30.7 4.0 %collective-permute-done.8.refs_1_ = bf16[96,1024]{1,0:T(8,128)(2,1)} collective-permute-done((bf16[96,1024]{1,0:T(8,128)(2,1)S(1)}, bf16[96,1024]{1,0:T(8,128)(2,1)}, u32[]{:S(2)}, u32[]{:S(2)}) %collective-permute-start.8) | collective-permute-done | bytes 196640 | tf_op jit(solution)/shard_map/ppermute | solution.py:358
  34.7 1.7 collective-permute-start.4
  36.5 2.1 join.1.refs_8_
  38.7 0.6 collective-permute-start.12
  39.3 0.8 reshape.313
  40.4 4.6 %collective-permute-start.14 = (bf16[4,128,1024]{2,1,0:T(8,128)(2,1)S(1)}, bf16[4,128,1024]{2,1,0:T(8,128)(2,1)S(1)}, u32[]{:S(2)}, u32[]{:S(2)}) collective-permute-start(bf16[4,128,1024]{2,1,0:T(8,128)(2,1)S(1)} %bitcast.35), channel_id=1, source_target_pairs={{0,31},{1,2},{2,1},{3,4},{4,3},{5,6},{6,5},{7,8},{8,7},{9,10},{10,... | collective-permute-start | bytes 3145736 | tf_op jit(solution)/shard_map/ppermute | solution.py:352
  45.7 0.6 collective-permute-start.15
  46.7 4.8 %shard_map.57.acc_ref = f32[4,128,1024]{2,1,0:T(8,128)S(1)} custom-call(s32[2,2,48]{2,1,0:T(2,128)S(1)} %pad_add_fusion.1.near_ref, bf16[2,4,12,128,128]{4,3,2,1,0:T(8,128)(2,1)S(1)} %copy-done, bf16[8,128,1024]{2,1,0:T(8,128)(2,1)S(1)} %bitcast.22, bf16[8,128,1024]{2,1,0:T(8,128)(2,1)} %collective-permute-done.refs_1_), custom_call_target="tpu_custom_call" | custom-call | flops 1610612736 | bytes 8388608 | tf_op jit(solution)/shard_map/pallas_call | solution.py:282
  51.5 4.3 %shard_map.55.acc_ref = f32[4,128,1024]{2,1,0:T(8,128)S(1)} custom-call(s32[2,2,48]{2,1,0:T(2,128)S(1)} %pad_add_fusion.1.near_ref, bf16[2,4,12,128,128]{4,3,2,1,0:T(8,128)(2,1)S(1)} %copy-done, bf16[8,128,1024]{2,1,0:T(8,128)(2,1)S(1)} %bitcast.23, bf16[8,128,1024]{2,1,0:T(8,128)(2,1)} %collective-permute-done.refs_1_), custom_call_target="tpu_custom_call" | custom-call | flops 1610612736 | bytes 8388608 | tf_op jit(solution)/shard_map/pallas_call | solution.py:282
  55.8 18.6 %collective-permute-start.17 = (bf16[512,1024]{1,0:T(8,128)(2,1)S(1)}, bf16[512,1024]{1,0:T(8,128)(2,1)S(1)}, u32[]{:S(2)}, u32[]{:S(2)}) collective-permute-start(bf16[512,1024]{1,0:T(8,128)(2,1)S(1)} %collective-permute-done.3.refs_4_.refs_0_), channel_id=1, source_target_pairs={{64,96},{65,97},{66,98},{67,99},{68,100},{69,101},{70,102},{71,103... | collective-permute-start | bytes 3145736 | tf_op jit(solution)/shard_map/ppermute | solution.py:355
  74.4 0.7 collective-permute-start.18
  75.2 1.9 pick.3
  77.1 2.6 %shard_map.56.refs_0_.resid_ref = bf16[4,128,1024]{2,1,0:T(8,128)(2,1)S(1)} custom-call(s32[2,3,48]{2,1,0:T(4,128)S(1)} %pad_add_fusion.far_ref, s32[4]{0:T(128)S(1)} %get-tuple-element.28.meta_ref, bf16[2,4,12,128,128]{4,3,2,1,0:T(8,128)(2,1)S(1)} %copy-done, f32[4,128,1024]{2,1,0:T(8,128)S(1)} %shard_map.55.acc_ref, bf16[8,128,1024]{2,1,0:T(8,128)(2,1)S(1)} %bitcast.24, ...), custom_call_target="tpu_custom_call" | custom-call | flops 2147483648 | bytes 8388608 | tf_op jit(solution)/shard_map/pallas_call | solution.py:311
  79.8 2.7 %shard_map.58.refs_1_.resid_ref = bf16[4,128,1024]{2,1,0:T(8,128)(2,1)S(1)} custom-call(s32[2,3,48]{2,1,0:T(4,128)S(1)} %pad_add_fusion.far_ref, s32[4]{0:T(128)S(1)} %get-tuple-element.28.meta_ref, bf16[2,4,12,128,128]{4,3,2,1,0:T(8,128)(2,1)S(1)} %copy-done, f32[4,128,1024]{2,1,0:T(8,128)S(1)} %shard_map.57.acc_ref, bf16[8,128,1024]{2,1,0:T(8,128)(2,1)S(1)} %bitcast.25, ...), custom_call_target="tpu_custom_call" | custom-call | flops 2147483648 | bytes 8388608 | tf_op jit(solution)/shard_map/pallas_call | solution.py:311
  82.5 0.6 collective-permute-start.22
  83.0 12.2 %collective-permute-done.17.refs_4_ = bf16[512,1024]{1,0:T(8,128)(2,1)S(1)} collective-permute-done((bf16[512,1024]{1,0:T(8,128)(2,1)S(1)}, bf16[512,1024]{1,0:T(8,128)(2,1)S(1)}, u32[]{:S(2)}, u32[]{:S(2)}) %collective-permute-start.17) | collective-permute-done | bytes 1048608 | tf_op jit(solution)/shard_map/ppermute | solution.py:355
  95.2 0.5 collective-permute-start.20
  95.8 2.4 %collective-permute-start.21 = (bf16[4,128,1024]{2,1,0:T(8,128)(2,1)S(1)}, bf16[4,128,1024]{2,1,0:T(8,128)(2,1)S(1)}, u32[]{:S(2)}, u32[]{:S(2)}) collective-permute-start(bf16[4,128,1024]{2,1,0:T(8,128)(2,1)S(1)} %shard_map.56.refs_0_.resid_ref), channel_id=1, source_target_pairs={{0,31},{1,2},{2,1},{3,4},{4,3},{5,6},{6,5},{7,8},{8,7},{9,10},{10,... | collective-permute-start | bytes 3145736 | tf_op jit(solution)/shard_map/ppermute | solution.py:352
  98.1 2.7 %collective-permute-start.23 = (bf16[4,128,1024]{2,1,0:T(8,128)(2,1)S(1)}, bf16[4,128,1024]{2,1,0:T(8,128)(2,1)S(1)}, u32[]{:S(2)}, u32[]{:S(2)}) collective-permute-start(bf16[4,128,1024]{2,1,0:T(8,128)(2,1)S(1)} %shard_map.58.refs_1_.resid_ref), channel_id=1, source_target_pairs={{0,31},{1,2},{2,1},{3,4},{4,3},{5,6},{6,5},{7,8},{8,7},{9,10},{10,... | collective-permute-start | bytes 3145736 | tf_op jit(solution)/shard_map/ppermute | solution.py:352
  100.8 11.2 %collective-permute-start.25 = (bf16[512,1024]{1,0:T(8,128)(2,1)S(1)}, bf16[512,1024]{1,0:T(8,128)(2,1)S(1)}, u32[]{:S(2)}, u32[]{:S(2)}) collective-permute-start(bf16[512,1024]{1,0:T(8,128)(2,1)S(1)} %copy-done.4), channel_id=1, source_target_pairs={{64,96},{65,97},{66,98},{67,99},{68,100},{69,101},{70,102},{71,103... | collective-permute-start | bytes 3145736 | tf_op jit(solution)/shard_map/ppermute | solution.py:355
  112.0 3.2 %shard_map.59.acc_ref = f32[4,128,1024]{2,1,0:T(8,128)S(1)} custom-call(s32[2,2,48]{2,1,0:T(2,128)S(1)} %pad_add_fusion.1.near_ref, bf16[2,4,12,128,128]{4,3,2,1,0:T(8,128)(2,1)S(1)} %copy-done, bf16[4,128,1024]{2,1,0:T(8,128)(2,1)S(1)} %shard_map.56.refs_0_.resid_ref, bf16[4,128,1024]{2,1,0:T(8,128)(2,1)S(1)} %collective-permute-done.16.refs_1_.refs_2_), custom_call_target="tpu_custom_call" | custom-call | flops 1610612736 | bytes 8388608 | tf_op jit(solution)/shard_map/pallas_call | solution.py:282
  115.2 3.4 %shard_map.61.acc_ref = f32[4,128,1024]{2,1,0:T(8,128)S(1)} custom-call(s32[2,2,48]{2,1,0:T(2,128)S(1)} %pad_add_fusion.1.near_ref, bf16[2,4,12,128,128]{4,3,2,1,0:T(8,128)(2,1)S(1)} %copy-done, bf16[4,128,1024]{2,1,0:T(8,128)(2,1)S(1)} %shard_map.56.refs_0_.resid_ref, bf16[4,128,1024]{2,1,0:T(8,128)(2,1)S(1)} %shard_map.58.refs_1_.resid_ref, ...), custom_call_target="tpu_custom_call" | custom-call | flops 1610612736 | bytes 8388608 | tf_op jit(solution)/shard_map/pallas_call | solution.py:282
  118.6 0.9 pick.4
  119.5 5.1 %collective-permute-done.23.refs_1_ = bf16[4,128,1024]{2,1,0:T(8,128)(2,1)S(1)} collective-permute-done((bf16[4,128,1024]{2,1,0:T(8,128)(2,1)S(1)}, bf16[4,128,1024]{2,1,0:T(8,128)(2,1)S(1)}, u32[]{:S(2)}, u32[]{:S(2)}) %collective-permute-start.23) | collective-permute-done | bytes 1048608 | tf_op jit(solution)/shard_map/ppermute | solution.py:352
  124.5 2.7 %shard_map.62.refs_1_.resid_ref.refs_3_ = bf16[4,128,1024]{2,1,0:T(8,128)(2,1)S(1)} custom-call(s32[2,3,48]{2,1,0:T(4,128)S(1)} %pad_add_fusion.far_ref, s32[4]{0:T(128)S(1)} %get-tuple-element.36.meta_ref, bf16[2,4,12,128,128]{4,3,2,1,0:T(8,128)(2,1)S(1)} %copy-done, f32[4,128,1024]{2,1,0:T(8,128)S(1)} %shard_map.61.acc_ref, ...), custom_call_target="tpu_custom_call" | custom-call | flops 2147483648 | bytes 8388608 | tf_op jit(solution)/shard_map/pallas_call | solution.py:311
  127.2 4.3 %collective-permute-done.25.refs_1_ = bf16[512,1024]{1,0:T(8,128)(2,1)S(1)} collective-permute-done((bf16[512,1024]{1,0:T(8,128)(2,1)S(1)}, bf16[512,1024]{1,0:T(8,128)(2,1)S(1)}, u32[]{:S(2)}, u32[]{:S(2)}) %collective-permute-start.25) | collective-permute-done | bytes 1048608 | tf_op jit(solution)/shard_map/ppermute | solution.py:355
  131.5 2.6 %shard_map.60.refs_0_.resid_ref.refs_2_ = bf16[4,128,1024]{2,1,0:T(8,128)(2,1)S(1)} custom-call(s32[2,3,48]{2,1,0:T(4,128)S(1)} %pad_add_fusion.far_ref, s32[4]{0:T(128)S(1)} %get-tuple-element.36.meta_ref, bf16[2,4,12,128,128]{4,3,2,1,0:T(8,128)(2,1)S(1)} %copy-done, f32[4,128,1024]{2,1,0:T(8,128)S(1)} %shard_map.59.acc_ref, ...), custom_call_target="tpu_custom_call" | custom-call | flops 2147483648 | bytes 8388608 | tf_op jit(solution)/shard_map/pallas_call | solution.py:311
  134.1 0.6 collective-permute-start.24
  134.7 2.4 %collective-permute-start.27 = (bf16[4,128,1024]{2,1,0:T(8,128)(2,1)S(1)}, bf16[4,128,1024]{2,1,0:T(8,128)(2,1)S(1)}, u32[]{:S(2)}, u32[]{:S(2)}) collective-permute-start(bf16[4,128,1024]{2,1,0:T(8,128)(2,1)S(1)} %shard_map.60.refs_0_.resid_ref.refs_2_), channel_id=1, source_target_pairs={{0,31},{1,2},{2,1},{3,4},{4,3},{5,6},{6,5},{7,8},{8,7},{9,10},{10,... | collective-permute-start | bytes 3145736 | tf_op jit(solution)/shard_map/ppermute | solution.py:352
  137.0 2.7 %collective-permute-start.30 = (bf16[4,128,1024]{2,1,0:T(8,128)(2,1)S(1)}, bf16[4,128,1024]{2,1,0:T(8,128)(2,1)S(1)}, u32[]{:S(2)}, u32[]{:S(2)}) collective-permute-start(bf16[4,128,1024]{2,1,0:T(8,128)(2,1)S(1)} %shard_map.62.refs_1_.resid_ref.refs_3_), channel_id=1, source_target_pairs={{0,31},{1,2},{2,1},{3,4},{4,3},{5,6},{6,5},{7,8},{8,7},{9,10},{10,... | collective-permute-start | bytes 3145736 | tf_op jit(solution)/shard_map/ppermute | solution.py:352
  139.7 0.9 pick.5
  140.6 3.2 %shard_map.63.acc_ref = f32[4,128,1024]{2,1,0:T(8,128)S(1)} custom-call(s32[2,2,48]{2,1,0:T(2,128)S(1)} %pad_add_fusion.1.near_ref, bf16[2,4,12,128,128]{4,3,2,1,0:T(8,128)(2,1)S(1)} %copy-done, bf16[4,128,1024]{2,1,0:T(8,128)(2,1)S(1)} %shard_map.60.refs_0_.resid_ref.refs_2_, bf16[4,128,1024]{2,1,0:T(8,128)(2,1)S(1)} %collective-permute-done.24.refs_1_.refs_2_), custom_call_target="tpu_custom_call" | custom-call | flops 1610612736 | bytes 8388608 | tf_op jit(solution)/shard_map/pallas_call | solution.py:282
  143.8 8.4 %collective-permute-done.27.refs_0_ = bf16[4,128,1024]{2,1,0:T(8,128)(2,1)S(1)} collective-permute-done((bf16[4,128,1024]{2,1,0:T(8,128)(2,1)S(1)}, bf16[4,128,1024]{2,1,0:T(8,128)(2,1)S(1)}, u32[]{:S(2)}, u32[]{:S(2)}) %collective-permute-start.27) | collective-permute-done | bytes 1048608 | tf_op jit(solution)/shard_map/ppermute | solution.py:352
  152.2 2.6 %shard_map.64.refs_0_.resid_ref = bf16[4,128,1024]{2,1,0:T(8,128)(2,1)S(1)} custom-call(s32[2,3,48]{2,1,0:T(4,128)S(1)} %pad_add_fusion.far_ref, s32[4]{0:T(128)S(1)} %pad_add_fusion.4.meta_ref, bf16[2,4,12,128,128]{4,3,2,1,0:T(8,128)(2,1)S(1)} %copy-done, f32[4,128,1024]{2,1,0:T(8,128)S(1)} %shard_map.63.acc_ref, ...), custom_call_target="tpu_custom_call" | custom-call | flops 2147483648 | bytes 8388608 | tf_op jit(solution)/shard_map/pallas_call | solution.py:311
  154.9 3.4 %shard_map.65.acc_ref = f32[4,128,1024]{2,1,0:T(8,128)S(1)} custom-call(s32[2,2,48]{2,1,0:T(2,128)S(1)} %pad_add_fusion.1.near_ref, bf16[2,4,12,128,128]{4,3,2,1,0:T(8,128)(2,1)S(1)} %copy-done, bf16[4,128,1024]{2,1,0:T(8,128)(2,1)S(1)} %shard_map.60.refs_0_.resid_ref.refs_2_, bf16[4,128,1024]{2,1,0:T(8,128)(2,1)S(1)} %shard_map.62.refs_1_.resid_ref.refs_3_, ...), custom_call_target="tpu_custom_call" | custom-call | flops 1610612736 | bytes 8388608 | tf_op jit(solution)/shard_map/pallas_call | solution.py:282
  158.2 5.2 %collective-permute-done.30.refs_1_ = bf16[4,128,1024]{2,1,0:T(8,128)(2,1)S(1)} collective-permute-done((bf16[4,128,1024]{2,1,0:T(8,128)(2,1)S(1)}, bf16[4,128,1024]{2,1,0:T(8,128)(2,1)S(1)}, u32[]{:S(2)}, u32[]{:S(2)}) %collective-permute-start.30) | collective-permute-done | bytes 1048608 | tf_op jit(solution)/shard_map/ppermute | solution.py:352
  163.4 2.7 %shard_map.66.refs_1_.resid_ref = bf16[4,128,1024]{2,1,0:T(8,128)(2,1)S(1)} custom-call(s32[2,3,48]{2,1,0:T(4,128)S(1)} %pad_add_fusion.far_ref, s32[4]{0:T(128)S(1)} %pad_add_fusion.4.meta_ref, bf16[2,4,12,128,128]{4,3,2,1,0:T(8,128)(2,1)S(1)} %copy-done, f32[4,128,1024]{2,1,0:T(8,128)S(1)} %shard_map.65.acc_ref, ...), custom_call_target="tpu_custom_call" | custom-call | flops 2147483648 | bytes 8388608 | tf_op jit(solution)/shard_map/pallas_call | solution.py:311
  166.2 2.4 %collective-permute-start.34 = (bf16[4,128,1024]{2,1,0:T(8,128)(2,1)S(1)}, bf16[4,128,1024]{2,1,0:T(8,128)(2,1)S(1)}, u32[]{:S(2)}, u32[]{:S(2)}) collective-permute-start(bf16[4,128,1024]{2,1,0:T(8,128)(2,1)S(1)} %shard_map.64.refs_0_.resid_ref), channel_id=1, source_target_pairs={{0,31},{1,2},{2,1},{3,4},{4,3},{5,6},{6,5},{7,8},{8,7},{9,10},{10,... | collective-permute-start | bytes 3145736 | tf_op jit(solution)/shard_map/ppermute | solution.py:352
  168.7 2.7 %collective-permute-start.35 = (bf16[4,128,1024]{2,1,0:T(8,128)(2,1)S(1)}, bf16[4,128,1024]{2,1,0:T(8,128)(2,1)S(1)}, u32[]{:S(2)}, u32[]{:S(2)}) collective-permute-start(bf16[4,128,1024]{2,1,0:T(8,128)(2,1)S(1)} %shard_map.66.refs_1_.resid_ref), channel_id=1, source_target_pairs={{0,31},{1,2},{2,1},{3,4},{4,3},{5,6},{6,5},{7,8},{8,7},{9,10},{10,... | collective-permute-start | bytes 3145736 | tf_op jit(solution)/shard_map/ppermute | solution.py:352
  171.4 1.3 collective-permute-start.28
  172.7 1.5 collective-permute-start.31
  174.2 3.2 %shard_map.68.acc_ref = f32[4,128,1024]{2,1,0:T(8,128)S(1)} custom-call(s32[2,2,48]{2,1,0:T(2,128)S(1)} %pad_add_fusion.1.near_ref, bf16[2,4,12,128,128]{4,3,2,1,0:T(8,128)(2,1)S(1)} %copy-done, bf16[4,128,1024]{2,1,0:T(8,128)(2,1)S(1)} %shard_map.64.refs_0_.resid_ref, bf16[4,128,1024]{2,1,0:T(8,128)(2,1)S(1)} %collective-permute-done.32.refs_2_.refs_1_), custom_call_target="tpu_custom_call" | custom-call | flops 1610612736 | bytes 8388608 | tf_op jit(solution)/shard_map/pallas_call | solution.py:282
  177.4 3.4 %shard_map.67.acc_ref = f32[4,128,1024]{2,1,0:T(8,128)S(1)} custom-call(s32[2,2,48]{2,1,0:T(2,128)S(1)} %pad_add_fusion.1.near_ref, bf16[2,4,12,128,128]{4,3,2,1,0:T(8,128)(2,1)S(1)} %copy-done, bf16[4,128,1024]{2,1,0:T(8,128)(2,1)S(1)} %shard_map.64.refs_0_.resid_ref, bf16[4,128,1024]{2,1,0:T(8,128)(2,1)S(1)} %shard_map.66.refs_1_.resid_ref, ...), custom_call_target="tpu_custom_call" | custom-call | flops 1610612736 | bytes 8388608 | tf_op jit(solution)/shard_map/pallas_call | solution.py:282
  180.8 3.0 %collective-permute-done.34.refs_0_ = bf16[4,128,1024]{2,1,0:T(8,128)(2,1)S(1)} collective-permute-done((bf16[4,128,1024]{2,1,0:T(8,128)(2,1)S(1)}, bf16[4,128,1024]{2,1,0:T(8,128)(2,1)S(1)}, u32[]{:S(2)}, u32[]{:S(2)}) %collective-permute-start.34) | collective-permute-done | bytes 1048608 | tf_op jit(solution)/shard_map/ppermute | solution.py:352
  183.9 2.6 %shard_map.69.refs_2_ = bf16[8,128,1024]{2,1,0:T(8,128)(2,1)} custom-call(s32[2,3,48]{2,1,0:T(4,128)S(1)} %pad_add_fusion.far_ref, s32[4]{0:T(128)S(1)} %pad_add_fusion.4.meta_ref, bf16[2,4,12,128,128]{4,3,2,1,0:T(8,128)(2,1)S(1)} %copy-done, f32[4,128,1024]{2,1,0:T(8,128)S(1)} %shard_map.68.acc_ref, bf16[4,128,1024]{2,1,0:T(8,128)(2,1)S(1)} %shard_map.64.refs_0_.resid_ref, ...), custom_call_target="tpu_custom_call" | custom-call | flops 2147483648 | bytes 8388608 | tf_op jit(solution)/shard_map/pallas_call | solution.py:311
  186.4 8.6 %collective-permute-done.35.refs_1_ = bf16[4,128,1024]{2,1,0:T(8,128)(2,1)S(1)} collective-permute-done((bf16[4,128,1024]{2,1,0:T(8,128)(2,1)S(1)}, bf16[4,128,1024]{2,1,0:T(8,128)(2,1)S(1)}, u32[]{:S(2)}, u32[]{:S(2)}) %collective-permute-start.35) | collective-permute-done | bytes 1048608 | tf_op jit(solution)/shard_map/ppermute | solution.py:352
  195.1 2.7 %shard_map.70.refs_6_ = bf16[8,128,1024]{2,1,0:T(8,128)(2,1)} custom-call(s32[2,3,48]{2,1,0:T(4,128)S(1)} %pad_add_fusion.far_ref, s32[4]{0:T(128)S(1)} %pad_add_fusion.4.meta_ref, bf16[2,4,12,128,128]{4,3,2,1,0:T(8,128)(2,1)S(1)} %copy-done, f32[4,128,1024]{2,1,0:T(8,128)S(1)} %shard_map.67.acc_ref, ...), custom_call_target="tpu_custom_call", output_to_operand_aliasing={{}: (9, {})} | custom-call | flops 2147483648 | bytes 8388608 | tf_op jit(solution)/shard_map/pallas_call | solution.py:311
  197.8 11.3 %collective-permute-done.28.refs_4_ = bf16[4,128,1024]{2,1,0:T(8,128)(2,1)S(1)} collective-permute-done((bf16[4,128,1024]{2,1,0:T(8,128)(2,1)S(1)}, bf16[4,128,1024]{2,1,0:T(8,128)(2,1)S(1)}, u32[]{:S(2)}, u32[]{:S(2)}) %collective-permute-start.28) | collective-permute-done | bytes 1048608 | tf_op jit(solution)/shard_map/ppermute | solution.py:355
  209.1 18.9 %collective-permute-done.31.refs_5_ = bf16[4,128,1024]{2,1,0:T(8,128)(2,1)S(1)} collective-permute-done((bf16[4,128,1024]{2,1,0:T(8,128)(2,1)S(1)}, bf16[4,128,1024]{2,1,0:T(8,128)(2,1)S(1)}, u32[]{:S(2)}, u32[]{:S(2)}) %collective-permute-start.31) | collective-permute-done | bytes 1048608 | tf_op jit(solution)/shard_map/ppermute | solution.py:355
  228.0 2.0 place.1
  (61 shorter events, 1.9 us)
Async XLA Ops:
  3.5 7.1 %copy-start.1 = (bf16[2,512,1024]{2,1,0:T(8,128)(2,1)S(1)}, bf16[2,512,1024]{2,1,0:T(8,128)(2,1)}, u32[]{:S(2)}) copy-start(bf16[2,512,1024]{2,1,0:T(8,128)(2,1)} %param.5) | copy-start | bytes 6291460
  3.5 32.9 %collective-permute-start.3 = (bf16[512,1024]{1,0:T(8,128)(2,1)}, bf16[512,1024]{1,0:T(8,128)(2,1)S(1)}, u32[]{:S(2)}, u32[]{:S(2)}) collective-permute-start(bf16[512,1024]{1,0:T(8,128)(2,1)} %get-tuple-element.30.refs_0_), channel_id=1, source_target_pairs={{0,32},{32,64},{64,96},{1,33},{33,65},{65,97},{2,34},{34,66},{66,9... | collective-permute-start | bytes 3145736 | tf_op jit(solution)/shard_map/ppermute | solution.py:355
  6.8 31.9 %collective-permute-start.1 = (bf16[512,1024]{1,0:T(8,128)(2,1)}, bf16[512,1024]{1,0:T(8,128)(2,1)}, u32[]{:S(2)}, u32[]{:S(2)}) collective-permute-start(bf16[512,1024]{1,0:T(8,128)(2,1)} %get-tuple-element.30.refs_0_), channel_id=1, source_target_pairs={{0,1},{1,0},{2,3},{3,2},{4,5},{5,4},{6,7},{7,6},{8,9},{9,8},{10,11... | collective-permute-start | bytes 3145736 | tf_op jit(solution)/shard_map/ppermute | solution.py:349
  9.9 1.3 collective-permute-start.7
  10.6 35.1 %collective-permute-start = (bf16[8,128,1024]{2,1,0:T(8,128)(2,1)S(1)}, bf16[8,128,1024]{2,1,0:T(8,128)(2,1)}, u32[]{:S(2)}, u32[]{:S(2)}) collective-permute-start(bf16[8,128,1024]{2,1,0:T(8,128)(2,1)S(1)} %bitcast.21), channel_id=1, source_target_pairs={{0,1},{1,0},{2,3},{3,2},{4,5},{5,4},{6,7},{7,6},{8,9},{9,8},{10,11... | collective-permute-start | bytes 6291464 | tf_op jit(solution)/shard_map/ppermute | solution.py:349
  11.2 9.0 %collective-permute-start.10 = (bf16[96,1024]{1,0:T(8,128)(2,1)S(1)}, bf16[96,1024]{1,0:T(8,128)(2,1)S(1)}, u32[]{:S(2)}, u32[]{:S(2)}) collective-permute-start(bf16[96,1024]{1,0:T(8,128)(2,1)S(1)} %collective-permute-done.7.refs_0_), channel_id=1, source_target_pairs={{0,16},{1,17},{2,18},{3,19},{4,20},{5,21},{6,22},{7,23},{8,24},{9,... | collective-permute-start | bytes 589832 | tf_op jit(solution)/shard_map/ppermute | solution.py:358
  15.1 25.2 %collective-permute-start.11 = (bf16[640,1024]{1,0:T(8,128)(2,1)}, bf16[640,1024]{1,0:T(8,128)(2,1)}, u32[]{:S(2)}, u32[]{:S(2)}) collective-permute-start(bf16[640,1024]{1,0:T(8,128)(2,1)} %get-tuple-element.33), channel_id=1, source_target_pairs={{0,96},{1,97},{2,98},{3,99},{4,100},{5,101},{6,102},{7,103},{8,104... | collective-permute-start | bytes 3932168 | tf_op jit(solution)/shard_map/ppermute | solution.py:355
  20.2 7.0 %collective-permute-start.9 = (bf16[96,1024]{1,0:T(8,128)(2,1)S(1)}, bf16[96,1024]{1,0:T(8,128)(2,1)}, u32[]{:S(2)}, u32[]{:S(2)}) collective-permute-start(bf16[96,1024]{1,0:T(8,128)(2,1)S(1)} %collective-permute-done.7.refs_0_), channel_id=1, source_target_pairs={{0,24},{1,25},{2,26},{3,27},{4,28},{5,29},{6,30},{7,31},{8,0},{9,1... | collective-permute-start | bytes 589832 | tf_op jit(solution)/shard_map/ppermute | solution.py:358
  27.2 7.5 %collective-permute-start.8 = (bf16[96,1024]{1,0:T(8,128)(2,1)S(1)}, bf16[96,1024]{1,0:T(8,128)(2,1)}, u32[]{:S(2)}, u32[]{:S(2)}) collective-permute-start(bf16[96,1024]{1,0:T(8,128)(2,1)S(1)} %collective-permute-done.7.refs_0_), channel_id=1, source_target_pairs={{0,8},{1,9},{2,10},{3,11},{4,12},{5,13},{6,14},{7,15},{8,16},{9,17... | collective-permute-start | bytes 589832 | tf_op jit(solution)/shard_map/ppermute | solution.py:358
  34.7 5.7 %collective-permute-start.4 = (bf16[512,1024]{1,0:T(8,128)(2,1)}, bf16[512,1024]{1,0:T(8,128)(2,1)}, u32[]{:S(2)}, u32[]{:S(2)}) collective-permute-start(bf16[512,1024]{1,0:T(8,128)(2,1)} %get-tuple-element.39.refs_1_), channel_id=1, source_target_pairs={{0,32},{1,33},{2,34},{3,35},{4,36},{5,37},{6,38},{7,39},{8,40},{9,... | collective-permute-start | bytes 3145736 | tf_op jit(solution)/shard_map/ppermute | solution.py:355
  36.5 8.6 %collective-permute-start.2 = (bf16[512,1024]{1,0:T(8,128)(2,1)}, bf16[512,1024]{1,0:T(8,128)(2,1)}, u32[]{:S(2)}, u32[]{:S(2)}) collective-permute-start(bf16[512,1024]{1,0:T(8,128)(2,1)} %get-tuple-element.39.refs_1_), channel_id=1, source_target_pairs={{0,1},{1,0},{2,3},{3,2},{4,5},{5,4},{6,7},{7,6},{8,9},{9,8},{10,11... | collective-permute-start | bytes 3145736 | tf_op jit(solution)/shard_map/ppermute | solution.py:349
  38.7 6.4 %collective-permute-start.12 = (bf16[384,1024]{1,0:T(8,128)(2,1)}, bf16[384,1024]{1,0:T(8,128)(2,1)}, u32[]{:S(2)}, u32[]{:S(2)}) collective-permute-start(bf16[384,1024]{1,0:T(8,128)(2,1)} %join.1.refs_8_), channel_id=1, source_target_pairs={{0,1},{1,0},{2,3},{3,2},{4,5},{5,4},{6,7},{7,6},{8,9},{9,8},{10,11... | collective-permute-start | bytes 2359304 | tf_op jit(solution)/shard_map/ppermute | solution.py:349
  40.1 6.5 %copy-start.5 = (s32[2]{0:T(128)S(1)}, s32[2]{0:T(128)}, u32[]{:S(2)}) copy-start(s32[2]{0:T(128)} %get-tuple-element.49) | copy-start | bytes 28
  40.1 6.6 %copy-start = (bf16[2,4,12,128,128]{4,3,2,1,0:T(8,128)(2,1)S(1)}, bf16[2,4,12,128,128]{4,3,2,1,0:T(8,128)(2,1)}, u32[]{:S(2)}) copy-start(bf16[2,4,12,128,128]{4,3,2,1,0:T(8,128)(2,1)} %tiles_ref.31) | copy-start | bytes 9437188
  40.3 34.9 %collective-permute-start.13 = (bf16[640,1024]{1,0:T(8,128)(2,1)}, bf16[640,1024]{1,0:T(8,128)(2,1)S(1)}, u32[]{:S(2)}, u32[]{:S(2)}) collective-permute-start(bf16[640,1024]{1,0:T(8,128)(2,1)} %collective-permute-done.11.refs_9_), channel_id=1, source_target_pairs={{0,1},{1,0},{2,3},{3,2},{4,5},{5,4},{6,7},{7,6},{8,9},{9,8},{10,11... | collective-permute-start | bytes 3932168 | tf_op jit(solution)/shard_map/ppermute | solution.py:349
  40.4 36.7 %collective-permute-start.14 = (bf16[4,128,1024]{2,1,0:T(8,128)(2,1)S(1)}, bf16[4,128,1024]{2,1,0:T(8,128)(2,1)S(1)}, u32[]{:S(2)}, u32[]{:S(2)}) collective-permute-start(bf16[4,128,1024]{2,1,0:T(8,128)(2,1)S(1)} %bitcast.35), channel_id=1, source_target_pairs={{0,31},{1,2},{2,1},{3,4},{4,3},{5,6},{6,5},{7,8},{8,7},{9,10},{10,... | collective-permute-start | bytes 3145736 | tf_op jit(solution)/shard_map/ppermute | solution.py:352
  45.1 10.8 %collective-permute-start.5 = (bf16[512,1024]{1,0:T(8,128)(2,1)S(1)}, bf16[512,1024]{1,0:T(8,128)(2,1)S(1)}, u32[]{:S(2)}, u32[]{:S(2)}) collective-permute-start(bf16[512,1024]{1,0:T(8,128)(2,1)S(1)} %collective-permute-done.3.refs_4_.refs_0_), channel_id=1, source_target_pairs={{0,1},{1,0},{2,3},{3,2},{4,5},{5,4},{6,7},{7,6},{8,9},{9,8},{10,11... | collective-permute-start | bytes 3145736 | tf_op jit(solution)/shard_map/ppermute | solution.py:349
  45.1 29.3 %collective-permute-start.6 = (bf16[512,1024]{1,0:T(8,128)(2,1)}, bf16[512,1024]{1,0:T(8,128)(2,1)S(1)}, u32[]{:S(2)}, u32[]{:S(2)}) collective-permute-start(bf16[512,1024]{1,0:T(8,128)(2,1)} %collective-permute-done.4.refs_5_), channel_id=1, source_target_pairs={{0,1},{1,0},{2,3},{3,2},{4,5},{5,4},{6,7},{7,6},{8,9},{9,8},{10,11... | collective-permute-start | bytes 3145736 | tf_op jit(solution)/shard_map/ppermute | solution.py:349
  45.7 34.0 %collective-permute-start.15 = (bf16[4,128,1024]{2,1,0:T(8,128)(2,1)S(1)}, bf16[4,128,1024]{2,1,0:T(8,128)(2,1)S(1)}, u32[]{:S(2)}, u32[]{:S(2)}) collective-permute-start(bf16[4,128,1024]{2,1,0:T(8,128)(2,1)S(1)} %bitcast.34), channel_id=1, source_target_pairs={{0,31},{1,2},{2,1},{3,4},{4,3},{5,6},{6,5},{7,8},{8,7},{9,10},{10,... | collective-permute-start | bytes 3145736 | tf_op jit(solution)/shard_map/ppermute | solution.py:352
  51.5 23.0 %copy-start.4 = (bf16[512,1024]{1,0:T(8,128)(2,1)S(1)}, bf16[512,1024]{1,0:T(8,128)(2,1)}, u32[]{:S(2)}) copy-start(bf16[512,1024]{1,0:T(8,128)(2,1)} %get-tuple-element.39.refs_1_) | copy-start | bytes 3145732
  55.8 39.4 %collective-permute-start.17 = (bf16[512,1024]{1,0:T(8,128)(2,1)S(1)}, bf16[512,1024]{1,0:T(8,128)(2,1)S(1)}, u32[]{:S(2)}, u32[]{:S(2)}) collective-permute-start(bf16[512,1024]{1,0:T(8,128)(2,1)S(1)} %collective-permute-done.3.refs_4_.refs_0_), channel_id=1, source_target_pairs={{64,96},{65,97},{66,98},{67,99},{68,100},{69,101},{70,102},{71,103... | collective-permute-start | bytes 3145736 | tf_op jit(solution)/shard_map/ppermute | solution.py:355
  74.4 20.8 %collective-permute-start.18 = (bf16[512,1024]{1,0:T(8,128)(2,1)S(1)}, bf16[512,1024]{1,0:T(8,128)(2,1)S(1)}, u32[]{:S(2)}, u32[]{:S(2)}) collective-permute-start(bf16[512,1024]{1,0:T(8,128)(2,1)S(1)} %copy-done.4), channel_id=1, source_target_pairs={{32,96},{33,97},{34,98},{35,99},{36,100},{37,101},{38,102},{39,103... | collective-permute-start | bytes 3145736 | tf_op jit(solution)/shard_map/ppermute | solution.py:355
  79.7 18.5 %collective-permute-start.16 = (bf16[4,128,1024]{2,1,0:T(8,128)(2,1)S(1)}, bf16[4,128,1024]{2,1,0:T(8,128)(2,1)S(1)}, u32[]{:S(2)}, u32[]{:S(2)}) collective-permute-start(bf16[4,128,1024]{2,1,0:T(8,128)(2,1)S(1)} %shard_map.56.refs_0_.resid_ref), channel_id=1, source_target_pairs={{0,1},{1,0},{2,3},{3,2},{4,5},{5,4},{6,7},{7,6},{8,9},{9,8},{10,11... | collective-permute-start | bytes 3145736 | tf_op jit(solution)/shard_map/ppermute | solution.py:349
  82.5 18.3 %collective-permute-start.22 = (bf16[4,128,1024]{2,1,0:T(8,128)(2,1)S(1)}, bf16[4,128,1024]{2,1,0:T(8,128)(2,1)S(1)}, u32[]{:S(2)}, u32[]{:S(2)}) collective-permute-start(bf16[4,128,1024]{2,1,0:T(8,128)(2,1)S(1)} %shard_map.58.refs_1_.resid_ref), channel_id=1, source_target_pairs={{0,1},{1,0},{2,3},{3,2},{4,5},{5,4},{6,7},{7,6},{8,9},{9,8},{10,11... | collective-permute-start | bytes 3145736 | tf_op jit(solution)/shard_map/ppermute | solution.py:349
  95.2 23.3 %collective-permute-start.19 = (bf16[512,1024]{1,0:T(8,128)(2,1)S(1)}, bf16[512,1024]{1,0:T(8,128)(2,1)S(1)}, u32[]{:S(2)}, u32[]{:S(2)}) collective-permute-start(bf16[512,1024]{1,0:T(8,128)(2,1)S(1)} %collective-permute-done.17.refs_4_), channel_id=1, source_target_pairs={{0,1},{1,0},{2,3},{3,2},{4,5},{5,4},{6,7},{7,6},{8,9},{9,8},{10,11... | collective-permute-start | bytes 3145736 | tf_op jit(solution)/shard_map/ppermute | solution.py:349
  95.2 23.3 %collective-permute-start.20 = (bf16[512,1024]{1,0:T(8,128)(2,1)S(1)}, bf16[512,1024]{1,0:T(8,128)(2,1)S(1)}, u32[]{:S(2)}, u32[]{:S(2)}) collective-permute-start(bf16[512,1024]{1,0:T(8,128)(2,1)S(1)} %collective-permute-done.18.refs_5_), channel_id=1, source_target_pairs={{0,1},{1,0},{2,3},{3,2},{4,5},{5,4},{6,7},{7,6},{8,9},{9,8},{10,11... | collective-permute-start | bytes 3145736 | tf_op jit(solution)/shard_map/ppermute | solution.py:349
  95.8 23.7 %collective-permute-start.21 = (bf16[4,128,1024]{2,1,0:T(8,128)(2,1)S(1)}, bf16[4,128,1024]{2,1,0:T(8,128)(2,1)S(1)}, u32[]{:S(2)}, u32[]{:S(2)}) collective-permute-start(bf16[4,128,1024]{2,1,0:T(8,128)(2,1)S(1)} %shard_map.56.refs_0_.resid_ref), channel_id=1, source_target_pairs={{0,31},{1,2},{2,1},{3,4},{4,3},{5,6},{6,5},{7,8},{8,7},{9,10},{10,... | collective-permute-start | bytes 3145736 | tf_op jit(solution)/shard_map/ppermute | solution.py:352
  98.1 26.4 %collective-permute-start.23 = (bf16[4,128,1024]{2,1,0:T(8,128)(2,1)S(1)}, bf16[4,128,1024]{2,1,0:T(8,128)(2,1)S(1)}, u32[]{:S(2)}, u32[]{:S(2)}) collective-permute-start(bf16[4,128,1024]{2,1,0:T(8,128)(2,1)S(1)} %shard_map.58.refs_1_.resid_ref), channel_id=1, source_target_pairs={{0,31},{1,2},{2,1},{3,4},{4,3},{5,6},{6,5},{7,8},{8,7},{9,10},{10,... | collective-permute-start | bytes 3145736 | tf_op jit(solution)/shard_map/ppermute | solution.py:352
  100.8 30.7 %collective-permute-start.25 = (bf16[512,1024]{1,0:T(8,128)(2,1)S(1)}, bf16[512,1024]{1,0:T(8,128)(2,1)S(1)}, u32[]{:S(2)}, u32[]{:S(2)}) collective-permute-start(bf16[512,1024]{1,0:T(8,128)(2,1)S(1)} %copy-done.4), channel_id=1, source_target_pairs={{64,96},{65,97},{66,98},{67,99},{68,100},{69,101},{70,102},{71,103... | collective-permute-start | bytes 3145736 | tf_op jit(solution)/shard_map/ppermute | solution.py:355
  131.5 8.2 %collective-permute-start.26 = (bf16[512,1024]{1,0:T(8,128)(2,1)S(1)}, bf16[512,1024]{1,0:T(8,128)(2,1)S(1)}, u32[]{:S(2)}, u32[]{:S(2)}) collective-permute-start(bf16[512,1024]{1,0:T(8,128)(2,1)S(1)} %collective-permute-done.25.refs_1_), channel_id=1, source_target_pairs={{0,1},{1,0},{2,3},{3,2},{4,5},{5,4},{6,7},{7,6},{8,9},{9,8},{10,11... | collective-permute-start | bytes 3145736 | tf_op jit(solution)/shard_map/ppermute | solution.py:349
  134.1 6.5 %collective-permute-start.24 = (bf16[4,128,1024]{2,1,0:T(8,128)(2,1)S(1)}, bf16[4,128,1024]{2,1,0:T(8,128)(2,1)S(1)}, u32[]{:S(2)}, u32[]{:S(2)}) collective-permute-start(bf16[4,128,1024]{2,1,0:T(8,128)(2,1)S(1)} %shard_map.60.refs_0_.resid_ref.refs_2_), channel_id=1, source_target_pairs={{0,1},{1,0},{2,3},{3,2},{4,5},{5,4},{6,7},{7,6},{8,9},{9,8},{10,11... | collective-permute-start | bytes 3145736 | tf_op jit(solution)/shard_map/ppermute | solution.py:349
  134.7 17.5 %collective-permute-start.27 = (bf16[4,128,1024]{2,1,0:T(8,128)(2,1)S(1)}, bf16[4,128,1024]{2,1,0:T(8,128)(2,1)S(1)}, u32[]{:S(2)}, u32[]{:S(2)}) collective-permute-start(bf16[4,128,1024]{2,1,0:T(8,128)(2,1)S(1)} %shard_map.60.refs_0_.resid_ref.refs_2_), channel_id=1, source_target_pairs={{0,31},{1,2},{2,1},{3,4},{4,3},{5,6},{6,5},{7,8},{8,7},{9,10},{10,... | collective-permute-start | bytes 3145736 | tf_op jit(solution)/shard_map/ppermute | solution.py:352
  137.0 17.8 %collective-permute-start.29 = (bf16[4,128,1024]{2,1,0:T(8,128)(2,1)S(1)}, bf16[4,128,1024]{2,1,0:T(8,128)(2,1)S(1)}, u32[]{:S(2)}, u32[]{:S(2)}) collective-permute-start(bf16[4,128,1024]{2,1,0:T(8,128)(2,1)S(1)} %shard_map.62.refs_1_.resid_ref.refs_3_), channel_id=1, source_target_pairs={{0,1},{1,0},{2,3},{3,2},{4,5},{5,4},{6,7},{7,6},{8,9},{9,8},{10,11... | collective-permute-start | bytes 3145736 | tf_op jit(solution)/shard_map/ppermute | solution.py:349
  137.0 26.4 %collective-permute-start.30 = (bf16[4,128,1024]{2,1,0:T(8,128)(2,1)S(1)}, bf16[4,128,1024]{2,1,0:T(8,128)(2,1)S(1)}, u32[]{:S(2)}, u32[]{:S(2)}) collective-permute-start(bf16[4,128,1024]{2,1,0:T(8,128)(2,1)S(1)} %shard_map.62.refs_1_.resid_ref.refs_3_), channel_id=1, source_target_pairs={{0,31},{1,2},{2,1},{3,4},{4,3},{5,6},{6,5},{7,8},{8,7},{9,10},{10,... | collective-permute-start | bytes 3145736 | tf_op jit(solution)/shard_map/ppermute | solution.py:352
  154.8 17.9 %collective-permute-start.32 = (bf16[4,128,1024]{2,1,0:T(8,128)(2,1)S(1)}, bf16[4,128,1024]{2,1,0:T(8,128)(2,1)S(1)}, u32[]{:S(2)}, u32[]{:S(2)}) collective-permute-start(bf16[4,128,1024]{2,1,0:T(8,128)(2,1)S(1)} %shard_map.64.refs_0_.resid_ref), channel_id=1, source_target_pairs={{0,1},{1,0},{2,3},{3,2},{4,5},{5,4},{6,7},{7,6},{8,9},{9,8},{10,11... | collective-permute-start | bytes 3145736 | tf_op jit(solution)/shard_map/ppermute | solution.py:349
  166.1 11.3 %collective-permute-start.33 = (bf16[4,128,1024]{2,1,0:T(8,128)(2,1)S(1)}, bf16[4,128,1024]{2,1,0:T(8,128)(2,1)S(1)}, u32[]{:S(2)}, u32[]{:S(2)}) collective-permute-start(bf16[4,128,1024]{2,1,0:T(8,128)(2,1)S(1)} %shard_map.66.refs_1_.resid_ref), channel_id=1, source_target_pairs={{0,1},{1,0},{2,3},{3,2},{4,5},{5,4},{6,7},{7,6},{8,9},{9,8},{10,11... | collective-permute-start | bytes 3145736 | tf_op jit(solution)/shard_map/ppermute | solution.py:349
  166.2 17.6 %collective-permute-start.34 = (bf16[4,128,1024]{2,1,0:T(8,128)(2,1)S(1)}, bf16[4,128,1024]{2,1,0:T(8,128)(2,1)S(1)}, u32[]{:S(2)}, u32[]{:S(2)}) collective-permute-start(bf16[4,128,1024]{2,1,0:T(8,128)(2,1)S(1)} %shard_map.64.refs_0_.resid_ref), channel_id=1, source_target_pairs={{0,31},{1,2},{2,1},{3,4},{4,3},{5,6},{6,5},{7,8},{8,7},{9,10},{10,... | collective-permute-start | bytes 3145736 | tf_op jit(solution)/shard_map/ppermute | solution.py:352
  168.7 26.4 %collective-permute-start.35 = (bf16[4,128,1024]{2,1,0:T(8,128)(2,1)S(1)}, bf16[4,128,1024]{2,1,0:T(8,128)(2,1)S(1)}, u32[]{:S(2)}, u32[]{:S(2)}) collective-permute-start(bf16[4,128,1024]{2,1,0:T(8,128)(2,1)S(1)} %shard_map.66.refs_1_.resid_ref), channel_id=1, source_target_pairs={{0,31},{1,2},{2,1},{3,4},{4,3},{5,6},{6,5},{7,8},{8,7},{9,10},{10,... | collective-permute-start | bytes 3145736 | tf_op jit(solution)/shard_map/ppermute | solution.py:352
  171.4 37.8 %collective-permute-start.28 = (bf16[4,128,1024]{2,1,0:T(8,128)(2,1)S(1)}, bf16[4,128,1024]{2,1,0:T(8,128)(2,1)S(1)}, u32[]{:S(2)}, u32[]{:S(2)}) collective-permute-start(bf16[4,128,1024]{2,1,0:T(8,128)(2,1)S(1)} %shard_map.64.refs_0_.resid_ref), channel_id=1, source_target_pairs={{96,64},{97,65},{98,66},{99,67},{100,68},{101,69},{102,70},{103,71... | collective-permute-start | bytes 3145736 | tf_op jit(solution)/shard_map/ppermute | solution.py:355
  172.7 55.3 %collective-permute-start.31 = (bf16[4,128,1024]{2,1,0:T(8,128)(2,1)S(1)}, bf16[4,128,1024]{2,1,0:T(8,128)(2,1)S(1)}, u32[]{:S(2)}, u32[]{:S(2)}) collective-permute-start(bf16[4,128,1024]{2,1,0:T(8,128)(2,1)S(1)} %shard_map.66.refs_1_.resid_ref), channel_id=1, source_target_pairs={{96,64},{97,65},{98,66},{99,67},{100,68},{101,69},{102,70},{103,71... | collective-permute-start | bytes 3145736 | tf_op jit(solution)/shard_map/ppermute | solution.py:355
  177.4 6.5 %copy-start.2 = (bf16[1,1024,1024]{2,1,0:T(8,128)(2,1)S(1)}, bf16[1,1024,1024]{2,1,0:T(8,128)(2,1)}, u32[]{:S(2)}) copy-start(bf16[1,1024,1024]{2,1,0:T(8,128)(2,1)} %param.7) | copy-start | bytes 6291460
  177.4 6.5 %copy-start.3 = (bf16[1,1024,1024]{2,1,0:T(8,128)(2,1)S(1)}, bf16[1,1024,1024]{2,1,0:T(8,128)(2,1)}, u32[]{:S(2)}) copy-start(bf16[1,1024,1024]{2,1,0:T(8,128)(2,1)} %param.8) | copy-start | bytes 6291460

commit v2 on v1

--- a/solution.py
+++ b/solution.py
@@ -90,12 +90,13 @@
 
     def shards(a, b):
         z = meta_ref[0]
-        quarter = a.shape[0] // 4
+        quarter = a.shape[0] // 3
         part = []
-        for k, away in enumerate((0, 3, 1, 2)):
+        for src, k, away in ((a, 0, 0), (a, 1, 3), (a, 2, 1), (b, 0, 2)):
             start = pl.multiple_of((z + away) % 4 * quarter, quarter)
-            part.append((a.at[pl.ds(k * quarter, quarter)], pl.ds(start, quarter)))
-        return part + [(b, pl.ds(4 * quarter, feat - 4 * quarter))]
+            part.append((src.at[pl.ds(k * quarter, quarter)], pl.ds(start, quarter)))
+        size = feat - 4 * quarter
+        return part + [(b.at[pl.ds(quarter, size)], pl.ds(4 * quarter, size))]
 
     choices = []
     for at in range(0, n_got, 4):
@@ -125,17 +126,20 @@
     )
 
 
-CUT = 384
+CUT = 768
 
 
 def mine_kernel(pieces, meta_ref, first_ref, second_ref, *refs):
     *outs, sem = refs
 
     def fetch(src):
-        for k, ((start, per_z), dst) in enumerate(zip(pieces, outs)):
-            size = dst.shape[0]
-            rows = pl.ds(pl.multiple_of(meta_ref[0] * size, size) if per_z else start, size)
-            pltpu.make_async_copy(src.at[rows], dst, sem.at[k]).start()
+        for k, (ranges, dst) in enumerate(zip(pieces, outs)):
+            at = 0
+            for start, away, size in ranges:
+                if away is not None:
+                    start = pl.multiple_of((meta_ref[0] + away) % 4 * size, size)
+                pltpu.make_async_copy(src.at[pl.ds(start, size)], dst.at[pl.ds(at, size)], sem.at[k]).start()
+                at += size
 
     pl.when(meta_ref[1] == 0)(functools.partial(fetch, first_ref))
     pl.when(meta_ref[1] != 0)(functools.partial(fetch, second_ref))
@@ -145,10 +149,10 @@
 
 def mine(meta, w_first, w_second, pieces):
     feat = w_first.shape[0]
-    fixed = tuple((start or 0, start is None) for start, _ in pieces)
+    shapes = [jax.ShapeDtypeStruct((sum(r[2] for r in one), feat), jnp.bfloat16) for one in pieces]
     return pl.pallas_call(
-        functools.partial(mine_kernel, fixed),
-        out_shape=[jax.ShapeDtypeStruct((size, feat), jnp.bfloat16) for _, size in pieces],
+        functools.partial(mine_kernel, pieces),
+        out_shape=shapes,
         in_specs=[SMEM, HBM, HBM],
         out_specs=[VMEM] * len(pieces),
         scratch_shapes=[pltpu.SemaphoreType.DMA((len(pieces),))],
@@ -381,15 +385,15 @@
             over_out.append(cross(out[s]))
         return out, chip_out, over_out, [sums(s, out, chip_out) for s in range(spans)]
 
-    shard, rest = mine(metas[3], w_first, w_second, [(None, CUT // 4), (CUT, feat - CUT)])
+    shard, rest = mine(metas[3], w_first, w_second, [[(0, 0, CUT // 4)], [(0, 2, CUT // 4), (CUT, None, feat - CUT)]])
     shard = hop(shard, [(0, hub)])
     zero_b = hop(rest, [(0, hub)])
-    mine_a, mine_b = mine(metas[3], w_first, w_second, [(0, feat // 2), (feat // 2, feat // 2)])
+    mine_a, mine_b = mine(metas[3], w_first, w_second, [[(0, None, feat // 2)], [(feat // 2, None, feat // 2)]])
     start = features.reshape(spans * blk_rows, tile_len, feat)
     chip0 = swap(start)
     over0 = [cross(start[s * blk_rows : (s + 1) * blk_rows]) for s in range(spans)]
     next_a = hop(mine_a, [(0, 1), (1, 2), (2, hub)])
-    zero_a = join(shard, along_z(shard, 1), along_z(shard, -1), along_z(shard, 2))
+    zero_a = join(shard, along_z(shard, 1), along_z(shard, -1))
     next_b = hop(mine_b, [(0, 1)])
     ids = lax.dynamic_slice_in_dim(tile_block, me * blk_rows, blk_rows, 1)
     near, far = entry_tables(ids, me, parts, parts * blk_rows)

time: 231 us -> 244 us (1.056)
  starting transfers between devices: 72.8 us -> 82.2 us
  waiting for transfers between devices: 88.1 us -> 91.3 us
    ppermute x9, starting transfers between devices: 40.6 us -> 53.1 us  [hop(): return lax.ppermute(value, 'section', pairs)]
    ppermute x9, waiting for transfers between devices: 46.7 us -> 56.4 us  [hop(): return lax.ppermute(value, 'section', pairs)]
    ppermute x8, waiting for transfers between devices: 30.4 us -> 25.3 us  [cross(): return lax.ppermute(value, 'dom', cross_pairs)]
    ppermute x3 -> x2, starting transfers between devices: 7.92 us -> 4.11 us  [along_z(): lax.ppermute(value, 'dom', [(p, (p + by * row_parts) % parts) for p in ra...]
    ppermute x3 -> x2, waiting for transfers between devices: 11 us -> 9.54 us  [along_z(): lax.ppermute(value, 'dom', [(p, (p + by * row_parts) % parts) for p in ra...]
  transfers between devices with their start and end apart: 36 -> 35, of which waited for: 12 -> 11; matrix products, arithmetic and copies ran while one was open for 2% -> 2% of each run, Pallas kernels for 25% -> 24%
where the time goes in v2:
time: 244 us; the launch traced here: 243 us
  waiting for transfers between devices  91.3 us (37%)
  starting transfers between devices  82.2 us (34%)
  Pallas kernels  63 us (26%)
  other arithmetic  3.23 us (1%)
  local copies, waits for them, and re-layouts  2.48 us (1%)
    ppermute x9, waiting for transfers between devices, hop(): return lax.ppermute(value, 'section', pairs)  56.4 us
    ppermute x9, starting transfers between devices, hop(): return lax.ppermute(value, 'section', pairs)  53.1 us
    pallas_call x8, Pallas kernels, early(): pl.pallas_call(functools.partial(early_kernel, span, n_src), out_shape=ja...  28.8 us
    ppermute x8, waiting for transfers between devices, cross(): return lax.ppermute(value, 'dom', cross_pairs)  25.3 us
    ppermute x8, starting transfers between devices, cross(): return lax.ppermute(value, 'dom', cross_pairs)  22 us
    pallas_call x8, Pallas kernels, late(): pl.pallas_call(functools.partial(late_kernel, span, len(crosses), final),...  21 us
    ppermute x2, waiting for transfers between devices, along_z(): lax.ppermute(value, 'dom', [(p, (p + by * row_parts) % parts) for p in ra...  9.54 us
    pallas_call x2, Pallas kernels, mine(): pl.pallas_call(functools.partial(mine_kernel, pieces), out_shape=shapes,...  6.25 us
  transfers between devices with their start and end apart: 35, of which 11 were waited for; matrix products, arithmetic and copies ran while one was open for 2% of the time, Pallas kernels for 24%

profile of v2, /device:TPU:4, one launch (start us, length us, event | category | flops | bytes accessed | tf_op | source)
XLA Modules:
  0.0 243.0 jit_solution(6887298884104987164)
XLA Ops:
  0.1 2.8 %mine.3 = (bf16[192,1024]{1,0:T(8,128)(2,1)S(1)}, bf16[448,1024]{1,0:T(8,128)(2,1)}) custom-call(s32[4]{0:T(128)S(1)} %pad_add_fusion.4.meta_ref, bf16[1024,1024]{1,0:T(8,128)(2,1)} %bitcast.26, bf16[1024,1024]{1,0:T(8,128)(2,1)} %bitcast.30), custom_call_target="tpu_custom_call" | custom-call | bytes 4194304 | tf_op jit(solution)/shard_map/mine/pallas_call | solution.py:153
  2.9 1.7 collective-permute-start.10
  4.7 3.4 %mine.2 = (bf16[512,1024]{1,0:T(8,128)(2,1)}, bf16[512,1024]{1,0:T(8,128)(2,1)}) custom-call(s32[4]{0:T(128)S(1)} %pad_add_fusion.4.meta_ref, bf16[1024,1024]{1,0:T(8,128)(2,1)} %bitcast.27, bf16[1024,1024]{1,0:T(8,128)(2,1)} %bitcast.31), custom_call_target="tpu_custom_call" | custom-call | bytes 4194304 | tf_op jit(solution)/shard_map/mine/pallas_call | solution.py:153
  8.1 2.8 %collective-permute-start.3 = (bf16[512,1024]{1,0:T(8,128)(2,1)}, bf16[512,1024]{1,0:T(8,128)(2,1)S(1)}, u32[]{:S(2)}, u32[]{:S(2)}) collective-permute-start(bf16[512,1024]{1,0:T(8,128)(2,1)} %get-tuple-element.30.refs_0_), channel_id=1, source_target_pairs={{0,32},{32,64},{64,96},{1,33},{33,65},{65,97},{2,34},{34,66},{66,9... | collective-permute-start | bytes 3145736 | tf_op jit(solution)/shard_map/ppermute | solution.py:359
  10.9 0.7 collective-permute-start.7
  11.7 4.1 %collective-permute-start.9 = (bf16[192,1024]{1,0:T(8,128)(2,1)S(1)}, bf16[192,1024]{1,0:T(8,128)(2,1)}, u32[]{:S(2)}, u32[]{:S(2)}) collective-permute-start(bf16[192,1024]{1,0:T(8,128)(2,1)S(1)} %collective-permute-done.7.refs_0_), channel_id=1, source_target_pairs={{0,24},{1,25},{2,26},{3,27},{4,28},{5,29},{6,30},{7,31},{8,0},{9,1... | collective-permute-start | bytes 1179656 | tf_op jit(solution)/shard_map/ppermute | solution.py:362
  15.8 1.5 fusion.3
  17.3 0.7 copy.16
  18.0 0.8 reshape.313
  18.7 6.0 %collective-permute-done.9.refs_2_ = bf16[192,1024]{1,0:T(8,128)(2,1)} collective-permute-done((bf16[192,1024]{1,0:T(8,128)(2,1)S(1)}, bf16[192,1024]{1,0:T(8,128)(2,1)}, u32[]{:S(2)}, u32[]{:S(2)}) %collective-permute-start.9) | collective-permute-done | bytes 393248 | tf_op jit(solution)/shard_map/ppermute | solution.py:362
  24.8 3.5 %collective-permute-done.8.refs_1_ = bf16[192,1024]{1,0:T(8,128)(2,1)} collective-permute-done((bf16[192,1024]{1,0:T(8,128)(2,1)S(1)}, bf16[192,1024]{1,0:T(8,128)(2,1)}, u32[]{:S(2)}, u32[]{:S(2)}) %collective-permute-start.8) | collective-permute-done | bytes 393248 | tf_op jit(solution)/shard_map/ppermute | solution.py:362
  28.3 1.7 collective-permute-start.4
  30.0 5.1 %collective-permute-done.3.refs_4_.refs_0_ = bf16[512,1024]{1,0:T(8,128)(2,1)S(1)} collective-permute-done((bf16[512,1024]{1,0:T(8,128)(2,1)}, bf16[512,1024]{1,0:T(8,128)(2,1)S(1)}, u32[]{:S(2)}, u32[]{:S(2)}) %collective-permute-start.3) | collective-permute-done | bytes 1048608 | tf_op jit(solution)/shard_map/ppermute | solution.py:359
  35.1 0.5 add_multiply_fusion
  35.6 0.8 reshape.312
  36.4 0.7 fusion.8
  37.1 0.2 fusion.9
  37.3 1.3 join.1.refs_8_
  38.6 0.6 collective-permute-start.11
  39.3 6.2 %collective-permute-start.13 = (bf16[4,128,1024]{2,1,0:T(8,128)(2,1)S(1)}, bf16[4,128,1024]{2,1,0:T(8,128)(2,1)S(1)}, u32[]{:S(2)}, u32[]{:S(2)}) collective-permute-start(bf16[4,128,1024]{2,1,0:T(8,128)(2,1)S(1)} %bitcast.35), channel_id=1, source_target_pairs={{0,31},{1,2},{2,1},{3,4},{4,3},{5,6},{6,5},{7,8},{8,7},{9,10},{10,... | collective-permute-start | bytes 3145736 | tf_op jit(solution)/shard_map/ppermute | solution.py:356
  45.5 0.5 collective-permute-start.6
  46.1 0.5 collective-permute-start.14
  47.0 4.8 %shard_map.57.acc_ref = f32[4,128,1024]{2,1,0:T(8,128)S(1)} custom-call(s32[2,2,48]{2,1,0:T(2,128)S(1)} %pad_add_fusion.1.near_ref, bf16[2,4,12,128,128]{4,3,2,1,0:T(8,128)(2,1)S(1)} %copy-done, bf16[8,128,1024]{2,1,0:T(8,128)(2,1)S(1)} %bitcast.22, bf16[8,128,1024]{2,1,0:T(8,128)(2,1)} %collective-permute-done.refs_1_), custom_call_target="tpu_custom_call" | custom-call | flops 1610612736 | bytes 8388608 | tf_op jit(solution)/shard_map/pallas_call | solution.py:286
  51.8 4.3 %shard_map.55.acc_ref = f32[4,128,1024]{2,1,0:T(8,128)S(1)} custom-call(s32[2,2,48]{2,1,0:T(2,128)S(1)} %pad_add_fusion.1.near_ref, bf16[2,4,12,128,128]{4,3,2,1,0:T(8,128)(2,1)S(1)} %copy-done, bf16[8,128,1024]{2,1,0:T(8,128)(2,1)S(1)} %bitcast.23, bf16[8,128,1024]{2,1,0:T(8,128)(2,1)} %collective-permute-done.refs_1_), custom_call_target="tpu_custom_call" | custom-call | flops 1610612736 | bytes 8388608 | tf_op jit(solution)/shard_map/pallas_call | solution.py:286
  56.1 20.4 %collective-permute-start.16 = (bf16[512,1024]{1,0:T(8,128)(2,1)S(1)}, bf16[512,1024]{1,0:T(8,128)(2,1)S(1)}, u32[]{:S(2)}, u32[]{:S(2)}) collective-permute-start(bf16[512,1024]{1,0:T(8,128)(2,1)S(1)} %collective-permute-done.3.refs_4_.refs_0_), channel_id=1, source_target_pairs={{64,96},{65,97},{66,98},{67,99},{68,100},{69,101},{70,102},{71,103... | collective-permute-start | bytes 3145736 | tf_op jit(solution)/shard_map/ppermute | solution.py:359
  76.5 0.7 collective-permute-start.17
  77.3 1.9 pick.3
  79.2 2.6 %shard_map.56.refs_0_.resid_ref = bf16[4,128,1024]{2,1,0:T(8,128)(2,1)S(1)} custom-call(s32[2,3,48]{2,1,0:T(4,128)S(1)} %pad_add_fusion.far_ref, s32[4]{0:T(128)S(1)} %get-tuple-element.28.meta_ref, bf16[2,4,12,128,128]{4,3,2,1,0:T(8,128)(2,1)S(1)} %copy-done, f32[4,128,1024]{2,1,0:T(8,128)S(1)} %shard_map.55.acc_ref, bf16[8,128,1024]{2,1,0:T(8,128)(2,1)S(1)} %bitcast.24, ...), custom_call_target="tpu_custom_call" | custom-call | flops 2147483648 | bytes 8388608 | tf_op jit(solution)/shard_map/pallas_call | solution.py:315
  81.8 2.7 %shard_map.58.refs_1_.resid_ref = bf16[4,128,1024]{2,1,0:T(8,128)(2,1)S(1)} custom-call(s32[2,3,48]{2,1,0:T(4,128)S(1)} %pad_add_fusion.far_ref, s32[4]{0:T(128)S(1)} %get-tuple-element.28.meta_ref, bf16[2,4,12,128,128]{4,3,2,1,0:T(8,128)(2,1)S(1)} %copy-done, f32[4,128,1024]{2,1,0:T(8,128)S(1)} %shard_map.57.acc_ref, bf16[8,128,1024]{2,1,0:T(8,128)(2,1)S(1)} %bitcast.25, ...), custom_call_target="tpu_custom_call" | custom-call | flops 2147483648 | bytes 8388608 | tf_op jit(solution)/shard_map/pallas_call | solution.py:315
  84.5 0.6 collective-permute-start.21
  85.1 11.8 %collective-permute-done.16.refs_4_ = bf16[512,1024]{1,0:T(8,128)(2,1)S(1)} collective-permute-done((bf16[512,1024]{1,0:T(8,128)(2,1)S(1)}, bf16[512,1024]{1,0:T(8,128)(2,1)S(1)}, u32[]{:S(2)}, u32[]{:S(2)}) %collective-permute-start.16) | collective-permute-done | bytes 1048608 | tf_op jit(solution)/shard_map/ppermute | solution.py:359
  96.9 0.5 collective-permute-start.19
  97.4 2.8 %collective-permute-start.20 = (bf16[4,128,1024]{2,1,0:T(8,128)(2,1)S(1)}, bf16[4,128,1024]{2,1,0:T(8,128)(2,1)S(1)}, u32[]{:S(2)}, u32[]{:S(2)}) collective-permute-start(bf16[4,128,1024]{2,1,0:T(8,128)(2,1)S(1)} %shard_map.56.refs_0_.resid_ref), channel_id=1, source_target_pairs={{0,31},{1,2},{2,1},{3,4},{4,3},{5,6},{6,5},{7,8},{8,7},{9,10},{10,... | collective-permute-start | bytes 3145736 | tf_op jit(solution)/shard_map/ppermute | solution.py:356
  100.2 2.3 collective-permute-start.22
  102.5 22.3 %collective-permute-start.24 = (bf16[512,1024]{1,0:T(8,128)(2,1)S(1)}, bf16[512,1024]{1,0:T(8,128)(2,1)S(1)}, u32[]{:S(2)}, u32[]{:S(2)}) collective-permute-start(bf16[512,1024]{1,0:T(8,128)(2,1)S(1)} %copy-done.4), channel_id=1, source_target_pairs={{64,96},{65,97},{66,98},{67,99},{68,100},{69,101},{70,102},{71,103... | collective-permute-start | bytes 3145736 | tf_op jit(solution)/shard_map/ppermute | solution.py:359
  124.8 3.2 %shard_map.59.acc_ref = f32[4,128,1024]{2,1,0:T(8,128)S(1)} custom-call(s32[2,2,48]{2,1,0:T(2,128)S(1)} %pad_add_fusion.1.near_ref, bf16[2,4,12,128,128]{4,3,2,1,0:T(8,128)(2,1)S(1)} %copy-done, bf16[4,128,1024]{2,1,0:T(8,128)(2,1)S(1)} %shard_map.56.refs_0_.resid_ref, bf16[4,128,1024]{2,1,0:T(8,128)(2,1)S(1)} %collective-permute-done.15.refs_1_.refs_2_), custom_call_target="tpu_custom_call" | custom-call | flops 1610612736 | bytes 8388608 | tf_op jit(solution)/shard_map/pallas_call | solution.py:286
  128.0 3.4 %shard_map.61.acc_ref = f32[4,128,1024]{2,1,0:T(8,128)S(1)} custom-call(s32[2,2,48]{2,1,0:T(2,128)S(1)} %pad_add_fusion.1.near_ref, bf16[2,4,12,128,128]{4,3,2,1,0:T(8,128)(2,1)S(1)} %copy-done, bf16[4,128,1024]{2,1,0:T(8,128)(2,1)S(1)} %shard_map.56.refs_0_.resid_ref, bf16[4,128,1024]{2,1,0:T(8,128)(2,1)S(1)} %shard_map.58.refs_1_.resid_ref, ...), custom_call_target="tpu_custom_call" | custom-call | flops 1610612736 | bytes 8388608 | tf_op jit(solution)/shard_map/pallas_call | solution.py:286
  131.4 0.9 pick.4
  132.3 2.7 %shard_map.62.refs_1_.resid_ref.refs_3_ = bf16[4,128,1024]{2,1,0:T(8,128)(2,1)S(1)} custom-call(s32[2,3,48]{2,1,0:T(4,128)S(1)} %pad_add_fusion.far_ref, s32[4]{0:T(128)S(1)} %get-tuple-element.36.meta_ref, bf16[2,4,12,128,128]{4,3,2,1,0:T(8,128)(2,1)S(1)} %copy-done, f32[4,128,1024]{2,1,0:T(8,128)S(1)} %shard_map.61.acc_ref, ...), custom_call_target="tpu_custom_call" | custom-call | flops 2147483648 | bytes 8388608 | tf_op jit(solution)/shard_map/pallas_call | solution.py:315
  135.0 9.3 %collective-permute-done.24.refs_1_ = bf16[512,1024]{1,0:T(8,128)(2,1)S(1)} collective-permute-done((bf16[512,1024]{1,0:T(8,128)(2,1)S(1)}, bf16[512,1024]{1,0:T(8,128)(2,1)S(1)}, u32[]{:S(2)}, u32[]{:S(2)}) %collective-permute-start.24) | collective-permute-done | bytes 1048608 | tf_op jit(solution)/shard_map/ppermute | solution.py:359
  144.3 2.6 %shard_map.60.refs_0_.resid_ref.refs_2_ = bf16[4,128,1024]{2,1,0:T(8,128)(2,1)S(1)} custom-call(s32[2,3,48]{2,1,0:T(4,128)S(1)} %pad_add_fusion.far_ref, s32[4]{0:T(128)S(1)} %get-tuple-element.36.meta_ref, bf16[2,4,12,128,128]{4,3,2,1,0:T(8,128)(2,1)S(1)} %copy-done, f32[4,128,1024]{2,1,0:T(8,128)S(1)} %shard_map.59.acc_ref, ...), custom_call_target="tpu_custom_call" | custom-call | flops 2147483648 | bytes 8388608 | tf_op jit(solution)/shard_map/pallas_call | solution.py:315
  146.9 0.6 collective-permute-start.23
  147.4 2.4 collective-permute-start.26
  149.8 2.7 %collective-permute-start.29 = (bf16[4,128,1024]{2,1,0:T(8,128)(2,1)S(1)}, bf16[4,128,1024]{2,1,0:T(8,128)(2,1)S(1)}, u32[]{:S(2)}, u32[]{:S(2)}) collective-permute-start(bf16[4,128,1024]{2,1,0:T(8,128)(2,1)S(1)} %shard_map.62.refs_1_.resid_ref.refs_3_), channel_id=1, source_target_pairs={{0,31},{1,2},{2,1},{3,4},{4,3},{5,6},{6,5},{7,8},{8,7},{9,10},{10,... | collective-permute-start | bytes 3145736 | tf_op jit(solution)/shard_map/ppermute | solution.py:356
  152.5 0.9 pick.5
  153.4 3.2 %shard_map.63.acc_ref = f32[4,128,1024]{2,1,0:T(8,128)S(1)} custom-call(s32[2,2,48]{2,1,0:T(2,128)S(1)} %pad_add_fusion.1.near_ref, bf16[2,4,12,128,128]{4,3,2,1,0:T(8,128)(2,1)S(1)} %copy-done, bf16[4,128,1024]{2,1,0:T(8,128)(2,1)S(1)} %shard_map.60.refs_0_.resid_ref.refs_2_, bf16[4,128,1024]{2,1,0:T(8,128)(2,1)S(1)} %collective-permute-done.23.refs_1_.refs_2_), custom_call_target="tpu_custom_call" | custom-call | flops 1610612736 | bytes 8388608 | tf_op jit(solution)/shard_map/pallas_call | solution.py:286
  156.6 8.4 %collective-permute-done.26.refs_0_ = bf16[4,128,1024]{2,1,0:T(8,128)(2,1)S(1)} collective-permute-done((bf16[4,128,1024]{2,1,0:T(8,128)(2,1)S(1)}, bf16[4,128,1024]{2,1,0:T(8,128)(2,1)S(1)}, u32[]{:S(2)}, u32[]{:S(2)}) %collective-permute-start.26) | collective-permute-done | bytes 1048608 | tf_op jit(solution)/shard_map/ppermute | solution.py:356
  165.0 2.6 %shard_map.64.refs_0_.resid_ref = bf16[4,128,1024]{2,1,0:T(8,128)(2,1)S(1)} custom-call(s32[2,3,48]{2,1,0:T(4,128)S(1)} %pad_add_fusion.far_ref, s32[4]{0:T(128)S(1)} %pad_add_fusion.4.meta_ref, bf16[2,4,12,128,128]{4,3,2,1,0:T(8,128)(2,1)S(1)} %copy-done, f32[4,128,1024]{2,1,0:T(8,128)S(1)} %shard_map.63.acc_ref, ...), custom_call_target="tpu_custom_call" | custom-call | flops 2147483648 | bytes 8388608 | tf_op jit(solution)/shard_map/pallas_call | solution.py:315
  167.7 3.4 %shard_map.65.acc_ref = f32[4,128,1024]{2,1,0:T(8,128)S(1)} custom-call(s32[2,2,48]{2,1,0:T(2,128)S(1)} %pad_add_fusion.1.near_ref, bf16[2,4,12,128,128]{4,3,2,1,0:T(8,128)(2,1)S(1)} %copy-done, bf16[4,128,1024]{2,1,0:T(8,128)(2,1)S(1)} %shard_map.60.refs_0_.resid_ref.refs_2_, bf16[4,128,1024]{2,1,0:T(8,128)(2,1)S(1)} %shard_map.62.refs_1_.resid_ref.refs_3_, ...), custom_call_target="tpu_custom_call" | custom-call | flops 1610612736 | bytes 8388608 | tf_op jit(solution)/shard_map/pallas_call | solution.py:286
  171.0 5.2 %collective-permute-done.29.refs_1_ = bf16[4,128,1024]{2,1,0:T(8,128)(2,1)S(1)} collective-permute-done((bf16[4,128,1024]{2,1,0:T(8,128)(2,1)S(1)}, bf16[4,128,1024]{2,1,0:T(8,128)(2,1)S(1)}, u32[]{:S(2)}, u32[]{:S(2)}) %collective-permute-start.29) | collective-permute-done | bytes 1048608 | tf_op jit(solution)/shard_map/ppermute | solution.py:356
  176.2 2.7 %shard_map.66.refs_1_.resid_ref = bf16[4,128,1024]{2,1,0:T(8,128)(2,1)S(1)} custom-call(s32[2,3,48]{2,1,0:T(4,128)S(1)} %pad_add_fusion.far_ref, s32[4]{0:T(128)S(1)} %pad_add_fusion.4.meta_ref, bf16[2,4,12,128,128]{4,3,2,1,0:T(8,128)(2,1)S(1)} %copy-done, f32[4,128,1024]{2,1,0:T(8,128)S(1)} %shard_map.65.acc_ref, ...), custom_call_target="tpu_custom_call" | custom-call | flops 2147483648 | bytes 8388608 | tf_op jit(solution)/shard_map/pallas_call | solution.py:315
  179.0 2.5 %collective-permute-start.33 = (bf16[4,128,1024]{2,1,0:T(8,128)(2,1)S(1)}, bf16[4,128,1024]{2,1,0:T(8,128)(2,1)S(1)}, u32[]{:S(2)}, u32[]{:S(2)}) collective-permute-start(bf16[4,128,1024]{2,1,0:T(8,128)(2,1)S(1)} %shard_map.64.refs_0_.resid_ref), channel_id=1, source_target_pairs={{0,31},{1,2},{2,1},{3,4},{4,3},{5,6},{6,5},{7,8},{8,7},{9,10},{10,... | collective-permute-start | bytes 3145736 | tf_op jit(solution)/shard_map/ppermute | solution.py:356
  181.5 2.7 %collective-permute-start.34 = (bf16[4,128,1024]{2,1,0:T(8,128)(2,1)S(1)}, bf16[4,128,1024]{2,1,0:T(8,128)(2,1)S(1)}, u32[]{:S(2)}, u32[]{:S(2)}) collective-permute-start(bf16[4,128,1024]{2,1,0:T(8,128)(2,1)S(1)} %shard_map.66.refs_1_.resid_ref), channel_id=1, source_target_pairs={{0,31},{1,2},{2,1},{3,4},{4,3},{5,6},{6,5},{7,8},{8,7},{9,10},{10,... | collective-permute-start | bytes 3145736 | tf_op jit(solution)/shard_map/ppermute | solution.py:356
  184.2 1.3 collective-permute-start.27
  185.5 1.5 collective-permute-start.30
  187.0 3.2 %shard_map.68.acc_ref = f32[4,128,1024]{2,1,0:T(8,128)S(1)} custom-call(s32[2,2,48]{2,1,0:T(2,128)S(1)} %pad_add_fusion.1.near_ref, bf16[2,4,12,128,128]{4,3,2,1,0:T(8,128)(2,1)S(1)} %copy-done, bf16[4,128,1024]{2,1,0:T(8,128)(2,1)S(1)} %shard_map.64.refs_0_.resid_ref, bf16[4,128,1024]{2,1,0:T(8,128)(2,1)S(1)} %collective-permute-done.31.refs_2_.refs_1_), custom_call_target="tpu_custom_call" | custom-call | flops 1610612736 | bytes 8388608 | tf_op jit(solution)/shard_map/pallas_call | solution.py:286
  190.2 3.4 %shard_map.67.acc_ref = f32[4,128,1024]{2,1,0:T(8,128)S(1)} custom-call(s32[2,2,48]{2,1,0:T(2,128)S(1)} %pad_add_fusion.1.near_ref, bf16[2,4,12,128,128]{4,3,2,1,0:T(8,128)(2,1)S(1)} %copy-done, bf16[4,128,1024]{2,1,0:T(8,128)(2,1)S(1)} %shard_map.64.refs_0_.resid_ref, bf16[4,128,1024]{2,1,0:T(8,128)(2,1)S(1)} %shard_map.66.refs_1_.resid_ref, ...), custom_call_target="tpu_custom_call" | custom-call | flops 1610612736 | bytes 8388608 | tf_op jit(solution)/shard_map/pallas_call | solution.py:286
  193.6 3.0 %collective-permute-done.33.refs_0_ = bf16[4,128,1024]{2,1,0:T(8,128)(2,1)S(1)} collective-permute-done((bf16[4,128,1024]{2,1,0:T(8,128)(2,1)S(1)}, bf16[4,128,1024]{2,1,0:T(8,128)(2,1)S(1)}, u32[]{:S(2)}, u32[]{:S(2)}) %collective-permute-start.33) | collective-permute-done | bytes 1048608 | tf_op jit(solution)/shard_map/ppermute | solution.py:356
  196.6 2.6 %shard_map.69.refs_2_ = bf16[8,128,1024]{2,1,0:T(8,128)(2,1)} custom-call(s32[2,3,48]{2,1,0:T(4,128)S(1)} %pad_add_fusion.far_ref, s32[4]{0:T(128)S(1)} %pad_add_fusion.4.meta_ref, bf16[2,4,12,128,128]{4,3,2,1,0:T(8,128)(2,1)S(1)} %copy-done, f32[4,128,1024]{2,1,0:T(8,128)S(1)} %shard_map.68.acc_ref, bf16[4,128,1024]{2,1,0:T(8,128)(2,1)S(1)} %shard_map.64.refs_0_.resid_ref, ...), custom_call_target="tpu_custom_call" | custom-call | flops 2147483648 | bytes 8388608 | tf_op jit(solution)/shard_map/pallas_call | solution.py:315
  199.2 8.6 %collective-permute-done.34.refs_1_ = bf16[4,128,1024]{2,1,0:T(8,128)(2,1)S(1)} collective-permute-done((bf16[4,128,1024]{2,1,0:T(8,128)(2,1)S(1)}, bf16[4,128,1024]{2,1,0:T(8,128)(2,1)S(1)}, u32[]{:S(2)}, u32[]{:S(2)}) %collective-permute-start.34) | collective-permute-done | bytes 1048608 | tf_op jit(solution)/shard_map/ppermute | solution.py:356
  207.9 2.7 %shard_map.70.refs_6_ = bf16[8,128,1024]{2,1,0:T(8,128)(2,1)} custom-call(s32[2,3,48]{2,1,0:T(4,128)S(1)} %pad_add_fusion.far_ref, s32[4]{0:T(128)S(1)} %pad_add_fusion.4.meta_ref, bf16[2,4,12,128,128]{4,3,2,1,0:T(8,128)(2,1)S(1)} %copy-done, f32[4,128,1024]{2,1,0:T(8,128)S(1)} %shard_map.67.acc_ref, ...), custom_call_target="tpu_custom_call", output_to_operand_aliasing={{}: (9, {})} | custom-call | flops 2147483648 | bytes 8388608 | tf_op jit(solution)/shard_map/pallas_call | solution.py:315
  210.6 11.4 %collective-permute-done.27.refs_4_ = bf16[4,128,1024]{2,1,0:T(8,128)(2,1)S(1)} collective-permute-done((bf16[4,128,1024]{2,1,0:T(8,128)(2,1)S(1)}, bf16[4,128,1024]{2,1,0:T(8,128)(2,1)S(1)}, u32[]{:S(2)}, u32[]{:S(2)}) %collective-permute-start.27) | collective-permute-done | bytes 1048608 | tf_op jit(solution)/shard_map/ppermute | solution.py:359
  221.9 18.9 %collective-permute-done.30.refs_5_ = bf16[4,128,1024]{2,1,0:T(8,128)(2,1)S(1)} collective-permute-done((bf16[4,128,1024]{2,1,0:T(8,128)(2,1)S(1)}, bf16[4,128,1024]{2,1,0:T(8,128)(2,1)S(1)}, u32[]{:S(2)}, u32[]{:S(2)}) %collective-permute-start.30) | collective-permute-done | bytes 1048608 | tf_op jit(solution)/shard_map/ppermute | solution.py:359
  240.8 2.0 place.1
  (59 shorter events, 1.0 us)
Async XLA Ops:
  2.9 8.7 %copy-start.1 = (bf16[2,512,1024]{2,1,0:T(8,128)(2,1)S(1)}, bf16[2,512,1024]{2,1,0:T(8,128)(2,1)}, u32[]{:S(2)}) copy-start(bf16[2,512,1024]{2,1,0:T(8,128)(2,1)} %param.5) | copy-start | bytes 6291460
  2.9 27.0 %collective-permute-start.10 = (bf16[448,1024]{1,0:T(8,128)(2,1)}, bf16[448,1024]{1,0:T(8,128)(2,1)}, u32[]{:S(2)}, u32[]{:S(2)}) collective-permute-start(bf16[448,1024]{1,0:T(8,128)(2,1)} %get-tuple-element.33), channel_id=1, source_target_pairs={{0,96},{1,97},{2,98},{3,99},{4,100},{5,101},{6,102},{7,103},{8,104... | collective-permute-start | bytes 2752520 | tf_op jit(solution)/shard_map/ppermute | solution.py:359
  8.1 27.0 %collective-permute-start.3 = (bf16[512,1024]{1,0:T(8,128)(2,1)}, bf16[512,1024]{1,0:T(8,128)(2,1)S(1)}, u32[]{:S(2)}, u32[]{:S(2)}) collective-permute-start(bf16[512,1024]{1,0:T(8,128)(2,1)} %get-tuple-element.30.refs_0_), channel_id=1, source_target_pairs={{0,32},{32,64},{64,96},{1,33},{33,65},{65,97},{2,34},{34,66},{66,9... | collective-permute-start | bytes 3145736 | tf_op jit(solution)/shard_map/ppermute | solution.py:359
  10.9 0.8 collective-permute-start.7
  11.6 34.5 %collective-permute-start = (bf16[8,128,1024]{2,1,0:T(8,128)(2,1)S(1)}, bf16[8,128,1024]{2,1,0:T(8,128)(2,1)}, u32[]{:S(2)}, u32[]{:S(2)}) collective-permute-start(bf16[8,128,1024]{2,1,0:T(8,128)(2,1)S(1)} %bitcast.21), channel_id=1, source_target_pairs={{0,1},{1,0},{2,3},{3,2},{4,5},{5,4},{6,7},{7,6},{8,9},{9,8},{10,11... | collective-permute-start | bytes 6291464 | tf_op jit(solution)/shard_map/ppermute | solution.py:353
  11.7 13.1 %collective-permute-start.9 = (bf16[192,1024]{1,0:T(8,128)(2,1)S(1)}, bf16[192,1024]{1,0:T(8,128)(2,1)}, u32[]{:S(2)}, u32[]{:S(2)}) collective-permute-start(bf16[192,1024]{1,0:T(8,128)(2,1)S(1)} %collective-permute-done.7.refs_0_), channel_id=1, source_target_pairs={{0,24},{1,25},{2,26},{3,27},{4,28},{5,29},{6,30},{7,31},{8,0},{9,1... | collective-permute-start | bytes 1179656 | tf_op jit(solution)/shard_map/ppermute | solution.py:362
  15.8 12.5 %collective-permute-start.8 = (bf16[192,1024]{1,0:T(8,128)(2,1)S(1)}, bf16[192,1024]{1,0:T(8,128)(2,1)}, u32[]{:S(2)}, u32[]{:S(2)}) collective-permute-start(bf16[192,1024]{1,0:T(8,128)(2,1)S(1)} %collective-permute-done.7.refs_0_), channel_id=1, source_target_pairs={{0,8},{1,9},{2,10},{3,11},{4,12},{5,13},{6,14},{7,15},{8,16},{9,17... | collective-permute-start | bytes 1179656 | tf_op jit(solution)/shard_map/ppermute | solution.py:362
  24.8 13.9 %collective-permute-start.1 = (bf16[512,1024]{1,0:T(8,128)(2,1)}, bf16[512,1024]{1,0:T(8,128)(2,1)}, u32[]{:S(2)}, u32[]{:S(2)}) collective-permute-start(bf16[512,1024]{1,0:T(8,128)(2,1)} %get-tuple-element.30.refs_0_), channel_id=1, source_target_pairs={{0,1},{1,0},{2,3},{3,2},{4,5},{5,4},{6,7},{7,6},{8,9},{9,8},{10,11... | collective-permute-start | bytes 3145736 | tf_op jit(solution)/shard_map/ppermute | solution.py:353
  28.3 10.9 %collective-permute-start.4 = (bf16[512,1024]{1,0:T(8,128)(2,1)}, bf16[512,1024]{1,0:T(8,128)(2,1)}, u32[]{:S(2)}, u32[]{:S(2)}) collective-permute-start(bf16[512,1024]{1,0:T(8,128)(2,1)} %get-tuple-element.39.refs_1_), channel_id=1, source_target_pairs={{0,32},{1,33},{2,34},{3,35},{4,36},{5,37},{6,38},{7,39},{8,40},{9,... | collective-permute-start | bytes 3145736 | tf_op jit(solution)/shard_map/ppermute | solution.py:359
  30.0 15.5 %collective-permute-start.2 = (bf16[512,1024]{1,0:T(8,128)(2,1)}, bf16[512,1024]{1,0:T(8,128)(2,1)}, u32[]{:S(2)}, u32[]{:S(2)}) collective-permute-start(bf16[512,1024]{1,0:T(8,128)(2,1)} %get-tuple-element.39.refs_1_), channel_id=1, source_target_pairs={{0,1},{1,0},{2,3},{3,2},{4,5},{5,4},{6,7},{7,6},{8,9},{9,8},{10,11... | collective-permute-start | bytes 3145736 | tf_op jit(solution)/shard_map/ppermute | solution.py:353
  35.1 10.4 %collective-permute-start.12 = (bf16[448,1024]{1,0:T(8,128)(2,1)}, bf16[448,1024]{1,0:T(8,128)(2,1)}, u32[]{:S(2)}, u32[]{:S(2)}) collective-permute-start(bf16[448,1024]{1,0:T(8,128)(2,1)} %collective-permute-done.10.refs_9_), channel_id=1, source_target_pairs={{0,1},{1,0},{2,3},{3,2},{4,5},{5,4},{6,7},{7,6},{8,9},{9,8},{10,11... | collective-permute-start | bytes 2752520 | tf_op jit(solution)/shard_map/ppermute | solution.py:353
  37.1 9.8 %copy-start = (bf16[2,4,12,128,128]{4,3,2,1,0:T(8,128)(2,1)S(1)}, bf16[2,4,12,128,128]{4,3,2,1,0:T(8,128)(2,1)}, u32[]{:S(2)}) copy-start(bf16[2,4,12,128,128]{4,3,2,1,0:T(8,128)(2,1)} %tiles_ref.31) | copy-start | bytes 9437188
  37.3 9.5 %copy-start.5 = (s32[2]{0:T(128)S(1)}, s32[2]{0:T(128)}, u32[]{:S(2)}) copy-start(s32[2]{0:T(128)} %get-tuple-element.49) | copy-start | bytes 28
  38.6 17.5 %collective-permute-start.11 = (bf16[576,1024]{1,0:T(8,128)(2,1)S(1)}, bf16[576,1024]{1,0:T(8,128)(2,1)S(1)}, u32[]{:S(2)}, u32[]{:S(2)}) collective-permute-start(bf16[576,1024]{1,0:T(8,128)(2,1)S(1)} %join.1.refs_8_), channel_id=1, source_target_pairs={{0,1},{1,0},{2,3},{3,2},{4,5},{5,4},{6,7},{7,6},{8,9},{9,8},{10,11... | collective-permute-start | bytes 3538952 | tf_op jit(solution)/shard_map/ppermute | solution.py:353
  39.3 39.9 %collective-permute-start.13 = (bf16[4,128,1024]{2,1,0:T(8,128)(2,1)S(1)}, bf16[4,128,1024]{2,1,0:T(8,128)(2,1)S(1)}, u32[]{:S(2)}, u32[]{:S(2)}) collective-permute-start(bf16[4,128,1024]{2,1,0:T(8,128)(2,1)S(1)} %bitcast.35), channel_id=1, source_target_pairs={{0,31},{1,2},{2,1},{3,4},{4,3},{5,6},{6,5},{7,8},{8,7},{9,10},{10,... | collective-permute-start | bytes 3145736 | tf_op jit(solution)/shard_map/ppermute | solution.py:356
  45.4 31.0 %collective-permute-start.5 = (bf16[512,1024]{1,0:T(8,128)(2,1)S(1)}, bf16[512,1024]{1,0:T(8,128)(2,1)S(1)}, u32[]{:S(2)}, u32[]{:S(2)}) collective-permute-start(bf16[512,1024]{1,0:T(8,128)(2,1)S(1)} %collective-permute-done.3.refs_4_.refs_0_), channel_id=1, source_target_pairs={{0,1},{1,0},{2,3},{3,2},{4,5},{5,4},{6,7},{7,6},{8,9},{9,8},{10,11... | collective-permute-start | bytes 3145736 | tf_op jit(solution)/shard_map/ppermute | solution.py:353
  45.5 31.8 %collective-permute-start.6 = (bf16[512,1024]{1,0:T(8,128)(2,1)}, bf16[512,1024]{1,0:T(8,128)(2,1)S(1)}, u32[]{:S(2)}, u32[]{:S(2)}) collective-permute-start(bf16[512,1024]{1,0:T(8,128)(2,1)} %collective-permute-done.4.refs_5_), channel_id=1, source_target_pairs={{0,1},{1,0},{2,3},{3,2},{4,5},{5,4},{6,7},{7,6},{8,9},{9,8},{10,11... | collective-permute-start | bytes 3145736 | tf_op jit(solution)/shard_map/ppermute | solution.py:353
  46.1 35.7 %collective-permute-start.14 = (bf16[4,128,1024]{2,1,0:T(8,128)(2,1)S(1)}, bf16[4,128,1024]{2,1,0:T(8,128)(2,1)S(1)}, u32[]{:S(2)}, u32[]{:S(2)}) collective-permute-start(bf16[4,128,1024]{2,1,0:T(8,128)(2,1)S(1)} %bitcast.34), channel_id=1, source_target_pairs={{0,31},{1,2},{2,1},{3,4},{4,3},{5,6},{6,5},{7,8},{8,7},{9,10},{10,... | collective-permute-start | bytes 3145736 | tf_op jit(solution)/shard_map/ppermute | solution.py:356
  51.8 24.8 %copy-start.4 = (bf16[512,1024]{1,0:T(8,128)(2,1)S(1)}, bf16[512,1024]{1,0:T(8,128)(2,1)}, u32[]{:S(2)}) copy-start(bf16[512,1024]{1,0:T(8,128)(2,1)} %get-tuple-element.39.refs_1_) | copy-start | bytes 3145732
  56.1 40.8 %collective-permute-start.16 = (bf16[512,1024]{1,0:T(8,128)(2,1)S(1)}, bf16[512,1024]{1,0:T(8,128)(2,1)S(1)}, u32[]{:S(2)}, u32[]{:S(2)}) collective-permute-start(bf16[512,1024]{1,0:T(8,128)(2,1)S(1)} %collective-permute-done.3.refs_4_.refs_0_), channel_id=1, source_target_pairs={{64,96},{65,97},{66,98},{67,99},{68,100},{69,101},{70,102},{71,103... | collective-permute-start | bytes 3145736 | tf_op jit(solution)/shard_map/ppermute | solution.py:359
  76.5 20.4 %collective-permute-start.17 = (bf16[512,1024]{1,0:T(8,128)(2,1)S(1)}, bf16[512,1024]{1,0:T(8,128)(2,1)S(1)}, u32[]{:S(2)}, u32[]{:S(2)}) collective-permute-start(bf16[512,1024]{1,0:T(8,128)(2,1)S(1)} %copy-done.4), channel_id=1, source_target_pairs={{32,96},{33,97},{34,98},{35,99},{36,100},{37,101},{38,102},{39,103... | collective-permute-start | bytes 3145736 | tf_op jit(solution)/shard_map/ppermute | solution.py:359
  81.7 18.4 %collective-permute-start.15 = (bf16[4,128,1024]{2,1,0:T(8,128)(2,1)S(1)}, bf16[4,128,1024]{2,1,0:T(8,128)(2,1)S(1)}, u32[]{:S(2)}, u32[]{:S(2)}) collective-permute-start(bf16[4,128,1024]{2,1,0:T(8,128)(2,1)S(1)} %shard_map.56.refs_0_.resid_ref), channel_id=1, source_target_pairs={{0,1},{1,0},{2,3},{3,2},{4,5},{5,4},{6,7},{7,6},{8,9},{9,8},{10,11... | collective-permute-start | bytes 3145736 | tf_op jit(solution)/shard_map/ppermute | solution.py:353
  84.5 17.9 %collective-permute-start.21 = (bf16[4,128,1024]{2,1,0:T(8,128)(2,1)S(1)}, bf16[4,128,1024]{2,1,0:T(8,128)(2,1)S(1)}, u32[]{:S(2)}, u32[]{:S(2)}) collective-permute-start(bf16[4,128,1024]{2,1,0:T(8,128)(2,1)S(1)} %shard_map.58.refs_1_.resid_ref), channel_id=1, source_target_pairs={{0,1},{1,0},{2,3},{3,2},{4,5},{5,4},{6,7},{7,6},{8,9},{9,8},{10,11... | collective-permute-start | bytes 3145736 | tf_op jit(solution)/shard_map/ppermute | solution.py:353
  96.9 34.5 %collective-permute-start.18 = (bf16[512,1024]{1,0:T(8,128)(2,1)S(1)}, bf16[512,1024]{1,0:T(8,128)(2,1)S(1)}, u32[]{:S(2)}, u32[]{:S(2)}) collective-permute-start(bf16[512,1024]{1,0:T(8,128)(2,1)S(1)} %collective-permute-done.16.refs_4_), channel_id=1, source_target_pairs={{0,1},{1,0},{2,3},{3,2},{4,5},{5,4},{6,7},{7,6},{8,9},{9,8},{10,11... | collective-permute-start | bytes 3145736 | tf_op jit(solution)/shard_map/ppermute | solution.py:353
  96.9 34.5 %collective-permute-start.19 = (bf16[512,1024]{1,0:T(8,128)(2,1)S(1)}, bf16[512,1024]{1,0:T(8,128)(2,1)S(1)}, u32[]{:S(2)}, u32[]{:S(2)}) collective-permute-start(bf16[512,1024]{1,0:T(8,128)(2,1)S(1)} %collective-permute-done.17.refs_5_), channel_id=1, source_target_pairs={{0,1},{1,0},{2,3},{3,2},{4,5},{5,4},{6,7},{7,6},{8,9},{9,8},{10,11... | collective-permute-start | bytes 3145736 | tf_op jit(solution)/shard_map/ppermute | solution.py:353
  97.4 34.8 %collective-permute-start.20 = (bf16[4,128,1024]{2,1,0:T(8,128)(2,1)S(1)}, bf16[4,128,1024]{2,1,0:T(8,128)(2,1)S(1)}, u32[]{:S(2)}, u32[]{:S(2)}) collective-permute-start(bf16[4,128,1024]{2,1,0:T(8,128)(2,1)S(1)} %shard_map.56.refs_0_.resid_ref), channel_id=1, source_target_pairs={{0,31},{1,2},{2,1},{3,4},{4,3},{5,6},{6,5},{7,8},{8,7},{9,10},{10,... | collective-permute-start | bytes 3145736 | tf_op jit(solution)/shard_map/ppermute | solution.py:356
  100.2 32.1 %collective-permute-start.22 = (bf16[4,128,1024]{2,1,0:T(8,128)(2,1)S(1)}, bf16[4,128,1024]{2,1,0:T(8,128)(2,1)S(1)}, u32[]{:S(2)}, u32[]{:S(2)}) collective-permute-start(bf16[4,128,1024]{2,1,0:T(8,128)(2,1)S(1)} %shard_map.58.refs_1_.resid_ref), channel_id=1, source_target_pairs={{0,31},{1,2},{2,1},{3,4},{4,3},{5,6},{6,5},{7,8},{8,7},{9,10},{10,... | collective-permute-start | bytes 3145736 | tf_op jit(solution)/shard_map/ppermute | solution.py:356
  102.5 41.8 %collective-permute-start.24 = (bf16[512,1024]{1,0:T(8,128)(2,1)S(1)}, bf16[512,1024]{1,0:T(8,128)(2,1)S(1)}, u32[]{:S(2)}, u32[]{:S(2)}) collective-permute-start(bf16[512,1024]{1,0:T(8,128)(2,1)S(1)} %copy-done.4), channel_id=1, source_target_pairs={{64,96},{65,97},{66,98},{67,99},{68,100},{69,101},{70,102},{71,103... | collective-permute-start | bytes 3145736 | tf_op jit(solution)/shard_map/ppermute | solution.py:359
  144.3 8.2 %collective-permute-start.25 = (bf16[512,1024]{1,0:T(8,128)(2,1)S(1)}, bf16[512,1024]{1,0:T(8,128)(2,1)S(1)}, u32[]{:S(2)}, u32[]{:S(2)}) collective-permute-start(bf16[512,1024]{1,0:T(8,128)(2,1)S(1)} %collective-permute-done.24.refs_1_), channel_id=1, source_target_pairs={{0,1},{1,0},{2,3},{3,2},{4,5},{5,4},{6,7},{7,6},{8,9},{9,8},{10,11... | collective-permute-start | bytes 3145736 | tf_op jit(solution)/shard_map/ppermute | solution.py:353
  146.9 6.5 %collective-permute-start.23 = (bf16[4,128,1024]{2,1,0:T(8,128)(2,1)S(1)}, bf16[4,128,1024]{2,1,0:T(8,128)(2,1)S(1)}, u32[]{:S(2)}, u32[]{:S(2)}) collective-permute-start(bf16[4,128,1024]{2,1,0:T(8,128)(2,1)S(1)} %shard_map.60.refs_0_.resid_ref.refs_2_), channel_id=1, source_target_pairs={{0,1},{1,0},{2,3},{3,2},{4,5},{5,4},{6,7},{7,6},{8,9},{9,8},{10,11... | collective-permute-start | bytes 3145736 | tf_op jit(solution)/shard_map/ppermute | solution.py:353
  147.4 17.5 %collective-permute-start.26 = (bf16[4,128,1024]{2,1,0:T(8,128)(2,1)S(1)}, bf16[4,128,1024]{2,1,0:T(8,128)(2,1)S(1)}, u32[]{:S(2)}, u32[]{:S(2)}) collective-permute-start(bf16[4,128,1024]{2,1,0:T(8,128)(2,1)S(1)} %shard_map.60.refs_0_.resid_ref.refs_2_), channel_id=1, source_target_pairs={{0,31},{1,2},{2,1},{3,4},{4,3},{5,6},{6,5},{7,8},{8,7},{9,10},{10,... | collective-permute-start | bytes 3145736 | tf_op jit(solution)/shard_map/ppermute | solution.py:356
  149.8 17.8 %collective-permute-start.28 = (bf16[4,128,1024]{2,1,0:T(8,128)(2,1)S(1)}, bf16[4,128,1024]{2,1,0:T(8,128)(2,1)S(1)}, u32[]{:S(2)}, u32[]{:S(2)}) collective-permute-start(bf16[4,128,1024]{2,1,0:T(8,128)(2,1)S(1)} %shard_map.62.refs_1_.resid_ref.refs_3_), channel_id=1, source_target_pairs={{0,1},{1,0},{2,3},{3,2},{4,5},{5,4},{6,7},{7,6},{8,9},{9,8},{10,11... | collective-permute-start | bytes 3145736 | tf_op jit(solution)/shard_map/ppermute | solution.py:353
  149.8 26.4 %collective-permute-start.29 = (bf16[4,128,1024]{2,1,0:T(8,128)(2,1)S(1)}, bf16[4,128,1024]{2,1,0:T(8,128)(2,1)S(1)}, u32[]{:S(2)}, u32[]{:S(2)}) collective-permute-start(bf16[4,128,1024]{2,1,0:T(8,128)(2,1)S(1)} %shard_map.62.refs_1_.resid_ref.refs_3_), channel_id=1, source_target_pairs={{0,31},{1,2},{2,1},{3,4},{4,3},{5,6},{6,5},{7,8},{8,7},{9,10},{10,... | collective-permute-start | bytes 3145736 | tf_op jit(solution)/shard_map/ppermute | solution.py:356
  167.5 17.9 %collective-permute-start.31 = (bf16[4,128,1024]{2,1,0:T(8,128)(2,1)S(1)}, bf16[4,128,1024]{2,1,0:T(8,128)(2,1)S(1)}, u32[]{:S(2)}, u32[]{:S(2)}) collective-permute-start(bf16[4,128,1024]{2,1,0:T(8,128)(2,1)S(1)} %shard_map.64.refs_0_.resid_ref), channel_id=1, source_target_pairs={{0,1},{1,0},{2,3},{3,2},{4,5},{5,4},{6,7},{7,6},{8,9},{9,8},{10,11... | collective-permute-start | bytes 3145736 | tf_op jit(solution)/shard_map/ppermute | solution.py:353
  178.9 11.3 %collective-permute-start.32 = (bf16[4,128,1024]{2,1,0:T(8,128)(2,1)S(1)}, bf16[4,128,1024]{2,1,0:T(8,128)(2,1)S(1)}, u32[]{:S(2)}, u32[]{:S(2)}) collective-permute-start(bf16[4,128,1024]{2,1,0:T(8,128)(2,1)S(1)} %shard_map.66.refs_1_.resid_ref), channel_id=1, source_target_pairs={{0,1},{1,0},{2,3},{3,2},{4,5},{5,4},{6,7},{7,6},{8,9},{9,8},{10,11... | collective-permute-start | bytes 3145736 | tf_op jit(solution)/shard_map/ppermute | solution.py:353
  179.0 17.6 %collective-permute-start.33 = (bf16[4,128,1024]{2,1,0:T(8,128)(2,1)S(1)}, bf16[4,128,1024]{2,1,0:T(8,128)(2,1)S(1)}, u32[]{:S(2)}, u32[]{:S(2)}) collective-permute-start(bf16[4,128,1024]{2,1,0:T(8,128)(2,1)S(1)} %shard_map.64.refs_0_.resid_ref), channel_id=1, source_target_pairs={{0,31},{1,2},{2,1},{3,4},{4,3},{5,6},{6,5},{7,8},{8,7},{9,10},{10,... | collective-permute-start | bytes 3145736 | tf_op jit(solution)/shard_map/ppermute | solution.py:356
  181.5 26.4 %collective-permute-start.34 = (bf16[4,128,1024]{2,1,0:T(8,128)(2,1)S(1)}, bf16[4,128,1024]{2,1,0:T(8,128)(2,1)S(1)}, u32[]{:S(2)}, u32[]{:S(2)}) collective-permute-start(bf16[4,128,1024]{2,1,0:T(8,128)(2,1)S(1)} %shard_map.66.refs_1_.resid_ref), channel_id=1, source_target_pairs={{0,31},{1,2},{2,1},{3,4},{4,3},{5,6},{6,5},{7,8},{8,7},{9,10},{10,... | collective-permute-start | bytes 3145736 | tf_op jit(solution)/shard_map/ppermute | solution.py:356
  184.2 37.8 %collective-permute-start.27 = (bf16[4,128,1024]{2,1,0:T(8,128)(2,1)S(1)}, bf16[4,128,1024]{2,1,0:T(8,128)(2,1)S(1)}, u32[]{:S(2)}, u32[]{:S(2)}) collective-permute-start(bf16[4,128,1024]{2,1,0:T(8,128)(2,1)S(1)} %shard_map.64.refs_0_.resid_ref), channel_id=1, source_target_pairs={{96,64},{97,65},{98,66},{99,67},{100,68},{101,69},{102,70},{103,71... | collective-permute-start | bytes 3145736 | tf_op jit(solution)/shard_map/ppermute | solution.py:359
  185.5 55.4 %collective-permute-start.30 = (bf16[4,128,1024]{2,1,0:T(8,128)(2,1)S(1)}, bf16[4,128,1024]{2,1,0:T(8,128)(2,1)S(1)}, u32[]{:S(2)}, u32[]{:S(2)}) collective-permute-start(bf16[4,128,1024]{2,1,0:T(8,128)(2,1)S(1)} %shard_map.66.refs_1_.resid_ref), channel_id=1, source_target_pairs={{96,64},{97,65},{98,66},{99,67},{100,68},{101,69},{102,70},{103,71... | collective-permute-start | bytes 3145736 | tf_op jit(solution)/shard_map/ppermute | solution.py:359
  190.2 6.5 %copy-start.2 = (bf16[1,1024,1024]{2,1,0:T(8,128)(2,1)S(1)}, bf16[1,1024,1024]{2,1,0:T(8,128)(2,1)}, u32[]{:S(2)}) copy-start(bf16[1,1024,1024]{2,1,0:T(8,128)(2,1)} %param.7) | copy-start | bytes 6291460
  190.2 6.5 %copy-start.3 = (bf16[1,1024,1024]{2,1,0:T(8,128)(2,1)S(1)}, bf16[1,1024,1024]{2,1,0:T(8,128)(2,1)}, u32[]{:S(2)}) copy-start(bf16[1,1024,1024]{2,1,0:T(8,128)(2,1)} %param.8) | copy-start | bytes 6291460

commit v3 on v2

--- a/solution.py
+++ b/solution.py
@@ -73,7 +73,7 @@
     lax.fori_loop(0, blk_rows, one_row, 0)
 
 
-def pick_kernel(n_got, meta_ref, *refs):
+def pick_kernel(n_got, pieced, meta_ref, *refs):
     got_refs = refs[:n_got]
     w1_ref, w2_ref, sem = refs[n_got:]
     feat = w1_ref.shape[0]
@@ -100,7 +100,7 @@
 
     choices = []
     for at in range(0, n_got, 4):
-        form = halves if at < 8 else shards
+        form = shards if pieced and at else halves
         one, two = form(*got_refs[at : at + 2]), form(*got_refs[at + 2 : at + 4])
         choices += [(at // 2, one, two), (at // 2 + 1, two, one)]
     for value, one, two in choices:
@@ -109,12 +109,12 @@
     pltpu.make_async_copy(w2_ref, w2_ref, sem.at[1]).wait()
 
 
-def pick(meta, got):
+def pick(meta, got, pieced=False):
     feat = got[0].shape[-1]
     shape = jax.ShapeDtypeStruct((feat, feat), jnp.bfloat16)
     return list(
         pl.pallas_call(
-            functools.partial(pick_kernel, len(got)),
+            functools.partial(pick_kernel, len(got), pieced),
             out_shape=[shape, shape],
             in_specs=[SMEM] + [ANY] * len(got),
             out_specs=[VMEM, VMEM],
@@ -160,6 +160,25 @@
         cost_estimate=pl.CostEstimate(flops=0, bytes_accessed=4 * MIB, transcendentals=0),
         name="mine",
     )(meta, w_first, w_second)
+
+
+def choose_kernel(meta_ref, one_ref, two_ref, out_ref, sem):
+    for use, src in ((meta_ref[2] != 1, one_ref), (meta_ref[2] == 1, two_ref)):
+        pl.when(use)(pltpu.make_async_copy(src, out_ref, sem).start)
+    pltpu.make_async_copy(out_ref, out_ref, sem).wait()
+
+
+def choose(meta, one, two):
+    return pl.pallas_call(
+        choose_kernel,
+        out_shape=jax.ShapeDtypeStruct(one.shape, one.dtype),
+        in_specs=[SMEM, ANY, ANY],
+        out_specs=VMEM,
+        scratch_shapes=[pltpu.SemaphoreType.DMA],
+        compiler_params=pltpu.CompilerParams(vmem_limit_bytes=4 * MIB),
+        cost_estimate=pl.CostEstimate(flops=0, bytes_accessed=MIB, transcendentals=0),
+        name="choose",
+    )(meta, one, two)
 
 
 def join_kernel(*refs):
@@ -371,7 +390,7 @@
 
     is_hub = section == hub
     metas = [
-        meta(jnp.where(section == 0, 0, jnp.where(is_hub, 4, 2)), section != 2),
+        meta(jnp.where(section == 0, 0, 2), section != 2),
         meta(jnp.where(section == 1, 0, 2), (section == 1) | is_hub),
         meta(jnp.zeros_like(me), is_hub),
         meta(jnp.zeros_like(me), is_hub),
@@ -386,15 +405,14 @@
         return out, chip_out, over_out, [sums(s, out, chip_out) for s in range(spans)]
 
     shard, rest = mine(metas[3], w_first, w_second, [[(0, 0, CUT // 4)], [(0, 2, CUT // 4), (CUT, None, feat - CUT)]])
-    shard = hop(shard, [(0, hub)])
-    zero_b = hop(rest, [(0, hub)])
+    shard = choose(metas[3], hop(shard, [(0, hub)]), hop(shard, [(0, 1)]))
+    zero_b = [hop(rest, [(0, hub)]), hop(rest, [(0, 1)])]
     mine_a, mine_b = mine(metas[3], w_first, w_second, [[(0, None, feat // 2)], [(feat // 2, None, feat // 2)]])
     start = features.reshape(spans * blk_rows, tile_len, feat)
     chip0 = swap(start)
     over0 = [cross(start[s * blk_rows : (s + 1) * blk_rows]) for s in range(spans)]
-    next_a = hop(mine_a, [(0, 1), (1, 2), (2, hub)])
+    next_a = hop(mine_a, [(1, 2), (2, hub)])
     zero_a = join(shard, along_z(shard, 1), along_z(shard, -1))
-    next_b = hop(mine_b, [(0, 1)])
     ids = lax.dynamic_slice_in_dim(tile_block, me * blk_rows, blk_rows, 1)
     near, far = entry_tables(ids, me, parts, parts * blk_rows)
     near, far, *metas = lax.optimization_barrier((near, far, *metas))
@@ -404,17 +422,17 @@
     one_b = hop(after(mine_b, *acc), [(1, hub)])
     two_b = hop(after(mine_b, *acc), [(2, hub)])
     kept = [mine_a, mine_b, swap(mine_a), swap(mine_b)]
-    swap_next = [swap(next_a), swap(next_b)]
+    zero_b = choose(metas[3], *after(tuple(zero_b), *acc))
     swap_zero = [swap(zero_a), swap(zero_b)]
-    got = [*kept, next_a, next_b, *swap_next, zero_a, zero_b, *swap_zero]
-    h1, _, over1, acc = layer(0, acc, [start] * spans, over0, pick(metas[0], got))
+    got = [*kept, zero_a, zero_b, *swap_zero]
+    h1, _, over1, acc = layer(0, acc, [start] * spans, over0, pick(metas[0], got, True))
     one_a, one_b = after(one_a, h1[1]), after(one_b, h1[1])
     got = [*kept, one_a, one_b, swap(one_a), swap(one_b)]
     weights = pick(metas[1], got)
 
     h2, _, over2, acc = layer(1, acc, h1, over1, weights)
     two_b = after(two_b, h2[1])
-    got = [next_a, two_b, swap_next[0], swap(two_b)]
+    got = [next_a, two_b, swap(after(next_a, h2[1])), swap(two_b)]
     weights = pick(metas[2], got)
 
     h3, _, over3, acc = layer(2, acc, h2, over2, weights)

time: 244 us -> 225 us (0.922)
  starting transfers between devices: 82.2 us -> 55.5 us
  Pallas kernels: 63 us -> 66.3 us
  waiting for transfers between devices: 91.3 us -> 94.3 us
    ppermute x9 -> x10, starting transfers between devices: 53.1 us -> 28.3 us  [hop(): return lax.ppermute(value, 'section', pairs)]
    ppermute x8, waiting for transfers between devices: 25.3 us -> 41.8 us  [cross(): return lax.ppermute(value, 'dom', cross_pairs)]
    ppermute x9 -> x10, waiting for transfers between devices: 56.4 us -> 43.8 us  [hop(): return lax.ppermute(value, 'section', pairs)]
    pallas_call x3 -> x5, Pallas kernels: 3.61 us -> 6.37 us  [the longest x3 3.89 us: pick(): pl.pallas_call(functools.partial(pick_kernel, len(got), pieced), out_shap...]
  transfers between devices with their start and end apart: 35 -> 35, of which waited for: 11 -> 12; matrix products, arithmetic and copies ran while one was open for 2% -> 3% of each run, Pallas kernels for 24% -> 27%
where the time goes in v3:
time: 225 us; the launch traced here: 224 us
  waiting for transfers between devices  94.3 us (42%)
  Pallas kernels  66.3 us (29%)
  starting transfers between devices  55.5 us (25%)
  local copies, waits for them, and re-layouts  3.89 us (2%)
  other arithmetic  3.88 us (2%)
    ppermute x10, waiting for transfers between devices, hop(): return lax.ppermute(value, 'section', pairs)  43.8 us
    ppermute x8, waiting for transfers between devices, cross(): return lax.ppermute(value, 'dom', cross_pairs)  41.8 us
    pallas_call x8, Pallas kernels, early(): pl.pallas_call(functools.partial(early_kernel, span, n_src), out_shape=ja...  28.9 us
    ppermute x10, starting transfers between devices, hop(): return lax.ppermute(value, 'section', pairs)  28.3 us
    pallas_call x8, Pallas kernels, late(): pl.pallas_call(functools.partial(late_kernel, span, len(crosses), final),...  21.4 us
    ppermute x8, starting transfers between devices, cross(): return lax.ppermute(value, 'dom', cross_pairs)  20.4 us
    ppermute x2, waiting for transfers between devices, along_z(): lax.ppermute(value, 'dom', [(p, (p + by * row_parts) % parts) for p in ra...  8.58 us
    pallas_call x2, Pallas kernels, mine(): pl.pallas_call(functools.partial(mine_kernel, pieces), out_shape=shapes,...  6.08 us
  transfers between devices with their start and end apart: 35, of which 12 were waited for; matrix products, arithmetic and copies ran while one was open for 3% of the time, Pallas kernels for 27%

profile of v3, /device:TPU:4, one launch (start us, length us, event | category | flops | bytes accessed | tf_op | source)
XLA Modules:
  0.0 224.5 jit_solution(6418071935667024911)
XLA Ops:
  0.1 3.0 %mine.3 = (bf16[192,1024]{1,0:T(8,128)(2,1)}, bf16[448,1024]{1,0:T(8,128)(2,1)}) custom-call(s32[4]{0:T(128)S(1)} %pad_add_fusion.4.meta_ref, bf16[1024,1024]{1,0:T(8,128)(2,1)} %bitcast.26, bf16[1024,1024]{1,0:T(8,128)(2,1)} %bitcast.30), custom_call_target="tpu_custom_call" | custom-call | bytes 4194304 | tf_op jit(solution)/shard_map/mine/pallas_call | solution.py:153
  3.1 0.7 collective-permute-start.3
  3.8 1.4 collective-permute-start.4
  5.2 1.6 collective-permute-start.7
  6.8 3.1 %mine.2 = (bf16[512,1024]{1,0:T(8,128)(2,1)S(1)}, bf16[512,1024]{1,0:T(8,128)(2,1)}) custom-call(s32[4]{0:T(128)S(1)} %pad_add_fusion.4.meta_ref, bf16[1024,1024]{1,0:T(8,128)(2,1)} %bitcast.27, bf16[1024,1024]{1,0:T(8,128)(2,1)} %bitcast.31), custom_call_target="tpu_custom_call" | custom-call | bytes 4194304 | tf_op jit(solution)/shard_map/mine/pallas_call | solution.py:153
  9.9 0.6 collective-permute-start.1
  10.5 2.0 fusion.3
  12.5 0.8 copy.16
  13.6 0.7 copy-done.5
  14.3 1.0 copy-done.6
  15.3 0.7 choose.2.refs_0_
  16.1 2.0 collective-permute-start.5
  18.1 2.2 collective-permute-start.6
  20.3 0.7 select_reduce_fusion.2
  21.0 8.6 %collective-permute-done.5.refs_1_ = bf16[192,1024]{1,0:T(8,128)(2,1)} collective-permute-done((bf16[192,1024]{1,0:T(8,128)(2,1)S(1)}, bf16[192,1024]{1,0:T(8,128)(2,1)}, u32[]{:S(2)}, u32[]{:S(2)}) %collective-permute-start.5) | collective-permute-done | bytes 393248 | tf_op jit(solution)/shard_map/ppermute | solution.py:381
  29.6 0.7 collective-permute-start.8
  30.4 5.7 %collective-permute-start.14 = (bf16[512,1024]{1,0:T(8,128)(2,1)S(1)}, bf16[512,1024]{1,0:T(8,128)(2,1)S(1)}, u32[]{:S(2)}, u32[]{:S(2)}) collective-permute-start(bf16[512,1024]{1,0:T(8,128)(2,1)S(1)} %get-tuple-element.33.refs_0_), channel_id=1, source_target_pairs={{32,64},{64,96},{33,65},{65,97},{34,66},{66,98},{35,67},{67,99},{3... | collective-permute-start | bytes 3145736 | tf_op jit(solution)/shard_map/ppermute | solution.py:378
  36.2 0.8 select_reduce_fusion.1
  37.0 0.7 stack.71
  37.9 1.5 join.1.refs_4_
  39.8 4.8 %shard_map.56.acc_ref = f32[4,128,1024]{2,1,0:T(8,128)S(1)} custom-call(s32[2,2,48]{2,1,0:T(2,128)S(1)} %pad_add_fusion.1.near_ref, bf16[2,4,12,128,128]{4,3,2,1,0:T(8,128)(2,1)S(1)} %copy-done, bf16[8,128,1024]{2,1,0:T(8,128)(2,1)S(1)} %bitcast.22, bf16[8,128,1024]{2,1,0:T(8,128)(2,1)} %collective-permute-done.refs_1_), custom_call_target="tpu_custom_call" | custom-call | flops 1610612736 | bytes 8388608 | tf_op jit(solution)/shard_map/pallas_call | solution.py:305
  44.9 4.6 %collective-permute-start.11 = (bf16[4,128,1024]{2,1,0:T(8,128)(2,1)S(1)}, bf16[4,128,1024]{2,1,0:T(8,128)(2,1)S(1)}, u32[]{:S(2)}, u32[]{:S(2)}) collective-permute-start(bf16[4,128,1024]{2,1,0:T(8,128)(2,1)S(1)} %bitcast.35), channel_id=1, source_target_pairs={{0,31},{1,2},{2,1},{3,4},{4,3},{5,6},{6,5},{7,8},{8,7},{9,10},{10,... | collective-permute-start | bytes 3145736 | tf_op jit(solution)/shard_map/ppermute | solution.py:375
  50.0 4.4 %shard_map.55.acc_ref = f32[4,128,1024]{2,1,0:T(8,128)S(1)} custom-call(s32[2,2,48]{2,1,0:T(2,128)S(1)} %pad_add_fusion.1.near_ref, bf16[2,4,12,128,128]{4,3,2,1,0:T(8,128)(2,1)S(1)} %copy-done, bf16[8,128,1024]{2,1,0:T(8,128)(2,1)S(1)} %bitcast.23, bf16[8,128,1024]{2,1,0:T(8,128)(2,1)} %collective-permute-done.refs_1_), custom_call_target="tpu_custom_call" | custom-call | flops 1610612736 | bytes 8388608 | tf_op jit(solution)/shard_map/pallas_call | solution.py:305
  54.3 1.7 choose.3.refs_5_
  56.1 2.6 %collective-permute-done.14.refs_0_ = bf16[512,1024]{1,0:T(8,128)(2,1)S(1)} collective-permute-done((bf16[512,1024]{1,0:T(8,128)(2,1)S(1)}, bf16[512,1024]{1,0:T(8,128)(2,1)S(1)}, u32[]{:S(2)}, u32[]{:S(2)}) %collective-permute-start.14) | collective-permute-done | bytes 1048608 | tf_op jit(solution)/shard_map/ppermute | solution.py:378
  58.7 0.7 collective-permute-start.16
  59.4 2.3 %collective-permute-start.15 = (bf16[512,1024]{1,0:T(8,128)(2,1)S(1)}, bf16[512,1024]{1,0:T(8,128)(2,1)S(1)}, u32[]{:S(2)}, u32[]{:S(2)}) collective-permute-start(bf16[512,1024]{1,0:T(8,128)(2,1)S(1)} %collective-permute-done.14.refs_0_), channel_id=1, source_target_pairs={{64,96},{65,97},{66,98},{67,99},{68,100},{69,101},{70,102},{71,103... | collective-permute-start | bytes 3145736 | tf_op jit(solution)/shard_map/ppermute | solution.py:378
  61.8 2.2 pick.3
  63.9 9.7 %collective-permute-done.12.refs_1_ = bf16[4,128,1024]{2,1,0:T(8,128)(2,1)S(1)} collective-permute-done((bf16[4,128,1024]{2,1,0:T(8,128)(2,1)S(1)}, bf16[4,128,1024]{2,1,0:T(8,128)(2,1)S(1)}, u32[]{:S(2)}, u32[]{:S(2)}) %collective-permute-start.12) | collective-permute-done | bytes 1048608 | tf_op jit(solution)/shard_map/ppermute | solution.py:375
  73.7 2.7 %shard_map.58.refs_1_.resid_ref = bf16[4,128,1024]{2,1,0:T(8,128)(2,1)S(1)} custom-call(s32[2,3,48]{2,1,0:T(4,128)S(1)} %pad_add_fusion.far_ref, s32[4]{0:T(128)S(1)} %get-tuple-element.31.meta_ref, bf16[2,4,12,128,128]{4,3,2,1,0:T(8,128)(2,1)S(1)} %copy-done, f32[4,128,1024]{2,1,0:T(8,128)S(1)} %shard_map.56.acc_ref, bf16[8,128,1024]{2,1,0:T(8,128)(2,1)S(1)} %bitcast.24, ...), custom_call_target="tpu_custom_call" | custom-call | flops 2147483648 | bytes 8388608 | tf_op jit(solution)/shard_map/pallas_call | solution.py:334
  76.5 2.6 %shard_map.57.refs_0_.resid_ref = bf16[4,128,1024]{2,1,0:T(8,128)(2,1)S(1)} custom-call(s32[2,3,48]{2,1,0:T(4,128)S(1)} %pad_add_fusion.far_ref, s32[4]{0:T(128)S(1)} %get-tuple-element.31.meta_ref, bf16[2,4,12,128,128]{4,3,2,1,0:T(8,128)(2,1)S(1)} %copy-done, f32[4,128,1024]{2,1,0:T(8,128)S(1)} %shard_map.55.acc_ref, bf16[8,128,1024]{2,1,0:T(8,128)(2,1)S(1)} %bitcast.25, ...), custom_call_target="tpu_custom_call" | custom-call | flops 2147483648 | bytes 8388608 | tf_op jit(solution)/shard_map/pallas_call | solution.py:334
  79.7 5.0 %collective-permute-done.15.refs_4_ = bf16[512,1024]{1,0:T(8,128)(2,1)S(1)} collective-permute-done((bf16[512,1024]{1,0:T(8,128)(2,1)S(1)}, bf16[512,1024]{1,0:T(8,128)(2,1)S(1)}, u32[]{:S(2)}, u32[]{:S(2)}) %collective-permute-start.15) | collective-permute-done | bytes 1048608 | tf_op jit(solution)/shard_map/ppermute | solution.py:378
  84.7 4.5 %collective-permute-start.21 = (bf16[4,128,1024]{2,1,0:T(8,128)(2,1)S(1)}, bf16[4,128,1024]{2,1,0:T(8,128)(2,1)S(1)}, u32[]{:S(2)}, u32[]{:S(2)}) collective-permute-start(bf16[4,128,1024]{2,1,0:T(8,128)(2,1)S(1)} %shard_map.58.refs_1_.resid_ref), channel_id=1, source_target_pairs={{0,31},{1,2},{2,1},{3,4},{4,3},{5,6},{6,5},{7,8},{8,7},{9,10},{10,... | collective-permute-start | bytes 3145736 | tf_op jit(solution)/shard_map/ppermute | solution.py:375
  89.8 12.6 %collective-permute-start.23 = (bf16[512,1024]{1,0:T(8,128)(2,1)S(1)}, bf16[512,1024]{1,0:T(8,128)(2,1)S(1)}, u32[]{:S(2)}, u32[]{:S(2)}) collective-permute-start(bf16[512,1024]{1,0:T(8,128)(2,1)S(1)} %copy-done.4), channel_id=1, source_target_pairs={{64,96},{65,97},{66,98},{67,99},{68,100},{69,101},{70,102},{71,103... | collective-permute-start | bytes 3145736 | tf_op jit(solution)/shard_map/ppermute | solution.py:378
  102.4 3.4 %shard_map.61.acc_ref = f32[4,128,1024]{2,1,0:T(8,128)S(1)} custom-call(s32[2,2,48]{2,1,0:T(2,128)S(1)} %pad_add_fusion.1.near_ref, bf16[2,4,12,128,128]{4,3,2,1,0:T(8,128)(2,1)S(1)} %copy-done, bf16[4,128,1024]{2,1,0:T(8,128)(2,1)S(1)} %shard_map.57.refs_0_.resid_ref, bf16[4,128,1024]{2,1,0:T(8,128)(2,1)S(1)} %shard_map.58.refs_1_.resid_ref, ...), custom_call_target="tpu_custom_call" | custom-call | flops 1610612736 | bytes 8388608 | tf_op jit(solution)/shard_map/pallas_call | solution.py:305
  105.8 0.9 pick.4
  106.7 6.8 %collective-permute-done.19.refs_0_ = bf16[4,128,1024]{2,1,0:T(8,128)(2,1)S(1)} collective-permute-done((bf16[4,128,1024]{2,1,0:T(8,128)(2,1)S(1)}, bf16[4,128,1024]{2,1,0:T(8,128)(2,1)S(1)}, u32[]{:S(2)}, u32[]{:S(2)}) %collective-permute-start.19) | collective-permute-done | bytes 1048608 | tf_op jit(solution)/shard_map/ppermute | solution.py:375
  113.5 2.9 %shard_map.62.refs_1_.resid_ref.refs_3_ = bf16[4,128,1024]{2,1,0:T(8,128)(2,1)S(1)} custom-call(s32[2,3,48]{2,1,0:T(4,128)S(1)} %pad_add_fusion.far_ref, s32[4]{0:T(128)S(1)} %get-tuple-element.41.meta_ref, bf16[2,4,12,128,128]{4,3,2,1,0:T(8,128)(2,1)S(1)} %copy-done, f32[4,128,1024]{2,1,0:T(8,128)S(1)} %shard_map.61.acc_ref, ...), custom_call_target="tpu_custom_call" | custom-call | flops 2147483648 | bytes 8388608 | tf_op jit(solution)/shard_map/pallas_call | solution.py:334
  116.4 5.2 %collective-permute-done.23.refs_1_ = bf16[512,1024]{1,0:T(8,128)(2,1)S(1)} collective-permute-done((bf16[512,1024]{1,0:T(8,128)(2,1)S(1)}, bf16[512,1024]{1,0:T(8,128)(2,1)S(1)}, u32[]{:S(2)}, u32[]{:S(2)}) %collective-permute-start.23) | collective-permute-done | bytes 1048608 | tf_op jit(solution)/shard_map/ppermute | solution.py:378
  121.6 3.2 %shard_map.59.acc_ref = f32[4,128,1024]{2,1,0:T(8,128)S(1)} custom-call(s32[2,2,48]{2,1,0:T(2,128)S(1)} %pad_add_fusion.1.near_ref, bf16[2,4,12,128,128]{4,3,2,1,0:T(8,128)(2,1)S(1)} %copy-done, bf16[4,128,1024]{2,1,0:T(8,128)(2,1)S(1)} %shard_map.57.refs_0_.resid_ref, bf16[4,128,1024]{2,1,0:T(8,128)(2,1)S(1)} %collective-permute-done.13.refs_1_.refs_2_), custom_call_target="tpu_custom_call" | custom-call | flops 1610612736 | bytes 8388608 | tf_op jit(solution)/shard_map/pallas_call | solution.py:305
  124.8 0.6 collective-permute-start.24
  125.4 2.6 %shard_map.60.refs_0_.resid_ref.refs_2_ = bf16[4,128,1024]{2,1,0:T(8,128)(2,1)S(1)} custom-call(s32[2,3,48]{2,1,0:T(4,128)S(1)} %pad_add_fusion.far_ref, s32[4]{0:T(128)S(1)} %get-tuple-element.41.meta_ref, bf16[2,4,12,128,128]{4,3,2,1,0:T(8,128)(2,1)S(1)} %copy-done, f32[4,128,1024]{2,1,0:T(8,128)S(1)} %shard_map.59.acc_ref, ...), custom_call_target="tpu_custom_call" | custom-call | flops 2147483648 | bytes 8388608 | tf_op jit(solution)/shard_map/pallas_call | solution.py:334
  128.0 1.8 collective-permute-start.26
  129.8 3.4 %collective-permute-start.29 = (bf16[4,128,1024]{2,1,0:T(8,128)(2,1)S(1)}, bf16[4,128,1024]{2,1,0:T(8,128)(2,1)S(1)}, u32[]{:S(2)}, u32[]{:S(2)}) collective-permute-start(bf16[4,128,1024]{2,1,0:T(8,128)(2,1)S(1)} %shard_map.62.refs_1_.resid_ref.refs_3_), channel_id=1, source_target_pairs={{0,31},{1,2},{2,1},{3,4},{4,3},{5,6},{6,5},{7,8},{8,7},{9,10},{10,... | collective-permute-start | bytes 3145736 | tf_op jit(solution)/shard_map/ppermute | solution.py:375
  133.2 0.9 pick.5
  134.1 3.2 %shard_map.63.acc_ref = f32[4,128,1024]{2,1,0:T(8,128)S(1)} custom-call(s32[2,2,48]{2,1,0:T(2,128)S(1)} %pad_add_fusion.1.near_ref, bf16[2,4,12,128,128]{4,3,2,1,0:T(8,128)(2,1)S(1)} %copy-done, bf16[4,128,1024]{2,1,0:T(8,128)(2,1)S(1)} %shard_map.60.refs_0_.resid_ref.refs_2_, bf16[4,128,1024]{2,1,0:T(8,128)(2,1)S(1)} %collective-permute-done.22.refs_1_.refs_2_), custom_call_target="tpu_custom_call" | custom-call | flops 1610612736 | bytes 8388608 | tf_op jit(solution)/shard_map/pallas_call | solution.py:305
  137.3 8.4 %collective-permute-done.26.refs_0_ = bf16[4,128,1024]{2,1,0:T(8,128)(2,1)S(1)} collective-permute-done((bf16[4,128,1024]{2,1,0:T(8,128)(2,1)S(1)}, bf16[4,128,1024]{2,1,0:T(8,128)(2,1)S(1)}, u32[]{:S(2)}, u32[]{:S(2)}) %collective-permute-start.26) | collective-permute-done | bytes 1048608 | tf_op jit(solution)/shard_map/ppermute | solution.py:375
  145.6 2.6 %shard_map.64.refs_0_.resid_ref = bf16[4,128,1024]{2,1,0:T(8,128)(2,1)S(1)} custom-call(s32[2,3,48]{2,1,0:T(4,128)S(1)} %pad_add_fusion.far_ref, s32[4]{0:T(128)S(1)} %pad_add_fusion.4.meta_ref, bf16[2,4,12,128,128]{4,3,2,1,0:T(8,128)(2,1)S(1)} %copy-done, f32[4,128,1024]{2,1,0:T(8,128)S(1)} %shard_map.63.acc_ref, ...), custom_call_target="tpu_custom_call" | custom-call | flops 2147483648 | bytes 8388608 | tf_op jit(solution)/shard_map/pallas_call | solution.py:334
  148.3 3.4 %shard_map.65.acc_ref = f32[4,128,1024]{2,1,0:T(8,128)S(1)} custom-call(s32[2,2,48]{2,1,0:T(2,128)S(1)} %pad_add_fusion.1.near_ref, bf16[2,4,12,128,128]{4,3,2,1,0:T(8,128)(2,1)S(1)} %copy-done, bf16[4,128,1024]{2,1,0:T(8,128)(2,1)S(1)} %shard_map.60.refs_0_.resid_ref.refs_2_, bf16[4,128,1024]{2,1,0:T(8,128)(2,1)S(1)} %shard_map.62.refs_1_.resid_ref.refs_3_, ...), custom_call_target="tpu_custom_call" | custom-call | flops 1610612736 | bytes 8388608 | tf_op jit(solution)/shard_map/pallas_call | solution.py:305
  151.7 5.2 %collective-permute-done.29.refs_1_ = bf16[4,128,1024]{2,1,0:T(8,128)(2,1)S(1)} collective-permute-done((bf16[4,128,1024]{2,1,0:T(8,128)(2,1)S(1)}, bf16[4,128,1024]{2,1,0:T(8,128)(2,1)S(1)}, u32[]{:S(2)}, u32[]{:S(2)}) %collective-permute-start.29) | collective-permute-done | bytes 1048608 | tf_op jit(solution)/shard_map/ppermute | solution.py:375
  156.9 2.7 %shard_map.66.refs_1_.resid_ref = bf16[4,128,1024]{2,1,0:T(8,128)(2,1)S(1)} custom-call(s32[2,3,48]{2,1,0:T(4,128)S(1)} %pad_add_fusion.far_ref, s32[4]{0:T(128)S(1)} %pad_add_fusion.4.meta_ref, bf16[2,4,12,128,128]{4,3,2,1,0:T(8,128)(2,1)S(1)} %copy-done, f32[4,128,1024]{2,1,0:T(8,128)S(1)} %shard_map.65.acc_ref, ...), custom_call_target="tpu_custom_call" | custom-call | flops 2147483648 | bytes 8388608 | tf_op jit(solution)/shard_map/pallas_call | solution.py:334
  159.7 1.8 collective-permute-start.33
  161.5 3.4 %collective-permute-start.34 = (bf16[4,128,1024]{2,1,0:T(8,128)(2,1)S(1)}, bf16[4,128,1024]{2,1,0:T(8,128)(2,1)S(1)}, u32[]{:S(2)}, u32[]{:S(2)}) collective-permute-start(bf16[4,128,1024]{2,1,0:T(8,128)(2,1)S(1)} %shard_map.66.refs_1_.resid_ref), channel_id=1, source_target_pairs={{0,31},{1,2},{2,1},{3,4},{4,3},{5,6},{6,5},{7,8},{8,7},{9,10},{10,... | collective-permute-start | bytes 3145736 | tf_op jit(solution)/shard_map/ppermute | solution.py:375
  164.8 1.3 collective-permute-start.30
  166.1 1.3 collective-permute-start.27
  167.4 3.2 %shard_map.68.acc_ref = f32[4,128,1024]{2,1,0:T(8,128)S(1)} custom-call(s32[2,2,48]{2,1,0:T(2,128)S(1)} %pad_add_fusion.1.near_ref, bf16[2,4,12,128,128]{4,3,2,1,0:T(8,128)(2,1)S(1)} %copy-done, bf16[4,128,1024]{2,1,0:T(8,128)(2,1)S(1)} %shard_map.64.refs_0_.resid_ref, bf16[4,128,1024]{2,1,0:T(8,128)(2,1)S(1)} %collective-permute-done.31.refs_2_.refs_1_), custom_call_target="tpu_custom_call" | custom-call | flops 1610612736 | bytes 8388608 | tf_op jit(solution)/shard_map/pallas_call | solution.py:305
  170.6 3.4 %shard_map.67.acc_ref = f32[4,128,1024]{2,1,0:T(8,128)S(1)} custom-call(s32[2,2,48]{2,1,0:T(2,128)S(1)} %pad_add_fusion.1.near_ref, bf16[2,4,12,128,128]{4,3,2,1,0:T(8,128)(2,1)S(1)} %copy-done, bf16[4,128,1024]{2,1,0:T(8,128)(2,1)S(1)} %shard_map.64.refs_0_.resid_ref, bf16[4,128,1024]{2,1,0:T(8,128)(2,1)S(1)} %shard_map.66.refs_1_.resid_ref, ...), custom_call_target="tpu_custom_call" | custom-call | flops 1610612736 | bytes 8388608 | tf_op jit(solution)/shard_map/pallas_call | solution.py:305
  174.0 3.2 %collective-permute-done.33.refs_0_ = bf16[4,128,1024]{2,1,0:T(8,128)(2,1)S(1)} collective-permute-done((bf16[4,128,1024]{2,1,0:T(8,128)(2,1)S(1)}, bf16[4,128,1024]{2,1,0:T(8,128)(2,1)S(1)}, u32[]{:S(2)}, u32[]{:S(2)}) %collective-permute-start.33) | collective-permute-done | bytes 1048608 | tf_op jit(solution)/shard_map/ppermute | solution.py:375
  177.3 2.8 %shard_map.69.refs_2_ = bf16[8,128,1024]{2,1,0:T(8,128)(2,1)} custom-call(s32[2,3,48]{2,1,0:T(4,128)S(1)} %pad_add_fusion.far_ref, s32[4]{0:T(128)S(1)} %pad_add_fusion.4.meta_ref, bf16[2,4,12,128,128]{4,3,2,1,0:T(8,128)(2,1)S(1)} %copy-done, f32[4,128,1024]{2,1,0:T(8,128)S(1)} %shard_map.68.acc_ref, bf16[4,128,1024]{2,1,0:T(8,128)(2,1)S(1)} %shard_map.64.refs_0_.resid_ref, ...), custom_call_target="tpu_custom_call" | custom-call | flops 2147483648 | bytes 8388608 | tf_op jit(solution)/shard_map/pallas_call | solution.py:334
  180.1 8.4 %collective-permute-done.34.refs_1_ = bf16[4,128,1024]{2,1,0:T(8,128)(2,1)S(1)} collective-permute-done((bf16[4,128,1024]{2,1,0:T(8,128)(2,1)S(1)}, bf16[4,128,1024]{2,1,0:T(8,128)(2,1)S(1)}, u32[]{:S(2)}, u32[]{:S(2)}) %collective-permute-start.34) | collective-permute-done | bytes 1048608 | tf_op jit(solution)/shard_map/ppermute | solution.py:375
  188.5 2.7 %shard_map.70.refs_6_ = bf16[8,128,1024]{2,1,0:T(8,128)(2,1)} custom-call(s32[2,3,48]{2,1,0:T(4,128)S(1)} %pad_add_fusion.far_ref, s32[4]{0:T(128)S(1)} %pad_add_fusion.4.meta_ref, bf16[2,4,12,128,128]{4,3,2,1,0:T(8,128)(2,1)S(1)} %copy-done, f32[4,128,1024]{2,1,0:T(8,128)S(1)} %shard_map.67.acc_ref, ...), custom_call_target="tpu_custom_call", output_to_operand_aliasing={{}: (9, {})} | custom-call | flops 2147483648 | bytes 8388608 | tf_op jit(solution)/shard_map/pallas_call | solution.py:334
  191.2 12.1 %collective-permute-done.30.refs_5_ = bf16[4,128,1024]{2,1,0:T(8,128)(2,1)S(1)} collective-permute-done((bf16[4,128,1024]{2,1,0:T(8,128)(2,1)S(1)}, bf16[4,128,1024]{2,1,0:T(8,128)(2,1)S(1)}, u32[]{:S(2)}, u32[]{:S(2)}) %collective-permute-start.30) | collective-permute-done | bytes 1048608 | tf_op jit(solution)/shard_map/ppermute | solution.py:378
  203.4 18.9 %collective-permute-done.27.refs_4_ = bf16[4,128,1024]{2,1,0:T(8,128)(2,1)S(1)} collective-permute-done((bf16[4,128,1024]{2,1,0:T(8,128)(2,1)S(1)}, bf16[4,128,1024]{2,1,0:T(8,128)(2,1)S(1)}, u32[]{:S(2)}, u32[]{:S(2)}) %collective-permute-start.27) | collective-permute-done | bytes 1048608 | tf_op jit(solution)/shard_map/ppermute | solution.py:378
  222.2 2.0 place.1
  (63 shorter events, 3.4 us)
Async XLA Ops:
  0.1 5.1 %copy-start.1 = (bf16[2,512,1024]{2,1,0:T(8,128)(2,1)S(1)}, bf16[2,512,1024]{2,1,0:T(8,128)(2,1)}, u32[]{:S(2)}) copy-start(bf16[2,512,1024]{2,1,0:T(8,128)(2,1)} %param.5) | copy-start | bytes 6291460
  3.1 10.5 %collective-permute-start.3 = (bf16[192,1024]{1,0:T(8,128)(2,1)}, bf16[192,1024]{1,0:T(8,128)(2,1)S(1)}, u32[]{:S(2)}, u32[]{:S(2)}) collective-permute-start(bf16[192,1024]{1,0:T(8,128)(2,1)} %get-tuple-element.35), channel_id=1, source_target_pairs={{0,96},{1,97},{2,98},{3,99},{4,100},{5,101},{6,102},{7,103},{8,104... | collective-permute-start | bytes 1179656 | tf_op jit(solution)/shard_map/ppermute | solution.py:378
  3.8 10.5 %collective-permute-start.4 = (bf16[192,1024]{1,0:T(8,128)(2,1)}, bf16[192,1024]{1,0:T(8,128)(2,1)}, u32[]{:S(2)}, u32[]{:S(2)}) collective-permute-start(bf16[192,1024]{1,0:T(8,128)(2,1)} %get-tuple-element.35), channel_id=1, source_target_pairs={{0,32},{1,33},{2,34},{3,35},{4,36},{5,37},{6,38},{7,39},{8,40},{9,... | collective-permute-start | bytes 1179656 | tf_op jit(solution)/shard_map/ppermute | solution.py:378
  5.2 34.2 %collective-permute-start = (bf16[8,128,1024]{2,1,0:T(8,128)(2,1)S(1)}, bf16[8,128,1024]{2,1,0:T(8,128)(2,1)}, u32[]{:S(2)}, u32[]{:S(2)}) collective-permute-start(bf16[8,128,1024]{2,1,0:T(8,128)(2,1)S(1)} %bitcast.21), channel_id=1, source_target_pairs={{0,1},{1,0},{2,3},{3,2},{4,5},{5,4},{6,7},{7,6},{8,9},{9,8},{10,11... | collective-permute-start | bytes 6291464 | tf_op jit(solution)/shard_map/ppermute | solution.py:372
  5.2 39.4 %collective-permute-start.7 = (bf16[448,1024]{1,0:T(8,128)(2,1)}, bf16[448,1024]{1,0:T(8,128)(2,1)}, u32[]{:S(2)}, u32[]{:S(2)}) collective-permute-start(bf16[448,1024]{1,0:T(8,128)(2,1)} %get-tuple-element.36), channel_id=1, source_target_pairs={{0,96},{1,97},{2,98},{3,99},{4,100},{5,101},{6,102},{7,103},{8,104... | collective-permute-start | bytes 2752520 | tf_op jit(solution)/shard_map/ppermute | solution.py:378
  9.9 39.6 %collective-permute-start.1 = (bf16[512,1024]{1,0:T(8,128)(2,1)S(1)}, bf16[512,1024]{1,0:T(8,128)(2,1)}, u32[]{:S(2)}, u32[]{:S(2)}) collective-permute-start(bf16[512,1024]{1,0:T(8,128)(2,1)S(1)} %get-tuple-element.33.refs_0_), channel_id=1, source_target_pairs={{0,1},{1,0},{2,3},{3,2},{4,5},{5,4},{6,7},{7,6},{8,9},{9,8},{10,11... | collective-permute-start | bytes 3145736 | tf_op jit(solution)/shard_map/ppermute | solution.py:372
  13.6 0.7 copy-start.5
  14.3 1.0 copy-start.6
  16.1 13.5 %collective-permute-start.5 = (bf16[192,1024]{1,0:T(8,128)(2,1)S(1)}, bf16[192,1024]{1,0:T(8,128)(2,1)}, u32[]{:S(2)}, u32[]{:S(2)}) collective-permute-start(bf16[192,1024]{1,0:T(8,128)(2,1)S(1)} %choose.2.refs_0_), channel_id=1, source_target_pairs={{0,8},{1,9},{2,10},{3,11},{4,12},{5,13},{6,14},{7,15},{8,16},{9,17... | collective-permute-start | bytes 1179656 | tf_op jit(solution)/shard_map/ppermute | solution.py:381
  18.1 12.3 %collective-permute-start.6 = (bf16[192,1024]{1,0:T(8,128)(2,1)S(1)}, bf16[192,1024]{1,0:T(8,128)(2,1)}, u32[]{:S(2)}, u32[]{:S(2)}) collective-permute-start(bf16[192,1024]{1,0:T(8,128)(2,1)S(1)} %choose.2.refs_0_), channel_id=1, source_target_pairs={{0,24},{1,25},{2,26},{3,27},{4,28},{5,29},{6,30},{7,31},{8,0},{9,1... | collective-permute-start | bytes 1179656 | tf_op jit(solution)/shard_map/ppermute | solution.py:381
  29.6 15.3 %collective-permute-start.8 = (bf16[448,1024]{1,0:T(8,128)(2,1)}, bf16[448,1024]{1,0:T(8,128)(2,1)S(1)}, u32[]{:S(2)}, u32[]{:S(2)}) collective-permute-start(bf16[448,1024]{1,0:T(8,128)(2,1)} %get-tuple-element.36), channel_id=1, source_target_pairs={{0,32},{1,33},{2,34},{3,35},{4,36},{5,37},{6,38},{7,39},{8,40},{9,... | collective-permute-start | bytes 2752520 | tf_op jit(solution)/shard_map/ppermute | solution.py:378
  30.4 28.3 %collective-permute-start.14 = (bf16[512,1024]{1,0:T(8,128)(2,1)S(1)}, bf16[512,1024]{1,0:T(8,128)(2,1)S(1)}, u32[]{:S(2)}, u32[]{:S(2)}) collective-permute-start(bf16[512,1024]{1,0:T(8,128)(2,1)S(1)} %get-tuple-element.33.refs_0_), channel_id=1, source_target_pairs={{32,64},{64,96},{33,65},{65,97},{34,66},{66,98},{35,67},{67,99},{3... | collective-permute-start | bytes 3145736 | tf_op jit(solution)/shard_map/ppermute | solution.py:378
  37.7 2.1 copy-start
  39.4 5.2 %copy-start.4 = (bf16[512,1024]{1,0:T(8,128)(2,1)S(1)}, bf16[512,1024]{1,0:T(8,128)(2,1)}, u32[]{:S(2)}) copy-start(bf16[512,1024]{1,0:T(8,128)(2,1)} %get-tuple-element.44.refs_1_) | copy-start | bytes 3145732
  39.4 20.0 %collective-permute-start.9 = (bf16[576,1024]{1,0:T(8,128)(2,1)S(1)}, bf16[576,1024]{1,0:T(8,128)(2,1)S(1)}, u32[]{:S(2)}, u32[]{:S(2)}) collective-permute-start(bf16[576,1024]{1,0:T(8,128)(2,1)S(1)} %join.1.refs_4_), channel_id=1, source_target_pairs={{0,1},{1,0},{2,3},{3,2},{4,5},{5,4},{6,7},{7,6},{8,9},{9,8},{10,11... | collective-permute-start | bytes 3538952 | tf_op jit(solution)/shard_map/ppermute | solution.py:372
  44.6 14.1 %collective-permute-start.2 = (bf16[512,1024]{1,0:T(8,128)(2,1)S(1)}, bf16[512,1024]{1,0:T(8,128)(2,1)S(1)}, u32[]{:S(2)}, u32[]{:S(2)}) collective-permute-start(bf16[512,1024]{1,0:T(8,128)(2,1)S(1)} %copy-done.4), channel_id=1, source_target_pairs={{0,1},{1,0},{2,3},{3,2},{4,5},{5,4},{6,7},{7,6},{8,9},{9,8},{10,11... | collective-permute-start | bytes 3145736 | tf_op jit(solution)/shard_map/ppermute | solution.py:372
  44.9 19.0 %collective-permute-start.11 = (bf16[4,128,1024]{2,1,0:T(8,128)(2,1)S(1)}, bf16[4,128,1024]{2,1,0:T(8,128)(2,1)S(1)}, u32[]{:S(2)}, u32[]{:S(2)}) collective-permute-start(bf16[4,128,1024]{2,1,0:T(8,128)(2,1)S(1)} %bitcast.35), channel_id=1, source_target_pairs={{0,31},{1,2},{2,1},{3,4},{4,3},{5,6},{6,5},{7,8},{8,7},{9,10},{10,... | collective-permute-start | bytes 3145736 | tf_op jit(solution)/shard_map/ppermute | solution.py:375
  49.6 24.1 %collective-permute-start.12 = (bf16[4,128,1024]{2,1,0:T(8,128)(2,1)S(1)}, bf16[4,128,1024]{2,1,0:T(8,128)(2,1)S(1)}, u32[]{:S(2)}, u32[]{:S(2)}) collective-permute-start(bf16[4,128,1024]{2,1,0:T(8,128)(2,1)S(1)} %bitcast.34), channel_id=1, source_target_pairs={{0,31},{1,2},{2,1},{3,4},{4,3},{5,6},{6,5},{7,8},{8,7},{9,10},{10,... | collective-permute-start | bytes 3145736 | tf_op jit(solution)/shard_map/ppermute | solution.py:375
  58.7 3.1 %collective-permute-start.10 = (bf16[448,1024]{1,0:T(8,128)(2,1)S(1)}, bf16[448,1024]{1,0:T(8,128)(2,1)S(1)}, u32[]{:S(2)}, u32[]{:S(2)}) collective-permute-start(bf16[448,1024]{1,0:T(8,128)(2,1)S(1)} %choose.3.refs_5_), channel_id=1, source_target_pairs={{0,1},{1,0},{2,3},{3,2},{4,5},{5,4},{6,7},{7,6},{8,9},{9,8},{10,11... | collective-permute-start | bytes 2752520 | tf_op jit(solution)/shard_map/ppermute | solution.py:372
  58.7 20.9 %collective-permute-start.16 = (bf16[512,1024]{1,0:T(8,128)(2,1)S(1)}, bf16[512,1024]{1,0:T(8,128)(2,1)S(1)}, u32[]{:S(2)}, u32[]{:S(2)}) collective-permute-start(bf16[512,1024]{1,0:T(8,128)(2,1)S(1)} %copy-done.4), channel_id=1, source_target_pairs={{32,96},{33,97},{34,98},{35,99},{36,100},{37,101},{38,102},{39,103... | collective-permute-start | bytes 3145736 | tf_op jit(solution)/shard_map/ppermute | solution.py:378
  59.4 25.3 %collective-permute-start.15 = (bf16[512,1024]{1,0:T(8,128)(2,1)S(1)}, bf16[512,1024]{1,0:T(8,128)(2,1)S(1)}, u32[]{:S(2)}, u32[]{:S(2)}) collective-permute-start(bf16[512,1024]{1,0:T(8,128)(2,1)S(1)} %collective-permute-done.14.refs_0_), channel_id=1, source_target_pairs={{64,96},{65,97},{66,98},{67,99},{68,100},{69,101},{70,102},{71,103... | collective-permute-start | bytes 3145736 | tf_op jit(solution)/shard_map/ppermute | solution.py:378
  76.4 12.9 %collective-permute-start.20 = (bf16[4,128,1024]{2,1,0:T(8,128)(2,1)S(1)}, bf16[4,128,1024]{2,1,0:T(8,128)(2,1)S(1)}, u32[]{:S(2)}, u32[]{:S(2)}) collective-permute-start(bf16[4,128,1024]{2,1,0:T(8,128)(2,1)S(1)} %shard_map.58.refs_1_.resid_ref), channel_id=1, source_target_pairs={{0,1},{1,0},{2,3},{3,2},{4,5},{5,4},{6,7},{7,6},{8,9},{9,8},{10,11... | collective-permute-start | bytes 3145736 | tf_op jit(solution)/shard_map/ppermute | solution.py:372
  79.0 10.8 %collective-permute-start.13 = (bf16[4,128,1024]{2,1,0:T(8,128)(2,1)S(1)}, bf16[4,128,1024]{2,1,0:T(8,128)(2,1)S(1)}, u32[]{:S(2)}, u32[]{:S(2)}) collective-permute-start(bf16[4,128,1024]{2,1,0:T(8,128)(2,1)S(1)} %shard_map.57.refs_0_.resid_ref), channel_id=1, source_target_pairs={{0,1},{1,0},{2,3},{3,2},{4,5},{5,4},{6,7},{7,6},{8,9},{9,8},{10,11... | collective-permute-start | bytes 3145736 | tf_op jit(solution)/shard_map/ppermute | solution.py:372
  79.6 26.2 %collective-permute-start.18 = (bf16[512,1024]{1,0:T(8,128)(2,1)S(1)}, bf16[512,1024]{1,0:T(8,128)(2,1)S(1)}, u32[]{:S(2)}, u32[]{:S(2)}) collective-permute-start(bf16[512,1024]{1,0:T(8,128)(2,1)S(1)} %collective-permute-done.16.refs_5_), channel_id=1, source_target_pairs={{0,1},{1,0},{2,3},{3,2},{4,5},{5,4},{6,7},{7,6},{8,9},{9,8},{10,11... | collective-permute-start | bytes 3145736 | tf_op jit(solution)/shard_map/ppermute | solution.py:372
  84.7 21.0 %collective-permute-start.17 = (bf16[512,1024]{1,0:T(8,128)(2,1)S(1)}, bf16[512,1024]{1,0:T(8,128)(2,1)S(1)}, u32[]{:S(2)}, u32[]{:S(2)}) collective-permute-start(bf16[512,1024]{1,0:T(8,128)(2,1)S(1)} %collective-permute-done.15.refs_4_), channel_id=1, source_target_pairs={{0,1},{1,0},{2,3},{3,2},{4,5},{5,4},{6,7},{7,6},{8,9},{9,8},{10,11... | collective-permute-start | bytes 3145736 | tf_op jit(solution)/shard_map/ppermute | solution.py:372
  84.7 21.9 %collective-permute-start.21 = (bf16[4,128,1024]{2,1,0:T(8,128)(2,1)S(1)}, bf16[4,128,1024]{2,1,0:T(8,128)(2,1)S(1)}, u32[]{:S(2)}, u32[]{:S(2)}) collective-permute-start(bf16[4,128,1024]{2,1,0:T(8,128)(2,1)S(1)} %shard_map.58.refs_1_.resid_ref), channel_id=1, source_target_pairs={{0,31},{1,2},{2,1},{3,4},{4,3},{5,6},{6,5},{7,8},{8,7},{9,10},{10,... | collective-permute-start | bytes 3145736 | tf_op jit(solution)/shard_map/ppermute | solution.py:375
  89.3 24.2 %collective-permute-start.19 = (bf16[4,128,1024]{2,1,0:T(8,128)(2,1)S(1)}, bf16[4,128,1024]{2,1,0:T(8,128)(2,1)S(1)}, u32[]{:S(2)}, u32[]{:S(2)}) collective-permute-start(bf16[4,128,1024]{2,1,0:T(8,128)(2,1)S(1)} %shard_map.57.refs_0_.resid_ref), channel_id=1, source_target_pairs={{0,31},{1,2},{2,1},{3,4},{4,3},{5,6},{6,5},{7,8},{8,7},{9,10},{10,... | collective-permute-start | bytes 3145736 | tf_op jit(solution)/shard_map/ppermute | solution.py:375
  89.8 31.7 %collective-permute-start.23 = (bf16[512,1024]{1,0:T(8,128)(2,1)S(1)}, bf16[512,1024]{1,0:T(8,128)(2,1)S(1)}, u32[]{:S(2)}, u32[]{:S(2)}) collective-permute-start(bf16[512,1024]{1,0:T(8,128)(2,1)S(1)} %copy-done.4), channel_id=1, source_target_pairs={{64,96},{65,97},{66,98},{67,99},{68,100},{69,101},{70,102},{71,103... | collective-permute-start | bytes 3145736 | tf_op jit(solution)/shard_map/ppermute | solution.py:378
  121.6 8.2 %collective-permute-start.25 = (bf16[512,1024]{1,0:T(8,128)(2,1)S(1)}, bf16[512,1024]{1,0:T(8,128)(2,1)S(1)}, u32[]{:S(2)}, u32[]{:S(2)}) collective-permute-start(bf16[512,1024]{1,0:T(8,128)(2,1)S(1)} %collective-permute-done.23.refs_1_), channel_id=1, source_target_pairs={{0,1},{1,0},{2,3},{3,2},{4,5},{5,4},{6,7},{7,6},{8,9},{9,8},{10,11... | collective-permute-start | bytes 3145736 | tf_op jit(solution)/shard_map/ppermute | solution.py:372
  124.8 8.4 %collective-permute-start.24 = (bf16[512,1024]{1,0:T(8,128)(2,1)S(1)}, bf16[512,1024]{1,0:T(8,128)(2,1)S(1)}, u32[]{:S(2)}, u32[]{:S(2)}) collective-permute-start(bf16[512,1024]{1,0:T(8,128)(2,1)S(1)} %collective-permute-done.14.refs_0_), channel_id=1, source_target_pairs={{0,1},{1,0},{2,3},{3,2},{4,5},{5,4},{6,7},{7,6},{8,9},{9,8},{10,11... | collective-permute-start | bytes 3145736 | tf_op jit(solution)/shard_map/ppermute | solution.py:372
  127.9 6.1 %collective-permute-start.22 = (bf16[4,128,1024]{2,1,0:T(8,128)(2,1)S(1)}, bf16[4,128,1024]{2,1,0:T(8,128)(2,1)S(1)}, u32[]{:S(2)}, u32[]{:S(2)}) collective-permute-start(bf16[4,128,1024]{2,1,0:T(8,128)(2,1)S(1)} %shard_map.60.refs_0_.resid_ref.refs_2_), channel_id=1, source_target_pairs={{0,1},{1,0},{2,3},{3,2},{4,5},{5,4},{6,7},{7,6},{8,9},{9,8},{10,11... | collective-permute-start | bytes 3145736 | tf_op jit(solution)/shard_map/ppermute | solution.py:372
  128.0 17.6 %collective-permute-start.26 = (bf16[4,128,1024]{2,1,0:T(8,128)(2,1)S(1)}, bf16[4,128,1024]{2,1,0:T(8,128)(2,1)S(1)}, u32[]{:S(2)}, u32[]{:S(2)}) collective-permute-start(bf16[4,128,1024]{2,1,0:T(8,128)(2,1)S(1)} %shard_map.60.refs_0_.resid_ref.refs_2_), channel_id=1, source_target_pairs={{0,31},{1,2},{2,1},{3,4},{4,3},{5,6},{6,5},{7,8},{8,7},{9,10},{10,... | collective-permute-start | bytes 3145736 | tf_op jit(solution)/shard_map/ppermute | solution.py:375
  129.8 18.5 %collective-permute-start.28 = (bf16[4,128,1024]{2,1,0:T(8,128)(2,1)S(1)}, bf16[4,128,1024]{2,1,0:T(8,128)(2,1)S(1)}, u32[]{:S(2)}, u32[]{:S(2)}) collective-permute-start(bf16[4,128,1024]{2,1,0:T(8,128)(2,1)S(1)} %shard_map.62.refs_1_.resid_ref.refs_3_), channel_id=1, source_target_pairs={{0,1},{1,0},{2,3},{3,2},{4,5},{5,4},{6,7},{7,6},{8,9},{9,8},{10,11... | collective-permute-start | bytes 3145736 | tf_op jit(solution)/shard_map/ppermute | solution.py:372
  129.8 27.1 %collective-permute-start.29 = (bf16[4,128,1024]{2,1,0:T(8,128)(2,1)S(1)}, bf16[4,128,1024]{2,1,0:T(8,128)(2,1)S(1)}, u32[]{:S(2)}, u32[]{:S(2)}) collective-permute-start(bf16[4,128,1024]{2,1,0:T(8,128)(2,1)S(1)} %shard_map.62.refs_1_.resid_ref.refs_3_), channel_id=1, source_target_pairs={{0,31},{1,2},{2,1},{3,4},{4,3},{5,6},{6,5},{7,8},{8,7},{9,10},{10,... | collective-permute-start | bytes 3145736 | tf_op jit(solution)/shard_map/ppermute | solution.py:375
  148.2 17.9 %collective-permute-start.31 = (bf16[4,128,1024]{2,1,0:T(8,128)(2,1)S(1)}, bf16[4,128,1024]{2,1,0:T(8,128)(2,1)S(1)}, u32[]{:S(2)}, u32[]{:S(2)}) collective-permute-start(bf16[4,128,1024]{2,1,0:T(8,128)(2,1)S(1)} %shard_map.64.refs_0_.resid_ref), channel_id=1, source_target_pairs={{0,1},{1,0},{2,3},{3,2},{4,5},{5,4},{6,7},{7,6},{8,9},{9,8},{10,11... | collective-permute-start | bytes 3145736 | tf_op jit(solution)/shard_map/ppermute | solution.py:372
  159.6 11.1 %collective-permute-start.32 = (bf16[4,128,1024]{2,1,0:T(8,128)(2,1)S(1)}, bf16[4,128,1024]{2,1,0:T(8,128)(2,1)S(1)}, u32[]{:S(2)}, u32[]{:S(2)}) collective-permute-start(bf16[4,128,1024]{2,1,0:T(8,128)(2,1)S(1)} %shard_map.66.refs_1_.resid_ref), channel_id=1, source_target_pairs={{0,1},{1,0},{2,3},{3,2},{4,5},{5,4},{6,7},{7,6},{8,9},{9,8},{10,11... | collective-permute-start | bytes 3145736 | tf_op jit(solution)/shard_map/ppermute | solution.py:372
  159.7 17.6 %collective-permute-start.33 = (bf16[4,128,1024]{2,1,0:T(8,128)(2,1)S(1)}, bf16[4,128,1024]{2,1,0:T(8,128)(2,1)S(1)}, u32[]{:S(2)}, u32[]{:S(2)}) collective-permute-start(bf16[4,128,1024]{2,1,0:T(8,128)(2,1)S(1)} %shard_map.64.refs_0_.resid_ref), channel_id=1, source_target_pairs={{0,31},{1,2},{2,1},{3,4},{4,3},{5,6},{6,5},{7,8},{8,7},{9,10},{10,... | collective-permute-start | bytes 3145736 | tf_op jit(solution)/shard_map/ppermute | solution.py:375
  161.5 27.1 %collective-permute-start.34 = (bf16[4,128,1024]{2,1,0:T(8,128)(2,1)S(1)}, bf16[4,128,1024]{2,1,0:T(8,128)(2,1)S(1)}, u32[]{:S(2)}, u32[]{:S(2)}) collective-permute-start(bf16[4,128,1024]{2,1,0:T(8,128)(2,1)S(1)} %shard_map.66.refs_1_.resid_ref), channel_id=1, source_target_pairs={{0,31},{1,2},{2,1},{3,4},{4,3},{5,6},{6,5},{7,8},{8,7},{9,10},{10,... | collective-permute-start | bytes 3145736 | tf_op jit(solution)/shard_map/ppermute | solution.py:375
  164.8 38.6 %collective-permute-start.30 = (bf16[4,128,1024]{2,1,0:T(8,128)(2,1)S(1)}, bf16[4,128,1024]{2,1,0:T(8,128)(2,1)S(1)}, u32[]{:S(2)}, u32[]{:S(2)}) collective-permute-start(bf16[4,128,1024]{2,1,0:T(8,128)(2,1)S(1)} %shard_map.66.refs_1_.resid_ref), channel_id=1, source_target_pairs={{96,64},{97,65},{98,66},{99,67},{100,68},{101,69},{102,70},{103,71... | collective-permute-start | bytes 3145736 | tf_op jit(solution)/shard_map/ppermute | solution.py:378
  166.1 56.1 %collective-permute-start.27 = (bf16[4,128,1024]{2,1,0:T(8,128)(2,1)S(1)}, bf16[4,128,1024]{2,1,0:T(8,128)(2,1)S(1)}, u32[]{:S(2)}, u32[]{:S(2)}) collective-permute-start(bf16[4,128,1024]{2,1,0:T(8,128)(2,1)S(1)} %shard_map.64.refs_0_.resid_ref), channel_id=1, source_target_pairs={{96,64},{97,65},{98,66},{99,67},{100,68},{101,69},{102,70},{103,71... | collective-permute-start | bytes 3145736 | tf_op jit(solution)/shard_map/ppermute | solution.py:378
  170.6 6.7 %copy-start.2 = (bf16[1,1024,1024]{2,1,0:T(8,128)(2,1)S(1)}, bf16[1,1024,1024]{2,1,0:T(8,128)(2,1)}, u32[]{:S(2)}) copy-start(bf16[1,1024,1024]{2,1,0:T(8,128)(2,1)} %param.7) | copy-start | bytes 6291460
  170.6 6.7 %copy-start.3 = (bf16[1,1024,1024]{2,1,0:T(8,128)(2,1)S(1)}, bf16[1,1024,1024]{2,1,0:T(8,128)(2,1)}, u32[]{:S(2)}) copy-start(bf16[1,1024,1024]{2,1,0:T(8,128)(2,1)} %param.8) | copy-start | bytes 6291460
